TPU v7x, 32 devices: a whole 2x2x4 slice. The times are simulated.
32 devices in a mesh: groups: 2 (over y), rows: 4 (over z), cols: 2 (over x), date: 2 (over core).
Axes of the slice: x: 2, y: 2, z: 4, core: 2. Of those that a mesh axis runs over, the one named last changes fastest.
Arguments:
- features: bfloat16 [2, 128, 256, 128], P('date', ('groups', 'rows'), 'cols'), parts along dimension 1, may hold values from -6 to 6
- scene_shift: int32 [8, 2, 2], P('groups'), parts along dimension 0, may hold values from -4 to 4, as said below
- w_lat: bfloat16 [128, 128], replicated, may hold values from -0.5 to 0.5
- b_lat: float32 [128], replicated, may hold values from -3 to 3
- w_fpn: bfloat16 [3, 3, 128, 128], replicated, may hold values from -0.1875 to 0.1875
- w_dec1: bfloat16 [3, 3, 128, 128], replicated, may hold values from -0.1875 to 0.1875
- b_dec1: float32 [128], replicated, may hold values from -3 to 3
- w_dec2: bfloat16 [3, 3, 128, 128], replicated, may hold values from -0.1875 to 0.1875
- b_dec2: float32 [128], replicated, may hold values from -3 to 3
- w_out: bfloat16 [128], replicated, may hold values from -0.5 to 0.5
- b_out: float32 [1], replicated, may hold values from -3 to 3
Outputs:
- change_logit: float32 [128, 256], P(('groups', 'rows', 'date'), 'cols'), parts along dimension 0
There are 2 independent parts, one for each index of `groups`. A program takes and returns all parts, laid end to end along the dimension named above; an argument that names none is the same for every part. Nothing has to cross between parts.
Inputs may be any that keep to these rules, and one draw needn't show every extreme that they name: `scene_shift`: each offset component lies between -4 and 4; 4 and -4 both occur in every draw.
All inputs are finite; a program needn't handle non-finite values.
Results may differ from a plain program's by a relative error of at most 0.0076.
Values may be sent and summed in bfloat16 or wider, within the bound.
No kernel may reach another device: no remote copies, remote signals or barrier semaphores. Data moves between devices by JAX's collectives and lax.ppermute only.
A program may use at most 64 MiB of HBM per device.

v0:
```python
import jax
import jax.numpy as jnp
from jax import lax
from jax.sharding import PartitionSpec as P

MO = 4


def extended(x, sides, width):
    for axis, dim in sides:
        size, length = (lax.axis_size(axis), x.shape[dim])
        up = [(i, (i + 1) % size) for i in range(size - 1)]
        down = [(j, i) for i, j in up]
        last = lax.slice_in_dim(x, length - width, length, axis=dim)
        first = lax.slice_in_dim(x, 0, width, axis=dim)
        before = lax.ppermute(last, axis, up)
        after = lax.ppermute(first, axis, down)
        x = jnp.concatenate([before, x, after], axis=dim)
    return x


def from_partner(value, axis, bit):
    mask = 2**bit
    pairs = [(source, source ^ mask) for source in range(lax.axis_size(axis))]
    return lax.ppermute(value, axis, pairs)


def conv_three(padded, weights):
    out_rows = padded.shape[0] - 2
    out_cols = padded.shape[1] - 2
    channels = padded.shape[2]
    total = jnp.zeros((out_rows * out_cols, weights.shape[3]), jnp.float32)
    for row_tap in range(3):
        for col_tap in range(3):
            window = padded[row_tap : row_tap + out_rows, col_tap : col_tap + out_cols].reshape(
                -1, channels
            )
            total = total + jnp.dot(
                window, weights[row_tap, col_tap], preferred_element_type=jnp.float32
            )
    return total.reshape(out_rows, out_cols, weights.shape[3])


def lateral_map(inputs, w_lat, b_lat):
    flat = (
        jnp.dot(inputs.reshape(-1, inputs.shape[-1]), w_lat, preferred_element_type=jnp.float32)
        + b_lat
    )
    return flat.astype(jnp.bfloat16).reshape(inputs.shape[:-1] + (w_lat.shape[1],))


def grid_mask(cycle, half_rows, tile_cols):
    global_row = (
        lax.axis_index(("rows", "date")) * half_rows - cycle + jnp.arange(half_rows + 2 * cycle)
    )
    global_col = lax.axis_index("cols") * tile_cols - cycle + jnp.arange(tile_cols + 2 * cycle)
    row_valid = (global_row >= 0) & (global_row < lax.axis_size(("rows", "date")) * half_rows)
    col_valid = (global_col >= 0) & (global_col < lax.axis_size("cols") * tile_cols)
    return (row_valid[:, None] & col_valid[None, :]).astype(jnp.float32)


def regrid(rim, half_rows, tile_cols, scene_shift, margin, extra):
    channels = rim.shape[2]
    width = margin + extra
    offset_base = width + margin
    place_row = lax.axis_index(("rows", "date"))
    place_col = lax.axis_index("cols")
    row_total = lax.axis_size(("rows", "date"))
    col_total = lax.axis_size("cols")
    date_total = lax.axis_size("date")
    canvas = jnp.zeros(
        (half_rows + 2 * offset_base, tile_cols + 2 * offset_base, channels), jnp.float32
    )
    counts = jnp.zeros((half_rows + 2 * offset_base, tile_cols + 2 * offset_base), jnp.float32)
    row_parts = (
        (-1, 0, width, half_rows - width),
        (0, width, half_rows, 0),
        (1, width + half_rows, width, 0),
    )
    col_parts = (
        (-1, 0, width, tile_cols - width),
        (0, width, tile_cols, 0),
        (1, width + tile_cols, width, 0),
    )
    zero = jnp.zeros((), jnp.int32)
    for row_step, row_from, row_len, row_start in row_parts:
        for col_step, col_from, col_len, col_start in col_parts:
            near_row = place_row + row_step
            near_col = place_col + col_step
            inside = (
                (near_row >= 0) & (near_row < row_total) & (near_col >= 0) & (near_col < col_total)
            )
            scene_row = jnp.clip(near_row, 0, row_total - 1) // date_total
            scene_col = jnp.clip(near_col, 0, col_total - 1)
            offset = scene_shift[scene_row, scene_col]
            top = row_step * half_rows + row_start + offset_base + offset[0]
            left = col_step * tile_cols + col_start + offset_base + offset[1]
            present = inside.astype(jnp.float32)
            piece = (
                rim[row_from : row_from + row_len, col_from : col_from + col_len].astype(
                    jnp.float32
                )
                * present
            )
            region = lax.dynamic_slice(canvas, (top, left, zero), (row_len, col_len, channels))
            canvas = lax.dynamic_update_slice(canvas, region + piece, (top, left, zero))
            region_count = lax.dynamic_slice(counts, (top, left), (row_len, col_len))
            counts = lax.dynamic_update_slice(counts, region_count + present, (top, left))
    low = offset_base - extra
    b_sum = canvas[low : low + half_rows + 2 * extra, low : low + tile_cols + 2 * extra]
    coverage = counts[low : low + half_rows + 2 * extra, low : low + tile_cols + 2 * extra]
    return (b_sum, coverage)


def per_device(
    features, scene_shift, w_lat, b_lat, w_fpn, w_dec1, b_dec1, w_dec2, b_dec2, w_out, b_out
):
    tile_rows = features.shape[1]
    tile_cols = features.shape[2]
    half_rows = tile_rows // 2
    which_date = lax.axis_index("date")
    is_first = which_date == 0
    lateral = lateral_map(features[0], w_lat, b_lat)
    padded = extended(lateral, (("rows", 0), ("cols", 1)), 1)
    pyramid = conv_three(padded, w_fpn).astype(jnp.bfloat16)
    kept_part = lax.dynamic_slice_in_dim(pyramid, which_date * half_rows, half_rows, 0)
    sent_part = lax.dynamic_slice_in_dim(pyramid, (1 - which_date) * half_rows, half_rows, 0)
    received = from_partner(sent_part, "date", 0)
    a_half = jnp.where(is_first, kept_part, received)
    b_half = jnp.where(is_first, received, kept_part)
    extra = 0
    rim = extended(b_half, ((("rows", "date"), 0), ("cols", 1)), MO + extra)
    b_sum, coverage = regrid(rim, half_rows, tile_cols, scene_shift, MO, extra)
    covered = jnp.minimum(coverage, 1.0)[:, :, None]
    regridded = b_sum / jnp.maximum(coverage, 1.0)[:, :, None]
    difference = (jnp.abs(a_half.astype(jnp.float32) - regridded) * covered).astype(jnp.bfloat16)
    padded_diff = extended(difference, ((("rows", "date"), 0), ("cols", 1)), 2)
    wide_hidden = jnp.maximum(conv_three(padded_diff, w_dec1) + b_dec1, 0.0)
    inside = grid_mask(1, half_rows, tile_cols)
    hidden_one = (wide_hidden * inside[:, :, None]).astype(jnp.bfloat16)
    hidden_two = jnp.maximum(conv_three(hidden_one, w_dec2) + b_dec2, 0.0).astype(jnp.bfloat16)
    logit = (
        jnp.dot(
            hidden_two.reshape(-1, hidden_two.shape[2]), w_out, preferred_element_type=jnp.float32
        )
        + b_out
    )
    return logit.reshape(half_rows, tile_cols)


def solution(mesh):
    return jax.shard_map(
        per_device,
        mesh=mesh,
        in_specs=(
            P("date", ("groups", "rows"), "cols", None),
            P("groups", None, None),
            P(),
            P(),
            P(),
            P(),
            P(),
            P(),
            P(),
            P(),
            P(),
        ),
        out_specs=P(("groups", "rows", "date"), "cols"),
        check_vma=False,
    )
```

profile of v0, /device:TPU:12, one launch (start us, length us, event | category | flops | bytes accessed | tf_op | source)
XLA Modules:
  0.0 105.2 jit_solution(506069014609525896)
XLA Ops:
  0.0 1.0 copy-done
  1.0 1.1 %fusion.1 = bf16[2048,128]{1,0:T(8,128)(2,1)S(1)} fusion(bf16[2048,128]{1,0:T(8,128)(2,1)S(1)} %bitcast.179, bf16[128,128]{1,0:T(8,128)(2,1)} %param.13, f32[128]{0:T(128)} %param.14), kind=kOutput, calls=%fused_computation.17 | convolution fusion | flops 67633152 | bytes 1081856 | tf_op jit(solution)/shard_map/dot_general | solution.py:46
  2.2 3.5 %collective-permute-start = (bf16[1,128,128]{2,1,0:T(8,128)(2,1)S(1)}, bf16[1,128,128]{2,1,0:T(8,128)(2,1)S(1)}, u32[]{:S(2)}, u32[]{:S(2)}) collective-permute-start(bf16[1,128,128]{2,1,0:T(8,128)(2,1)S(1)} %get-tuple-element.19), channel_id=1, source_target_pairs={{0,4},{4,8},{8,12},{1,5},{5,9},{9,13},{2,6},{6,10},{10,14},{3,7},{... | collective-permute-start | bytes 98312 | tf_op jit(solution)/shard_map/ppermute | solution.py:16
  5.6 2.4 %collective-permute-start.1 = (bf16[1,128,128]{2,1,0:T(8,128)(2,1)S(1)}, bf16[1,128,128]{2,1,0:T(8,128)(2,1)S(1)}, u32[]{:S(2)}, u32[]{:S(2)}) collective-permute-start(bf16[1,128,128]{2,1,0:T(8,128)(2,1)S(1)} %get-tuple-element.20), channel_id=1, source_target_pairs={{4,0},{8,4},{12,8},{5,1},{9,5},{13,9},{6,2},{10,6},{14,10},{7,3},{... | collective-permute-start | bytes 98312 | tf_op jit(solution)/shard_map/ppermute | solution.py:17
  8.1 1.0 constant_dynamic-slice_fusion
  34.1 3.4 %collective-permute-start.2 = (bf16[18,1,128]{2,1,0:T(2,128)(2,1)S(1)}, bf16[18,1,128]{2,1,0:T(2,128)(2,1)S(1)}, u32[]{:S(2)}, u32[]{:S(2)}) collective-permute-start(bf16[18,1,128]{2,1,0:T(2,128)(2,1)S(1)} %get-tuple-element.13), channel_id=1, source_target_pairs={{0,2},{1,3},{4,6},{5,7},{8,10},{9,11},{12,14},{13,15},{16,18},{17,... | collective-permute-start | bytes 13832 | tf_op jit(solution)/shard_map/ppermute | solution.py:16
  37.5 1.3 %collective-permute-start.3 = (bf16[18,1,128]{2,1,0:T(2,128)(2,1)S(1)}, bf16[18,1,128]{2,1,0:T(2,128)(2,1)S(1)}, u32[]{:S(2)}, u32[]{:S(2)}) collective-permute-start(bf16[18,1,128]{2,1,0:T(2,128)(2,1)S(1)} %get-tuple-element.14), channel_id=1, source_target_pairs={{2,0},{3,1},{6,4},{7,5},{10,8},{11,9},{14,12},{15,13},{18,16},{19,... | collective-permute-start | bytes 13832 | tf_op jit(solution)/shard_map/ppermute | solution.py:17
  39.2 3.9 %collective-permute-done.3 = bf16[18,1,128]{2,1,0:T(2,128)(2,1)S(1)} collective-permute-done((bf16[18,1,128]{2,1,0:T(2,128)(2,1)S(1)}, bf16[18,1,128]{2,1,0:T(2,128)(2,1)S(1)}, u32[]{:S(2)}, u32[]{:S(2)}) %collective-permute-start.3) | collective-permute-done | bytes 4640 | tf_op jit(solution)/shard_map/ppermute | solution.py:17
  53.4 2.4 %collective-permute-start.5 = (bf16[4,128,128]{2,1,0:T(8,128)(2,1)S(1)}, bf16[4,128,128]{2,1,0:T(8,128)(2,1)S(1)}, u32[]{:S(2)}, u32[]{:S(2)}) collective-permute-start(bf16[4,128,128]{2,1,0:T(8,128)(2,1)S(1)} %get-tuple-element.45), channel_id=1, source_target_pairs={{0,1},{1,4},{4,5},{5,8},{8,9},{9,12},{12,13},{2,3},{3,6},{6,7},{7,... | collective-permute-start | bytes 393224 | tf_op jit(solution)/shard_map/ppermute | solution.py:16
  55.8 3.2 %collective-permute-start.6 = (bf16[4,128,128]{2,1,0:T(8,128)(2,1)S(1)}, bf16[4,128,128]{2,1,0:T(8,128)(2,1)S(1)}, u32[]{:S(2)}, u32[]{:S(2)}) collective-permute-start(bf16[4,128,128]{2,1,0:T(8,128)(2,1)S(1)} %get-tuple-element.46), channel_id=1, source_target_pairs={{1,0},{4,1},{5,4},{8,5},{9,8},{12,9},{13,12},{3,2},{6,3},{7,6},{10... | collective-permute-start | bytes 393224 | tf_op jit(solution)/shard_map/ppermute | solution.py:17
  59.7 1.8 %collective-permute-done.6 = bf16[4,128,128]{2,1,0:T(8,128)(2,1)S(1)} collective-permute-done((bf16[4,128,128]{2,1,0:T(8,128)(2,1)S(1)}, bf16[4,128,128]{2,1,0:T(8,128)(2,1)S(1)}, u32[]{:S(2)}, u32[]{:S(2)}) %collective-permute-start.6) | collective-permute-done | bytes 131104 | tf_op jit(solution)/shard_map/ppermute | solution.py:17
  61.5 1.7 %collective-permute-start.7 = (bf16[16,4,128]{2,1,0:T(4,128)(2,1)S(1)}, bf16[16,4,128]{2,1,0:T(4,128)(2,1)S(1)}, u32[]{:S(2)}, u32[]{:S(2)}) collective-permute-start(bf16[16,4,128]{2,1,0:T(4,128)(2,1)S(1)} %get-tuple-element.16), channel_id=1, source_target_pairs={{0,2},{1,3},{4,6},{5,7},{8,10},{9,11},{12,14},{13,15},{16,18},{17,... | collective-permute-start | bytes 49160 | tf_op jit(solution)/shard_map/ppermute | solution.py:16
  63.2 1.3 %collective-permute-start.8 = (bf16[16,4,128]{2,1,0:T(4,128)(2,1)S(1)}, bf16[16,4,128]{2,1,0:T(4,128)(2,1)S(1)}, u32[]{:S(2)}, u32[]{:S(2)}) collective-permute-start(bf16[16,4,128]{2,1,0:T(4,128)(2,1)S(1)} %get-tuple-element.15), channel_id=1, source_target_pairs={{2,0},{3,1},{6,4},{7,5},{10,8},{11,9},{14,12},{15,13},{18,16},{19,... | collective-permute-start | bytes 49160 | tf_op jit(solution)/shard_map/ppermute | solution.py:17
  66.3 2.5 %collective-permute-done.8 = bf16[16,4,128]{2,1,0:T(4,128)(2,1)S(1)} collective-permute-done((bf16[16,4,128]{2,1,0:T(4,128)(2,1)S(1)}, bf16[16,4,128]{2,1,0:T(4,128)(2,1)S(1)}, u32[]{:S(2)}, u32[]{:S(2)}) %collective-permute-start.8) | collective-permute-done | bytes 16416 | tf_op jit(solution)/shard_map/ppermute | solution.py:17
  70.1 2.7 %dynamic_update_slice.58 = f32[24,144,128]{2,1,0:T(8,128)S(1)} dynamic-update-slice(f32[24,144,128]{2,1,0:T(8,128)S(1)} %dynamic_update_slice.57, f32[8,128,128]{2,1,0:T(8,128)} %multiply_add_fusion, s32[]{:T(128)S(6)} %select_n.92, s32[]{:T(128)S(6)} %select_n.93, s32[]{:T(128)} %constant.131.clone.1) | dynamic-update-slice | bytes 1048580 | tf_op jit(solution)/shard_map/dynamic_update_slice | solution.py:106
  74.2 2.3 %collective-permute-start.10 = (bf16[2,128,128]{2,1,0:T(8,128)(2,1)S(1)}, bf16[2,128,128]{2,1,0:T(8,128)(2,1)S(1)}, u32[]{:S(2)}, u32[]{:S(2)}) collective-permute-start(bf16[2,128,128]{2,1,0:T(8,128)(2,1)S(1)} %get-tuple-element.44), channel_id=1, source_target_pairs={{1,0},{4,1},{5,4},{8,5},{9,8},{12,9},{13,12},{3,2},{6,3},{7,6},{10... | collective-permute-start | bytes 196616 | tf_op jit(solution)/shard_map/ppermute | solution.py:17
  76.6 2.0 %collective-permute-start.9 = (bf16[2,128,128]{2,1,0:T(8,128)(2,1)S(1)}, bf16[2,128,128]{2,1,0:T(8,128)(2,1)S(1)}, u32[]{:S(2)}, u32[]{:S(2)}) collective-permute-start(bf16[2,128,128]{2,1,0:T(8,128)(2,1)S(1)} %get-tuple-element.43), channel_id=1, source_target_pairs={{0,1},{1,4},{4,5},{5,8},{8,9},{9,12},{12,13},{2,3},{3,6},{6,7},{7,... | collective-permute-start | bytes 196616 | tf_op jit(solution)/shard_map/ppermute | solution.py:16
  78.6 3.6 %collective-permute-done.9 = bf16[2,128,128]{2,1,0:T(8,128)(2,1)S(1)} collective-permute-done((bf16[2,128,128]{2,1,0:T(8,128)(2,1)S(1)}, bf16[2,128,128]{2,1,0:T(8,128)(2,1)S(1)}, u32[]{:S(2)}, u32[]{:S(2)}) %collective-permute-start.9) | collective-permute-done | bytes 65568 | tf_op jit(solution)/shard_map/ppermute | solution.py:16
  82.2 2.9 %collective-permute-start.11 = (bf16[12,2,128]{2,1,0:T(2,128)(2,1)S(1)}, bf16[12,2,128]{2,1,0:T(2,128)(2,1)S(1)}, u32[]{:S(2)}, u32[]{:S(2)}) collective-permute-start(bf16[12,2,128]{2,1,0:T(2,128)(2,1)S(1)} %get-tuple-element.32), channel_id=1, source_target_pairs={{0,2},{1,3},{4,6},{5,7},{8,10},{9,11},{12,14},{13,15},{16,18},{17,... | collective-permute-start | bytes 18440 | tf_op jit(solution)/shard_map/ppermute | solution.py:16
  85.0 1.5 %collective-permute-start.12 = (bf16[12,2,128]{2,1,0:T(2,128)(2,1)S(1)}, bf16[12,2,128]{2,1,0:T(2,128)(2,1)S(1)}, u32[]{:S(2)}, u32[]{:S(2)}) collective-permute-start(bf16[12,2,128]{2,1,0:T(2,128)(2,1)S(1)} %get-tuple-element.33), channel_id=1, source_target_pairs={{2,0},{3,1},{6,4},{7,5},{10,8},{11,9},{14,12},{15,13},{18,16},{19,... | collective-permute-start | bytes 18440 | tf_op jit(solution)/shard_map/ppermute | solution.py:17
  87.2 3.3 %collective-permute-done.12 = bf16[12,2,128]{2,1,0:T(2,128)(2,1)S(1)} collective-permute-done((bf16[12,2,128]{2,1,0:T(2,128)(2,1)S(1)}, bf16[12,2,128]{2,1,0:T(2,128)(2,1)S(1)}, u32[]{:S(2)}, u32[]{:S(2)}) %collective-permute-start.12) | collective-permute-done | bytes 6176 | tf_op jit(solution)/shard_map/ppermute | solution.py:17
  95.5 1.1 %fusion.31 = f32[1300,128]{1,0:T(8,128)S(1)} fusion(bf16[1300,128]{1,0:T(8,128)(2,1)S(1)} %copy-done.2, bf16[3,3,128,128]{3,2,1,0:T(8,128)(2,1)} %param.16), kind=kOutput, calls=%fused_computation.69 | convolution fusion | flops 42598400 | bytes 1031168 | tf_op jit(solution)/shard_map/dot_general | solution.py:38
  96.7 1.1 %convolution_add_fusion.7 = f32[1300,128]{1,0:T(8,128)S(1)} fusion(f32[1300,128]{1,0:T(8,128)S(1)} %fusion.31, bf16[1300,128]{1,0:T(8,128)(2,1)S(1)} %copy-done.1, bf16[3,3,128,128]{3,2,1,0:T(8,128)(2,1)} %param.16), kind=kOutput, calls=%fused_computation.7 | convolution fusion | flops 42764800 | bytes 1696768 | tf_op jit(solution)/shard_map/dot_general | solution.py:38
  97.8 1.1 %convolution_add_fusion.6 = f32[1300,128]{1,0:T(8,128)S(1)} fusion(f32[1300,128]{1,0:T(8,128)S(1)} %convolution_add_fusion.7, bf16[1300,128]{1,0:T(8,128)(2,1)S(1)} %copy-done.4, bf16[3,3,128,128]{3,2,1,0:T(8,128)(2,1)} %param.16), kind=kOutput, calls=%fused_computation.6 | convolution fusion | flops 42764800 | bytes 1696768 | tf_op jit(solution)/shard_map/dot_general | solution.py:38
  (136 shorter events, 28.8 us)
Async XLA Ops:
  0.0 1.0 copy-start
  1.0 37.9 %copy-start.8 = (bf16[3,3,128,128]{3,2,1,0:T(8,128)(2,1)S(1)}, bf16[3,3,128,128]{3,2,1,0:T(8,128)(2,1)}, u32[]{:S(2)}) copy-start(bf16[3,3,128,128]{3,2,1,0:T(8,128)(2,1)} %param.15) | copy-start | bytes 884740
  2.2 31.9 %collective-permute-start = (bf16[1,128,128]{2,1,0:T(8,128)(2,1)S(1)}, bf16[1,128,128]{2,1,0:T(8,128)(2,1)S(1)}, u32[]{:S(2)}, u32[]{:S(2)}) collective-permute-start(bf16[1,128,128]{2,1,0:T(8,128)(2,1)S(1)} %get-tuple-element.19), channel_id=1, source_target_pairs={{0,4},{4,8},{8,12},{1,5},{5,9},{9,13},{2,6},{6,10},{10,14},{3,7},{... | collective-permute-start | bytes 98312 | tf_op jit(solution)/shard_map/ppermute | solution.py:16
  5.6 28.5 %collective-permute-start.1 = (bf16[1,128,128]{2,1,0:T(8,128)(2,1)S(1)}, bf16[1,128,128]{2,1,0:T(8,128)(2,1)S(1)}, u32[]{:S(2)}, u32[]{:S(2)}) collective-permute-start(bf16[1,128,128]{2,1,0:T(8,128)(2,1)S(1)} %get-tuple-element.20), channel_id=1, source_target_pairs={{4,0},{8,4},{12,8},{5,1},{9,5},{13,9},{6,2},{10,6},{14,10},{7,3},{... | collective-permute-start | bytes 98312 | tf_op jit(solution)/shard_map/ppermute | solution.py:17
  34.1 5.1 %collective-permute-start.2 = (bf16[18,1,128]{2,1,0:T(2,128)(2,1)S(1)}, bf16[18,1,128]{2,1,0:T(2,128)(2,1)S(1)}, u32[]{:S(2)}, u32[]{:S(2)}) collective-permute-start(bf16[18,1,128]{2,1,0:T(2,128)(2,1)S(1)} %get-tuple-element.13), channel_id=1, source_target_pairs={{0,2},{1,3},{4,6},{5,7},{8,10},{9,11},{12,14},{13,15},{16,18},{17,... | collective-permute-start | bytes 13832 | tf_op jit(solution)/shard_map/ppermute | solution.py:16
  37.5 5.6 %collective-permute-start.3 = (bf16[18,1,128]{2,1,0:T(2,128)(2,1)S(1)}, bf16[18,1,128]{2,1,0:T(2,128)(2,1)S(1)}, u32[]{:S(2)}, u32[]{:S(2)}) collective-permute-start(bf16[18,1,128]{2,1,0:T(2,128)(2,1)S(1)} %get-tuple-element.14), channel_id=1, source_target_pairs={{2,0},{3,1},{6,4},{7,5},{10,8},{11,9},{14,12},{15,13},{18,16},{19,... | collective-permute-start | bytes 13832 | tf_op jit(solution)/shard_map/ppermute | solution.py:17
  46.2 7.1 %collective-permute-start.4 = (bf16[8,128,128]{2,1,0:T(8,128)(2,1)S(1)}, bf16[8,128,128]{2,1,0:T(8,128)(2,1)S(1)}, u32[]{:S(2)}, u32[]{:S(2)}) collective-permute-start(bf16[8,128,128]{2,1,0:T(8,128)(2,1)S(1)} %constant_dynamic-slice_fusion.9), channel_id=1, source_target_pairs={{0,1},{1,0},{2,3},{3,2},{4,5},{5,4},{6,7},{7,6},{8,9},{9,8},{10,11... | collective-permute-start | bytes 786440 | tf_op jit(solution)/shard_map/ppermute | solution.py:25
  53.3 11.3 %copy-start.5 = (bf16[8,128,128]{2,1,0:T(8,128)(2,1)}, bf16[8,128,128]{2,1,0:T(8,128)(2,1)S(1)}, u32[]{:S(2)}) copy-start(bf16[8,128,128]{2,1,0:T(8,128)(2,1)S(1)} %collective-permute-done.4) | copy-start | bytes 786436
  53.4 6.3 %collective-permute-start.5 = (bf16[4,128,128]{2,1,0:T(8,128)(2,1)S(1)}, bf16[4,128,128]{2,1,0:T(8,128)(2,1)S(1)}, u32[]{:S(2)}, u32[]{:S(2)}) collective-permute-start(bf16[4,128,128]{2,1,0:T(8,128)(2,1)S(1)} %get-tuple-element.45), channel_id=1, source_target_pairs={{0,1},{1,4},{4,5},{5,8},{8,9},{9,12},{12,13},{2,3},{3,6},{6,7},{7,... | collective-permute-start | bytes 393224 | tf_op jit(solution)/shard_map/ppermute | solution.py:16
  55.8 5.7 %collective-permute-start.6 = (bf16[4,128,128]{2,1,0:T(8,128)(2,1)S(1)}, bf16[4,128,128]{2,1,0:T(8,128)(2,1)S(1)}, u32[]{:S(2)}, u32[]{:S(2)}) collective-permute-start(bf16[4,128,128]{2,1,0:T(8,128)(2,1)S(1)} %get-tuple-element.46), channel_id=1, source_target_pairs={{1,0},{4,1},{5,4},{8,5},{9,8},{12,9},{13,12},{3,2},{6,3},{7,6},{10... | collective-permute-start | bytes 393224 | tf_op jit(solution)/shard_map/ppermute | solution.py:17
  59.7 4.9 %copy-start.7 = (bf16[4,128,128]{2,1,0:T(8,128)(2,1)}, bf16[4,128,128]{2,1,0:T(8,128)(2,1)S(1)}, u32[]{:S(2)}) copy-start(bf16[4,128,128]{2,1,0:T(8,128)(2,1)S(1)} %collective-permute-done.5) | copy-start | bytes 393220
  61.5 3.1 %collective-permute-start.7 = (bf16[16,4,128]{2,1,0:T(4,128)(2,1)S(1)}, bf16[16,4,128]{2,1,0:T(4,128)(2,1)S(1)}, u32[]{:S(2)}, u32[]{:S(2)}) collective-permute-start(bf16[16,4,128]{2,1,0:T(4,128)(2,1)S(1)} %get-tuple-element.16), channel_id=1, source_target_pairs={{0,2},{1,3},{4,6},{5,7},{8,10},{9,11},{12,14},{13,15},{16,18},{17,... | collective-permute-start | bytes 49160 | tf_op jit(solution)/shard_map/ppermute | solution.py:16
  63.2 5.6 %collective-permute-start.8 = (bf16[16,4,128]{2,1,0:T(4,128)(2,1)S(1)}, bf16[16,4,128]{2,1,0:T(4,128)(2,1)S(1)}, u32[]{:S(2)}, u32[]{:S(2)}) collective-permute-start(bf16[16,4,128]{2,1,0:T(4,128)(2,1)S(1)} %get-tuple-element.15), channel_id=1, source_target_pairs={{2,0},{3,1},{6,4},{7,5},{10,8},{11,9},{14,12},{15,13},{18,16},{19,... | collective-permute-start | bytes 49160 | tf_op jit(solution)/shard_map/ppermute | solution.py:17
  69.2 4.7 %copy-start.6 = (bf16[8,128,128]{2,1,0:T(8,128)(2,1)S(1)}, bf16[8,128,128]{2,1,0:T(8,128)(2,1)}, u32[]{:S(2)}) copy-start(bf16[8,128,128]{2,1,0:T(8,128)(2,1)} %copy-done.5) | copy-start | bytes 786436
  74.2 4.4 %collective-permute-start.10 = (bf16[2,128,128]{2,1,0:T(8,128)(2,1)S(1)}, bf16[2,128,128]{2,1,0:T(8,128)(2,1)S(1)}, u32[]{:S(2)}, u32[]{:S(2)}) collective-permute-start(bf16[2,128,128]{2,1,0:T(8,128)(2,1)S(1)} %get-tuple-element.44), channel_id=1, source_target_pairs={{1,0},{4,1},{5,4},{8,5},{9,8},{12,9},{13,12},{3,2},{6,3},{7,6},{10... | collective-permute-start | bytes 196616 | tf_op jit(solution)/shard_map/ppermute | solution.py:17
  76.6 5.6 %collective-permute-start.9 = (bf16[2,128,128]{2,1,0:T(8,128)(2,1)S(1)}, bf16[2,128,128]{2,1,0:T(8,128)(2,1)S(1)}, u32[]{:S(2)}, u32[]{:S(2)}) collective-permute-start(bf16[2,128,128]{2,1,0:T(8,128)(2,1)S(1)} %get-tuple-element.43), channel_id=1, source_target_pairs={{0,1},{1,4},{4,5},{5,8},{8,9},{9,12},{12,13},{2,3},{3,6},{6,7},{7,... | collective-permute-start | bytes 196616 | tf_op jit(solution)/shard_map/ppermute | solution.py:16
  82.2 5.1 %collective-permute-start.11 = (bf16[12,2,128]{2,1,0:T(2,128)(2,1)S(1)}, bf16[12,2,128]{2,1,0:T(2,128)(2,1)S(1)}, u32[]{:S(2)}, u32[]{:S(2)}) collective-permute-start(bf16[12,2,128]{2,1,0:T(2,128)(2,1)S(1)} %get-tuple-element.32), channel_id=1, source_target_pairs={{0,2},{1,3},{4,6},{5,7},{8,10},{9,11},{12,14},{13,15},{16,18},{17,... | collective-permute-start | bytes 18440 | tf_op jit(solution)/shard_map/ppermute | solution.py:16
  85.0 5.5 %collective-permute-start.12 = (bf16[12,2,128]{2,1,0:T(2,128)(2,1)S(1)}, bf16[12,2,128]{2,1,0:T(2,128)(2,1)S(1)}, u32[]{:S(2)}, u32[]{:S(2)}) collective-permute-start(bf16[12,2,128]{2,1,0:T(2,128)(2,1)S(1)} %get-tuple-element.33), channel_id=1, source_target_pairs={{2,0},{3,1},{6,4},{7,5},{10,8},{11,9},{14,12},{15,13},{18,16},{19,... | collective-permute-start | bytes 18440 | tf_op jit(solution)/shard_map/ppermute | solution.py:17
  94.6 1.0 copy-start.2
  94.6 2.0 %copy-start.1 = (bf16[1300,128]{1,0:T(8,128)(2,1)S(1)}, bf16[1300,128]{1,0:T(8,128)(2,1)}, u32[]{:S(2)}) copy-start(bf16[1300,128]{1,0:T(8,128)(2,1)} %reshape.257) | copy-start | bytes 998404
  95.5 2.3 %copy-start.4 = (bf16[1300,128]{1,0:T(8,128)(2,1)S(1)}, bf16[1300,128]{1,0:T(8,128)(2,1)}, u32[]{:S(2)}) copy-start(bf16[1300,128]{1,0:T(8,128)(2,1)} %reshape.259) | copy-start | bytes 998404
  96.7 2.3 %copy-start.3 = (bf16[1300,128]{1,0:T(8,128)(2,1)S(1)}, bf16[1300,128]{1,0:T(8,128)(2,1)}, u32[]{:S(2)}) copy-start(bf16[1300,128]{1,0:T(8,128)(2,1)} %reshape.260) | copy-start | bytes 998404
  96.7 2.3 %copy-start.10 = (bf16[3,3,128,128]{3,2,1,0:T(8,128)(2,1)S(1)}, bf16[3,3,128,128]{3,2,1,0:T(8,128)(2,1)}, u32[]{:S(2)}) copy-start(bf16[3,3,128,128]{3,2,1,0:T(8,128)(2,1)} %param.16) | copy-start | bytes 884740
  101.5 1.0 copy-start.9
  (3 other events, 2.0 us)
where the time goes:
time: 106 us; the launch traced here: 105 us
  starting transfers between devices  27.7 us (26%)
  between operations  24.6 us (23%)
  local copies, waits for them, and re-layouts  21.4 us (20%)
  waiting for transfers between devices  15.8 us (15%)
  matrix products  10.9 us (10%)
  other arithmetic  4.82 us (5%)
    ppermute x6, starting transfers between devices, extended(): before = lax.ppermute(last, axis, up)  15.7 us
    ppermute x6, starting transfers between devices, extended(): after = lax.ppermute(first, axis, down)  12 us
    ppermute x6, waiting for transfers between devices, extended(): after = lax.ppermute(first, axis, down)  11.5 us
    dot_general x26, matrix products, conv_three(): jnp.dot(window, weights[row_tap, col_tap], preferred_element_type=jnp.flo...  9.4 us
    dynamic_update_slice x9, local copies, waits for them, and re-layouts, regrid(): lax.dynamic_update_slice(counts, region_count + present, (top, left))  5.36 us
    dynamic_update_slice x9, local copies, waits for them, and re-layouts, regrid(): canvas = lax.dynamic_update_slice(canvas, region + piece, (top, left, zero))  4.47 us
    ppermute x6, waiting for transfers between devices, extended(): before = lax.ppermute(last, axis, up)  4.32 us
    reshape x9, local copies, waits for them, and re-layouts, conv_three(): padded[row_tap:row_tap + out_rows, col_tap:col_tap + out_cols]  3.69 us
  transfers between devices with their start and end apart: 13, of which 7 were waited for; matrix products, arithmetic and copies ran while one was open for 12% of the time, Pallas kernels for 0%

commit v1 on v0

v1 whole, which is shorter than its diff:
```python
import functools

import jax
import jax.numpy as jnp
from jax import lax
from jax.experimental import pallas as pl
from jax.experimental.pallas import tpu as pltpu
from jax.sharding import PartitionSpec as P

MO = 4
HA = 3
HB = HA + MO
CW = 8
F32 = jnp.float32
BF16 = jnp.bfloat16


def column_partner(col, parity, n_cols):
    right = col % 2 == parity
    return (col + 1) % n_cols if right else (col - 1) % n_cols


def row_partner(row, date, n_rows):
    near = row + (1 if date else -1)
    return (near, 1 - date) if 0 <= near < n_rows else None


def send(value, sizes, target):
    n_rows, n_cols, n_dates = sizes
    pairs = []
    for row in range(n_rows):
        for col in range(n_cols):
            for date in range(n_dates):
                to_row, to_col, to_date = target(row, col, date)
                source = (row * n_cols + col) * n_dates + date
                pairs.append((source, (to_row * n_cols + to_col) * n_dates + to_date))
    return lax.ppermute(value, ("rows", "cols", "date"), pairs)


def conv_weights(w_ref):
    chans = w_ref.shape[-1]
    tall = w_ref[...].reshape(-1, chans)
    none = jnp.zeros((3 * chans, chans), tall.dtype)
    return jnp.concatenate(
        [jnp.concatenate([tall, none], axis=0), jnp.concatenate([none, tall], axis=0)], axis=1
    )


def body(
    n_par, n_rows, n_cols, tile_rows, tile_cols,
    shift, own, oth, *refs,
):
    sides = refs[:n_par]
    v_ref = refs[n_par]
    corners = refs[n_par + 1 : 2 * n_par + 1]
    (w_lat, b_lat, w_fpn, w_dec1, b_dec1, w_dec2, b_dec2, w_out, b_out, out_ref,
     lat, cat_a, cat_b, pyr_a, pyr_b, dif, cat_d, hid, cat_h) = refs[2 * n_par + 1 :]
    row, col, date = lax.axis_index("rows"), lax.axis_index("cols"), lax.axis_index("date")
    half = tile_rows // 2
    width = tile_cols + 2 * CW
    chans = own.shape[-1]
    first_half = row * 2 + date
    other = 1 - date
    has_row = jnp.where(date == 0, row > 0, row < n_rows - 1)
    row_keep = has_row.astype(F32)

    def at(line, column):
        return CW + line * width + CW + column

    weight, bias = w_lat[...], b_lat[...]

    def lateral(x):
        return jnp.dot(x.reshape(-1, chans), weight, preferred_element_type=F32) + bias

    if n_cols == 2:
        blank = jnp.zeros((CW, chans), F32)
        at_blank = jnp.where(col % 2 == 0, -CW, tile_cols)
        for which in range(2):
            for line in range(tile_rows + 2 * HB):
                lat[which, pl.ds(pl.multiple_of(at(line, at_blank), 8), CW)] = blank
    for which, x_ref in ((date, own), (other, oth)):
        z = lateral(x_ref[...])
        for t in range(tile_rows):
            lat[which, at(t + HB, 0) : at(t + HB, 0) + tile_cols] = z[
                t * tile_cols : (t + 1) * tile_cols
            ]
    base_a = jnp.where(date == 0, HB - HA, HB + tile_rows)
    base_b = jnp.where(date == 0, 0, HB + tile_rows)
    z = lateral(v_ref[...]) * row_keep
    for i in range(HA + HB):
        which, line = (0, base_a + i) if i < HA else (1, base_b + i - HA)
        lat[which, pl.ds(pl.multiple_of(at(line, 0), 8), tile_cols)] = z[
            i * tile_cols : (i + 1) * tile_cols
        ]
    for parity in range(n_par):
        right = col % 2 == parity
        exists = jnp.where(right, col < n_cols - 1, col > 0).astype(F32)
        at_col = jnp.where(right, tile_cols, -CW)
        z = lateral(sides[parity][...]) * exists
        for t in range(2 * tile_rows):
            which = date if t < tile_rows else other
            line = t % tile_rows + HB
            lat[which, pl.ds(pl.multiple_of(at(line, at_col), 8), CW)] = z[t * CW : (t + 1) * CW]
        z = lateral(corners[parity][...]) * (exists * row_keep)
        for i in range(HA + HB):
            which, line = (0, base_a + i) if i < HA else (1, base_b + i - HA)
            lat[which, pl.ds(pl.multiple_of(at(line, at_col), 8), CW)] = z[i * CW : (i + 1) * CW]

    def gather(source, line0, cat, lines, count, column):
        def step(i, carry):
            start = (line0 + i) * width + CW + CW + column
            for tap in range(3):
                cat[i, :, tap * chans : (tap + 1) * chans] = source[
                    pl.ds(start + (tap - 1), count)
                ].astype(BF16)
            return carry

        lax.fori_loop(0, lines, step, 0)

    def conv(cat, pairs, big):
        lines = [
            jnp.concatenate([cat[2 * i + j] for i in range(pairs)], axis=0) for j in range(4)
        ]
        return jnp.dot(jnp.concatenate(lines, axis=1), big, preferred_element_type=F32)

    big = conv_weights(w_fpn)
    lines_a, lines_b = half + 4, half + 4 + 2 * MO
    gather(lat.at[0], HB - HA + half * date, cat_a, lines_a + 2, width, -CW)
    gather(lat.at[1], half * date, cat_b, lines_b + 2, width, -CW)
    z = conv(cat_a, lines_a // 2, big).astype(BF16)
    for i in range(lines_a // 2):
        for k in range(2):
            pyr_a[2 * i + k] = z[i * width : (i + 1) * width, k * chans : (k + 1) * chans]
    z = conv(cat_b, lines_b // 2, big).astype(BF16).astype(F32)
    for i in range(lines_b // 2):
        for k in range(2):
            start = CW + (2 * i + k) * width
            pyr_b[start : start + width] = z[
                i * width : (i + 1) * width, k * chans : (k + 1) * chans
            ]

    near_row = jnp.clip(row + jnp.where(date == 0, -1, 1), 0, n_rows - 1)
    cells = lax.broadcasted_iota(jnp.int32, (width, chans), 0) - CW
    in_cols = ((cells + col * tile_cols >= 0) & (cells + col * tile_cols < n_cols * tile_cols)).astype(F32)
    tiles = []
    for is_near in (False, True):
        for step in (0, -1, 1):
            r = near_row if is_near else row
            c = jnp.clip(col + step, 0, n_cols - 1)
            there = (col + step >= 0) & (col + step < n_cols)
            if is_near:
                there = there & has_row
            sy, sx = shift[r, c, 0], shift[r, c, 1]
            low = sx + step * tile_cols
            lo, n = {0: (0, width), -1: (0, 16), 1: (width - 16, 16)}[step]
            x = cells[lo : lo + n]
            cols = ((x >= low) & (x < low + tile_cols)).astype(F32) * there.astype(F32)
            tiles.append((is_near, lo, n, sy, sx, cols))

    def line_step(y, carry):
        total = jnp.zeros((width, chans), F32)
        count = jnp.zeros((width, chans), F32)
        for is_near, lo, n, sy, sx, cols in tiles:
            q = y - 2 - sy
            is_own = jnp.where(date == 0, q >= 0, q < half)
            hit = (~is_own if is_near else is_own).astype(F32)
            mask = cols * hit
            start = CW + (q + 2 + MO) * width + lo - sx
            part = jnp.where(mask > 0, pyr_b[pl.ds(start, n)], 0.0)
            if n < width:
                pad = jnp.zeros((width - n, chans), F32)
                order = (lambda p: [p, pad]) if lo == 0 else (lambda p: [pad, p])
                part, mask = jnp.concatenate(order(part), 0), jnp.concatenate(order(mask), 0)
            total, count = total + part, count + mask
        line = first_half * half + y - 2
        in_row = ((line >= 0) & (line < n_rows * tile_rows)).astype(F32)
        level = total / jnp.maximum(count, 1.0)
        value = jnp.abs(pyr_a[y].astype(F32) - level)
        value = jnp.where(jnp.minimum(count, 1.0) * in_cols * in_row > 0, value, 0.0)
        dif[pl.ds(pl.multiple_of(CW + y * width, 8), width)] = value
        return carry

    lax.fori_loop(0, lines_a, line_step, 0)

    gather(dif, 0, cat_d, half + 4, width, -CW)
    z = jnp.maximum(conv(cat_d, half // 2 + 1, conv_weights(w_dec1)) + jnp.concatenate([b_dec1[...]] * 2, 1), 0.0)
    for i in range(half // 2 + 1):
        for k in range(2):
            y = 2 * i + k
            line = first_half * half + y - 1
            in_row = ((line >= 0) & (line < n_rows * tile_rows)).astype(F32)
            start = CW + y * width
            hid[start : start + width] = z[
                i * width : (i + 1) * width, k * chans : (k + 1) * chans
            ] * (in_cols * in_row)
    gather(hid, 0, cat_h, half + 2, tile_cols, 0)
    z = jnp.maximum(conv(cat_h, half // 2, conv_weights(w_dec2)) + jnp.concatenate([b_dec2[...]] * 2, 1), 0.0)
    z = z.astype(BF16)
    weight = jnp.broadcast_to(w_out[...], (16, chans))
    for i in range(half // 2):
        for k in range(2):
            logit = lax.dot_general(
                weight,
                z[i * tile_cols : (i + 1) * tile_cols, k * chans : (k + 1) * chans],
                (((1,), (1,)), ((), ())),
                preferred_element_type=F32,
            )
            y = 2 * i + k
            out_ref[y : y + 1] = logit[:1] + b_out[0]


def per_device(
    sizes, features, scene_shift, w_lat, b_lat, w_fpn, w_dec1, b_dec1, w_dec2, b_dec2, w_out, b_out
):
    n_rows, n_cols, _ = sizes
    tile_rows, tile_cols, chans = features.shape[1:]
    col, date = lax.axis_index("cols"), lax.axis_index("date")
    half, width = tile_rows // 2, tile_cols + 2 * CW
    n_par = 1 if n_cols == 2 else 2
    own = features[0]
    oth = send(own, sizes, lambda r, c, d: (r, c, 1 - d))

    def edge(x, parity):
        return jnp.where(col % 2 == parity, x[:, tile_cols - CW :], x[:, :CW])

    first = date == 0
    for_row = jnp.concatenate(
        [
            jnp.where(first, own[:HA], oth[tile_rows - HA :]),
            jnp.where(first, oth[:HB], own[tile_rows - HB :]),
        ],
        axis=0,
    )

    def over(r, c, d, to_col):
        near = row_partner(r, d, n_rows)
        return (r, c ^ 1 if to_col is None else to_col, d) if near is None else (
            near[0], c if to_col is None else to_col, near[1])

    from_row = send(for_row, sizes, lambda r, c, d: over(r, c, d, None))
    sides, corners = [], []
    for parity in range(n_par):
        for_side = jnp.concatenate([edge(own, parity), edge(oth, parity)], axis=0)
        partner = functools.partial(column_partner, parity=parity, n_cols=n_cols)
        sides.append(send(for_side, sizes, lambda r, c, d: (r, partner(c), d)))
        corners.append(
            send(edge(for_row, parity), sizes, lambda r, c, d: over(r, c, d, partner(c)))
        )
    vmem = pl.BlockSpec(memory_space=pltpu.VMEM)
    smem = pl.BlockSpec(memory_space=pltpu.SMEM)
    lines_a, lines_b = half + 4, half + 4 + 2 * MO
    flat = lambda lines: (2 * CW + lines * width, chans)
    return pl.pallas_call(
        functools.partial(body, n_par, n_rows, n_cols, tile_rows, tile_cols),
        out_shape=jax.ShapeDtypeStruct((half, tile_cols), F32),
        in_specs=[smem] + [vmem] * (2 + 2 * n_par + 1) + [vmem] * 8 + [smem],
        out_specs=vmem,
        scratch_shapes=[
            pltpu.VMEM((2,) + flat(tile_rows + 2 * HB), F32),
            pltpu.VMEM((lines_a + 2, width, 3 * chans), BF16),
            pltpu.VMEM((lines_b + 2, width, 3 * chans), BF16),
            pltpu.VMEM((lines_a, width, chans), BF16),
            pltpu.VMEM(flat(lines_b), F32),
            pltpu.VMEM(flat(lines_a), F32),
            pltpu.VMEM((half + 4, width, 3 * chans), BF16),
            pltpu.VMEM(flat(half + 2), F32),
            pltpu.VMEM((half + 2, tile_cols, 3 * chans), BF16),
        ],
        compiler_params=pltpu.CompilerParams(vmem_limit_bytes=40 * 2**20),
        name="change",
    )(
        scene_shift, own, oth, *sides, from_row, *corners,
        w_lat, b_lat[None], w_fpn, w_dec1, b_dec1[None], w_dec2, b_dec2[None], w_out[None], b_out,
    )


def solution(mesh):
    sizes = (mesh.shape["rows"], mesh.shape["cols"], mesh.shape["date"])
    return jax.shard_map(
        functools.partial(per_device, sizes),
        mesh=mesh,
        in_specs=(P("date", ("groups", "rows"), "cols", None), P("groups", None, None)) + (P(),) * 9,
        out_specs=P(("groups", "rows", "date"), "cols"),
        check_vma=False,
    )
```

time: 106 us -> 22.8 us (0.22)
  the two profiles are of different devices: /device:TPU:12 before, /device:TPU:0 now
where the time goes in v1:
time: 22.8 us; the launch traced here: 22.6 us
  Pallas kernels  8.8 us (39%)
  starting transfers between devices  5.55 us (24%)
  waiting for transfers between devices  4.91 us (22%)
  other arithmetic  1.82 us (8%)
  between operations  0.81 us (4%)
  local copies, waits for them, and re-layouts  0.76 us (3%)
    pallas_call x1, Pallas kernels, per_device(): pl.pallas_call(functools.partial(body, n_par, n_rows, n_cols, tile_rows,...  8.8 us
    ppermute x4, starting transfers between devices, send(): return lax.ppermute(value, ('rows', 'cols', 'date'), pairs)  5.55 us
    ppermute x4, waiting for transfers between devices, send(): return lax.ppermute(value, ('rows', 'cols', 'date'), pairs)  4.91 us
    select_n x1, other arithmetic, per_device(): jnp.where(first, oth[:HB], own[tile_rows - HB:])  0.96 us
    select_n x3, other arithmetic, edge(): return jnp.where(col % 2 == parity, x[:, tile_cols - CW:], x[:, :CW])  0.8 us
    unnamed x21, local copies, waits for them, and re-layouts  0.76 us
  transfers between devices with their start and end apart: 4, of which 2 were waited for; matrix products, arithmetic and copies ran while one was open for 4% of the time, Pallas kernels for 0%

profile of v1, /device:TPU:0, one launch (start us, length us, event | category | flops | bytes accessed | tf_op | source)
XLA Modules:
  0.0 22.6 jit_solution(6623687426908073839)
XLA Ops:
  0.0 0.5 %collective-permute-start = (bf16[16,128,128]{2,1,0:T(8,128)(2,1)}, bf16[16,128,128]{2,1,0:T(8,128)(2,1)S(1)}, u32[]{:S(2)}, u32[]{:S(2)}) collective-permute-start(bf16[16,128,128]{2,1,0:T(8,128)(2,1)} %bitcast.9), channel_id=1, source_target_pairs={{0,1},{1,0},{2,3},{3,2},{4,5},{5,4},{6,7},{7,6},{8,9},{9,8},{10,11... | collective-permute-start | bytes 1572872 | tf_op jit(solution)/shard_map/ppermute | solution.py:37
  0.5 0.8 %slice_select_fusion.3 = bf16[16,8,128]{2,1,0:T(8,128)(2,1)S(1)} fusion(bf16[16,128,128]{2,1,0:T(8,128)(2,1)} %bitcast.10, pred[]{:T(512)S(6)} %eq.12), kind=kLoop, calls=%fused_computation.9 | loop fusion | flops 16384 | bytes 98305 | tf_op jit(solution)/shard_map/jit(_where)/select_n | solution.py:224
  1.3 1.0 %collective-permute-done.oth = bf16[16,128,128]{2,1,0:T(8,128)(2,1)S(1)} collective-permute-done((bf16[16,128,128]{2,1,0:T(8,128)(2,1)}, bf16[16,128,128]{2,1,0:T(8,128)(2,1)S(1)}, u32[]{:S(2)}, u32[]{:S(2)}) %collective-permute-start) | collective-permute-done | bytes 524320 | tf_op jit(solution)/shard_map/ppermute | solution.py:37
  2.2 1.0 %slice_select_fusion = bf16[7,128,128]{2,1,0:T(8,128)(2,1)S(1)} fusion(bf16[16,128,128]{2,1,0:T(8,128)(2,1)S(1)} %collective-permute-done.oth, bf16[1,16,128,128]{3,2,1,0:T(8,128)(2,1)} %param.11, pred[]{:T(512)S(6)} %eq.13), kind=kLoop, calls=%fused_computation.5 | loop fusion | flops 114688 | bytes 688129 | tf_op jit(solution)/shard_map/jit(_where)/select_n | solution.py:230
  3.2 0.0 copy-done
  3.2 0.0 copy-start.9
  3.3 0.0 copy-start.3
  3.3 0.0 copy-start.4
  3.3 0.0 copy-start.1
  3.3 0.0 copy-start.2
  3.3 2.9 %collective-permute-start.2 = (bf16[10,128,128]{2,1,0:T(8,128)(2,1)S(1)}, bf16[10,128,128]{2,1,0:T(8,128)(2,1)S(1)}, u32[]{:S(2)}, u32[]{:S(2)}) collective-permute-start(bf16[10,128,128]{2,1,0:T(8,128)(2,1)S(1)} %pad_maximum_fusion), channel_id=1, source_target_pairs={{0,2},{1,4},{2,0},{3,6},{4,1},{5,8},{6,3},{7,10},{8,5},{9,12},{10,... | collective-permute-start | bytes 983048 | tf_op jit(solution)/shard_map/ppermute | solution.py:37
  6.3 0.1 collective-permute-start.1
  6.4 2.1 %collective-permute-start.3 = (bf16[10,8,128]{2,1,0:T(8,128)(2,1)S(1)}, bf16[10,8,128]{2,1,0:T(8,128)(2,1)S(1)}, u32[]{:S(2)}, u32[]{:S(2)}) collective-permute-start(bf16[10,8,128]{2,1,0:T(8,128)(2,1)S(1)} %fusion.2), channel_id=1, source_target_pairs={{0,2},{1,6},{2,0},{3,4},{4,3},{5,10},{6,1},{7,8},{8,7},{9,14},{10,... | collective-permute-start | bytes 61448 | tf_op jit(solution)/shard_map/ppermute | solution.py:37
  8.5 0.0 copy-done.9
  8.5 0.1 copy.12.shift
  9.2 3.9 %collective-permute-done.3.refs_2_ = bf16[10,8,128]{2,1,0:T(8,128)(2,1)S(1)} collective-permute-done((bf16[10,8,128]{2,1,0:T(8,128)(2,1)S(1)}, bf16[10,8,128]{2,1,0:T(8,128)(2,1)S(1)}, u32[]{:S(2)}, u32[]{:S(2)}) %collective-permute-start.3) | collective-permute-done | bytes 20512 | tf_op jit(solution)/shard_map/ppermute | solution.py:37
  13.2 0.0 collective-permute-done.1.refs_0_
  13.2 0.0 collective-permute-done.2.refs_1_
  13.2 0.0 copy-start.6
  13.2 0.0 copy-start.7
  13.2 0.6 %copy-done.5 = f32[128]{0:T(128)S(1)} copy-done((f32[128]{0:T(128)S(1)}, f32[128]{0:T(128)}, u32[]{:S(2)}) %copy-start.5) | copy-done | bytes 536
  13.8 0.0 copy-done.6
  13.8 0.0 copy-done.7
  13.9 8.8 %change.1 = f32[8,128]{1,0:T(8,128)} custom-call(s32[4,2,2]{2,1,0:T(2,128)S(1)} %copy.12.shift, bf16[16,128,128]{2,1,0:T(8,128)(2,1)S(1)} %bitcast.11, bf16[16,128,128]{2,1,0:T(8,128)(2,1)S(1)} %collective-permute-done.oth, bf16[32,8,128]{2,1,0:T(8,128)(2,1)S(1)} %collective-permute-done.1.refs_0_, bf16[10,128,128]{2,1,0:T(8,128)(2,1)S(1)} %collective-permute-done.2.refs_1_, ...), custom_call_target="tpu_custom_call" | custom-call | tf_op jit(solution)/shard_map/change/pallas_call | solution.py:253
  (13 shorter events, 0.1 us)
Async XLA Ops:
  0.0 3.2 %copy-start = (bf16[1,16,128,128]{3,2,1,0:T(8,128)(2,1)S(1)}, bf16[1,16,128,128]{3,2,1,0:T(8,128)(2,1)}, u32[]{:S(2)}) copy-start(bf16[1,16,128,128]{3,2,1,0:T(8,128)(2,1)} %param.11) | copy-start | bytes 1572868
  0.0 2.2 %collective-permute-start = (bf16[16,128,128]{2,1,0:T(8,128)(2,1)}, bf16[16,128,128]{2,1,0:T(8,128)(2,1)S(1)}, u32[]{:S(2)}, u32[]{:S(2)}) collective-permute-start(bf16[16,128,128]{2,1,0:T(8,128)(2,1)} %bitcast.9), channel_id=1, source_target_pairs={{0,1},{1,0},{2,3},{3,2},{4,5},{5,4},{6,7},{7,6},{8,9},{9,8},{10,11... | collective-permute-start | bytes 1572872 | tf_op jit(solution)/shard_map/ppermute | solution.py:37
  3.2 5.2 %copy-start.9 = (s32[4,2,2]{0,2,1:T(2,128)S(1)}, s32[4,2,2]{0,2,1:T(2,128)}, u32[]{:S(2)}) copy-start(s32[4,2,2]{0,2,1:T(2,128)} %param.12) | copy-start | bytes 196
  3.3 9.9 %copy-start.3 = (bf16[3,3,128,128]{3,2,1,0:T(8,128)(2,1)S(1)}, bf16[3,3,128,128]{3,2,1,0:T(8,128)(2,1)}, u32[]{:S(2)}) copy-start(bf16[3,3,128,128]{3,2,1,0:T(8,128)(2,1)} %refs_8_.1) | copy-start | bytes 884740
  3.3 9.9 %copy-start.4 = (bf16[128,128]{1,0:T(8,128)(2,1)S(1)}, bf16[128,128]{1,0:T(8,128)(2,1)}, u32[]{:S(2)}) copy-start(bf16[128,128]{1,0:T(8,128)(2,1)} %refs_3_.1) | copy-start | bytes 98308
  3.3 9.9 %copy-start.1 = (bf16[3,3,128,128]{3,2,1,0:T(8,128)(2,1)S(1)}, bf16[3,3,128,128]{3,2,1,0:T(8,128)(2,1)}, u32[]{:S(2)}) copy-start(bf16[3,3,128,128]{3,2,1,0:T(8,128)(2,1)} %refs_5_.1) | copy-start | bytes 884740
  3.3 9.9 %copy-start.2 = (bf16[3,3,128,128]{3,2,1,0:T(8,128)(2,1)S(1)}, bf16[3,3,128,128]{3,2,1,0:T(8,128)(2,1)}, u32[]{:S(2)}) copy-start(bf16[3,3,128,128]{3,2,1,0:T(8,128)(2,1)} %refs_6_.1) | copy-start | bytes 884740
  3.3 9.8 %collective-permute-start.2 = (bf16[10,128,128]{2,1,0:T(8,128)(2,1)S(1)}, bf16[10,128,128]{2,1,0:T(8,128)(2,1)S(1)}, u32[]{:S(2)}, u32[]{:S(2)}) collective-permute-start(bf16[10,128,128]{2,1,0:T(8,128)(2,1)S(1)} %pad_maximum_fusion), channel_id=1, source_target_pairs={{0,2},{1,4},{2,0},{3,6},{4,1},{5,8},{6,3},{7,10},{8,5},{9,12},{10,... | collective-permute-start | bytes 983048 | tf_op jit(solution)/shard_map/ppermute | solution.py:37
  6.3 6.9 %collective-permute-start.1 = (bf16[32,8,128]{2,1,0:T(8,128)(2,1)S(1)}, bf16[32,8,128]{2,1,0:T(8,128)(2,1)S(1)}, u32[]{:S(2)}, u32[]{:S(2)}) collective-permute-start(bf16[32,8,128]{2,1,0:T(8,128)(2,1)S(1)} %pad_maximum_fusion.1), channel_id=1, source_target_pairs={{0,2},{1,3},{2,0},{3,1},{4,6},{5,7},{6,4},{7,5},{8,10},{9,11},{10,... | collective-permute-start | bytes 196616 | tf_op jit(solution)/shard_map/ppermute | solution.py:37
  6.4 6.9 %copy-start.8 = (bf16[128]{0:T(256)(128)(2,1)S(1)}, bf16[128]{0:T(256)(128)(2,1)}, u32[]{:S(2)}) copy-start(bf16[128]{0:T(256)(128)(2,1)} %param.20) | copy-start | bytes 772
  6.4 6.8 %collective-permute-start.3 = (bf16[10,8,128]{2,1,0:T(8,128)(2,1)S(1)}, bf16[10,8,128]{2,1,0:T(8,128)(2,1)S(1)}, u32[]{:S(2)}, u32[]{:S(2)}) collective-permute-start(bf16[10,8,128]{2,1,0:T(8,128)(2,1)S(1)} %fusion.2), channel_id=1, source_target_pairs={{0,2},{1,6},{2,0},{3,4},{4,3},{5,10},{6,1},{7,8},{8,7},{9,14},{10,... | collective-permute-start | bytes 61448 | tf_op jit(solution)/shard_map/ppermute | solution.py:37
  13.2 0.7 %copy-start.5 = (f32[128]{0:T(128)S(1)}, f32[128]{0:T(128)}, u32[]{:S(2)}) copy-start(f32[128]{0:T(128)} %param.14) | copy-start | bytes 1540
  13.2 0.7 %copy-start.6 = (f32[128]{0:T(128)S(1)}, f32[128]{0:T(128)}, u32[]{:S(2)}) copy-start(f32[128]{0:T(128)} %param.17) | copy-start | bytes 1540
  13.2 0.7 %copy-start.7 = (f32[128]{0:T(128)S(1)}, f32[128]{0:T(128)}, u32[]{:S(2)}) copy-start(f32[128]{0:T(128)} %param.19) | copy-start | bytes 1540

commit v2 on v1

v2 whole, which is shorter than its diff:
```python
import functools

import jax
import jax.numpy as jnp
from jax import lax
from jax.experimental import pallas as pl
from jax.experimental.pallas import tpu as pltpu
from jax.sharding import PartitionSpec as P


MO = 4
HA = 3
HB = HA + MO
CW = 8
STRIP = 16
F32 = jnp.float32
BF16 = jnp.bfloat16


def column_partner(col, parity, n_cols):
    right = col % 2 == parity
    return (col + 1) % n_cols if right else (col - 1) % n_cols


def send(value, sizes, target):
    n_groups, n_rows, n_cols, n_dates = sizes

    def place(group, row, col, date):
        return ((group * n_rows + row) * n_cols + col) * n_dates + date

    pairs = []
    for group in range(n_groups):
        for row in range(n_rows):
            for col in range(n_cols):
                for date in range(n_dates):
                    to = target(row, col, date)
                    end = (
                        place((group + 1) % n_groups, row, col, date)
                        if to is None
                        else place(group, *to)
                    )
                    pairs.append((place(group, row, col, date), end))
    return lax.ppermute(value, ("groups", "rows", "cols", "date"), pairs)


def conv_weights(w_ref):
    chans = w_ref.shape[-1]
    tall = w_ref[...].reshape(-1, chans)
    none = jnp.zeros((3 * chans, chans), tall.dtype)
    return jnp.concatenate(
        [jnp.concatenate([tall, none], axis=0), jnp.concatenate([none, tall], axis=0)], axis=1
    )


def at(line, column, width):
    return CW + line * width + CW + column


def position():
    return lax.axis_index("rows"), lax.axis_index("cols"), lax.axis_index("date")


def put(target, line, column, width, value):
    start = at(line, column, width)
    if not isinstance(start, int):
        start = pl.multiple_of(start, 8)
    target[pl.ds(start, value.shape[0])] = value


def gather(source, line, cat, index, count, column, width):
    chans = source.shape[-1]
    start = at(line, column, width)
    for tap in range(3):
        cat[index, :, tap * chans : (tap + 1) * chans] = source[
            pl.ds(start + (tap - 1), count)
        ].astype(BF16)


def conv(parts, big):
    lines = [
        jnp.concatenate(
            [cat[first + 2 * i + j] for cat, first, pairs in parts for i in range(pairs)], axis=0
        )
        for j in range(4)
    ]
    return jnp.dot(jnp.concatenate(lines, axis=1), big, preferred_element_type=F32)


def line_of(z, index, columns):
    chans = z.shape[1] // 2
    pair, k = divmod(index, 2)
    return z[pair * columns : (pair + 1) * columns, k * chans : (k + 1) * chans]


def tile_columns(row, col, there, shift, n_cols, tile_cols, width, chans):
    cells = lax.broadcasted_iota(jnp.int32, (width, chans), 0) - CW
    tiles = []
    for step in (0, -1, 1):
        c = jnp.clip(col + step, 0, n_cols - 1)
        is_tile = there & (col + step >= 0) & (col + step < n_cols)
        sy, sx = shift[row, c, 0], shift[row, c, 1]
        low = sx + step * tile_cols
        lo, n = {0: (0, width), -1: (0, STRIP), 1: (width - STRIP, STRIP)}[step]
        x = cells[lo : lo + n]
        mask = ((x >= low) & (x < low + tile_cols)).astype(F32) * is_tile.astype(F32)
        tiles.append((sy, sx, lo, mask))
    return tiles


def spread(full, left, right):
    return jnp.concatenate(
        [full[:STRIP] + left, full[STRIP:-STRIP], full[-STRIP:] + right], axis=0
    )


def placed(pyr_b, q_of, tiles, hits, width):
    parts = []
    for (sy, sx, lo, mask), hit in zip(tiles, hits, strict=True):
        start = CW + (q_of(sy) + 2 + MO) * width + lo - sx
        value = pyr_b[pl.ds(start, mask.shape[0])] * mask
        parts.append(value if hit is None else value * hit)
    return spread(*parts)


def grid_columns(col, n_cols, tile_cols, width, chans):
    x = lax.broadcasted_iota(jnp.int32, (width, chans), 0) - CW + col * tile_cols
    return ((x >= 0) & (x < n_cols * tile_cols)).astype(F32)


def in_grid(line, n_rows, tile_rows):
    return ((line >= 0) & (line < n_rows * tile_rows)).astype(F32)


def blank_side(lat, lines, col, tile_cols, width):
    column = jnp.where(col % 2 == 0, -CW, tile_cols)
    for line in range(lines):
        put(lat, line, column, width, jnp.zeros((CW, lat.shape[-1]), F32))


def side_of(parity, col, n_cols, tile_cols):
    right = col % 2 == parity
    exists = jnp.where(right, col < n_cols - 1, col > 0).astype(F32)
    return jnp.where(right, tile_cols, -CW), exists


def inner_body(n_par, n_rows, n_cols, tile_rows, tile_cols, shift, own, oth, *refs):
    mine, others = refs[:n_par], refs[n_par : 2 * n_par]
    (w_lat, b_lat, w_fpn, w_dec1, b_dec1,
     pyr_a, pyr_b, cat_a, cat_b, cat_d, hid, lat, dif) = refs[2 * n_par :]
    row, col, date = position()
    half, width, chans = tile_rows // 2, tile_cols + 2 * CW, own.shape[-1]
    weight, bias = w_lat[...], b_lat[...]
    first_half = row * 2 + date

    def lateral(x):
        return jnp.dot(x.reshape(-1, chans), weight, preferred_element_type=F32) + bias

    for which, x_ref, side_refs in ((date, own, mine), (1 - date, oth, others)):
        flat = lat.at[which]
        z = lateral(x_ref[...])
        for t in range(tile_rows):
            put(flat, t, 0, width, z[t * tile_cols : (t + 1) * tile_cols])
        if n_cols == 2:
            blank_side(flat, tile_rows, col, tile_cols, width)
        for parity in range(n_par):
            column, exists = side_of(parity, col, n_cols, tile_cols)
            z = lateral(side_refs[parity][...]) * exists
            for t in range(tile_rows):
                put(flat, t, column, width, z[t * CW : (t + 1) * CW])

    for j in range(half + HA):
        gather(lat.at[0], j + (half - HA) * date, cat_a, j + date, width, -CW, width)
    for j in range(half + HB):
        gather(lat.at[1], j + (half - HB) * date, cat_b, j + date, width, -CW, width)
    pairs_a, pairs_b = half // 2, half // 2 + MO // 2
    z = conv([(cat_a, 1, pairs_a), (cat_b, 1, pairs_b)], conv_weights(w_fpn)).astype(BF16)
    for i in range(2 * pairs_a):
        pyr_a[i + 4 * (1 - date)] = line_of(z, i, width)
    pyr_b[:CW] = jnp.zeros((CW, chans), F32)
    pyr_b[pyr_b.shape[0] - CW :] = jnp.zeros((CW, chans), F32)
    for i in range(2 * pairs_b):
        put(pyr_b, i + (4 + MO) * (1 - date), -CW, width, line_of(z, 2 * pairs_a + i, width).astype(F32))

    tiles = tile_columns(row, col, row >= 0, shift, n_cols, tile_cols, width, chans)
    count = spread(*[mask for *_, mask in tiles])
    inside = grid_columns(col, n_cols, tile_cols, width, chans)
    share = 1.0 / jnp.maximum(count, 1.0)
    keep = jnp.minimum(count, 1.0) * inside
    for i in range(4):
        y = i + half * (1 - date)
        level = placed(pyr_b, lambda sy, y=y: y - 2 - sy, tiles, [None] * 3, width) * share
        value = jnp.abs(pyr_a[y].astype(F32) - level)
        line = first_half * half + y - 2
        put(dif, i, -CW, width, value * (keep * in_grid(line, n_rows, tile_rows)))
    for i in range(4):
        gather(dif, i, cat_d, i, width, -CW, width)
    z = conv([(cat_d, 0, 1)], conv_weights(w_dec1))
    z = jnp.maximum(z + jnp.concatenate([b_dec1[...]] * 2, 1), 0.0)
    for i in range(2):
        line = first_half * half + i + half * (1 - date) - 1
        put(hid, i, -CW, width, line_of(z, i, width) * (inside * in_grid(line, n_rows, tile_rows)))


def outer_body(n_par, n_rows, n_cols, tile_rows, tile_cols, shift, v_ref, *refs):
    corners = refs[:n_par]
    (_, _, t_a, t_b, t_d, t_h, w_lat, b_lat, w_fpn, w_dec1, b_dec1, w_dec2, b_dec2, w_out, b_out,
     out_ref, pyr_a, pyr_b, lat, cat_a, cat_b, dif, cat_d, hid, cat_h) = refs[n_par:]
    row, col, date = position()
    half, width, chans = tile_rows // 2, tile_cols + 2 * CW, w_lat.shape[-1]
    first_half = row * 2 + date
    has_row = jnp.where(date == 0, row > 0, row < n_rows - 1)
    row_keep = has_row.astype(F32)
    weight, bias = w_lat[...], b_lat[...]

    def lateral(x):
        return jnp.dot(x.reshape(-1, chans), weight, preferred_element_type=F32) + bias

    z = lateral(v_ref[...]) * row_keep
    for i in range(HA + HB):
        put(lat, i, 0, width, z[i * tile_cols : (i + 1) * tile_cols])
    if n_cols == 2:
        blank_side(lat, HA + HB, col, tile_cols, width)
    for parity in range(n_par):
        column, exists = side_of(parity, col, n_cols, tile_cols)
        z = lateral(corners[parity][...]) * (exists * row_keep)
        for i in range(HA + HB):
            put(lat, i, column, width, z[i * CW : (i + 1) * CW])
    for i in range(3):
        cat_a[i + HA * (1 - date)] = t_a[i + (half + 1) * date]
        cat_b[i + HB * (1 - date)] = t_b[i + (half + MO + 1) * date]
    for i in range(HA):
        gather(lat, i, cat_a, i + 3 * date, width, -CW, width)
    for i in range(HB):
        gather(lat, i + HA, cat_b, i + 3 * date, width, -CW, width)
    pairs_b = 2 + MO // 2
    z = conv([(cat_a, 0, 2), (cat_b, 0, pairs_b)], conv_weights(w_fpn)).astype(BF16)
    for i in range(4):
        pyr_a[i + half * date] = line_of(z, i, width)
    for i in range(2 * pairs_b):
        put(pyr_b, i + (half + MO) * date, -CW, width, line_of(z, 4 + i, width).astype(F32))

    near_row = jnp.clip(row + jnp.where(date == 0, -1, 1), 0, n_rows - 1)
    tiles = tile_columns(row, col, row >= 0, shift, n_cols, tile_cols, width, chans)
    near = tile_columns(near_row, col, has_row, shift, n_cols, tile_cols, width, chans)
    inside = grid_columns(col, n_cols, tile_cols, width, chans)
    for i in range(half):
        y = i + 4 * date
        q_of = lambda sy, y=y: y - 2 - sy

        def is_own(sy):
            return jnp.where(date == 0, q_of(sy) >= 0, q_of(sy) < half).astype(F32)

        own_hits = [is_own(sy) for sy, *_ in tiles]
        near_hits = [1.0 - is_own(sy) for sy, *_ in near]
        total = placed(pyr_b, q_of, tiles, own_hits, width) + placed(pyr_b, q_of, near, near_hits, width)
        count = spread(*[t[-1] * h for t, h in zip(tiles, own_hits)]) + spread(*[t[-1] * h for t, h in zip(near, near_hits)])
        value = jnp.abs(pyr_a[y].astype(F32) - total / jnp.maximum(count, 1.0))
        line = first_half * half + y - 2
        keep = jnp.minimum(count, 1.0) * inside * in_grid(line, n_rows, tile_rows)
        put(dif, i, -CW, width, value * keep)

    for i in range(2):
        cat_d[i + half * (1 - date)] = t_d[i + 2 * date]
        put(hid, i + half * (1 - date), -CW, width, t_h[pl.ds(CW + i * width, width)])
    for i in range(half):
        gather(dif, i, cat_d, i + 2 * date, width, -CW, width)
    z = conv([(cat_d, 0, half // 2)], conv_weights(w_dec1))
    z = jnp.maximum(z + jnp.concatenate([b_dec1[...]] * 2, 1), 0.0)
    for i in range(half):
        y = i + 2 * date
        line = first_half * half + y - 1
        put(hid, y, -CW, width, line_of(z, i, width) * (inside * in_grid(line, n_rows, tile_rows)))
    for i in range(half + 2):
        gather(hid, i, cat_h, i, tile_cols, 0, width)
    z = conv([(cat_h, 0, half // 2)], conv_weights(w_dec2))
    z = jnp.maximum(z + jnp.concatenate([b_dec2[...]] * 2, 1), 0.0).astype(BF16)
    weight = jnp.broadcast_to(w_out[...], (16, chans))
    for i in range(half):
        logit = lax.dot_general(
            weight, line_of(z, i, tile_cols), (((1,), (1,)), ((), ())), preferred_element_type=F32
        )
        out_ref[i : i + 1] = logit[:1] + b_out[0]


def per_device(
    sizes, features, scene_shift, w_lat, b_lat, w_fpn, w_dec1, b_dec1, w_dec2, b_dec2, w_out, b_out
):
    _, n_rows, n_cols, _ = sizes
    tile_rows, tile_cols, chans = features.shape[1:]
    col, date = lax.axis_index("cols"), lax.axis_index("date")
    half, width = tile_rows // 2, tile_cols + 2 * CW
    n_par = 1 if n_cols == 2 else 2
    own = features[0]
    first = date == 0

    def swap(value):
        return send(value, sizes, lambda r, c, d: (r, c, 1 - d))

    def edge(x, parity):
        return jnp.where(col % 2 == parity, x[:, tile_cols - CW :], x[:, :CW])

    def partner(c, parity):
        return column_partner(c, parity, n_cols)

    oth = swap(own)

    def shift_row(r, c, d):
        near = r - 1 + 2 * d
        return (near, c, 1 - d) if 0 <= near < n_rows else None

    def corner(p, r, c, d):
        near = shift_row(r, c, d)
        return None if near is None else (near[0], partner(c, p), near[2])

    mine, corners, others = [], [], []
    for p in range(n_par):
        mine.append(send(edge(own, p), sizes, lambda r, c, d, p=p: (r, partner(c, p), d)))
    rows_own = lax.dynamic_slice_in_dim(own, (tile_rows - HB) * date, HB, 0)
    rows_own = lax.optimization_barrier(rows_own)
    rows_oth = lax.dynamic_slice_in_dim(oth, (tile_rows - HB) * date, HB, 0)
    for_row = jnp.concatenate(
        [
            jnp.where(first, rows_own[:HA], rows_oth[HB - HA :]),
            jnp.where(first, rows_oth, rows_own),
        ],
        axis=0,
    )
    from_row = send(for_row, sizes, shift_row)
    for p in range(n_par):
        corners.append(send(edge(for_row, p), sizes, functools.partial(corner, p)))
    for p in range(n_par):
        others.append(swap(mine[p]))

    vmem = pl.BlockSpec(memory_space=pltpu.VMEM)
    smem = pl.BlockSpec(memory_space=pltpu.SMEM)
    lines_a, lines_b = half + 4, half + 4 + 2 * MO

    def flat(lines, kind=F32):
        return jax.ShapeDtypeStruct((2 * CW + lines * width, chans), kind)

    def cat(lines, columns=width):
        return jax.ShapeDtypeStruct((lines, columns, 3 * chans), BF16)

    def scratch(shape):
        return pltpu.VMEM(shape.shape, shape.dtype)

    row_a = jax.ShapeDtypeStruct((lines_a, width, chans), BF16)
    lat_tile = flat(tile_rows)
    pyr_a, pyr_b, *kept = pl.pallas_call(
        functools.partial(inner_body, n_par, n_rows, n_cols, tile_rows, tile_cols),
        out_shape=(row_a, flat(lines_b), cat(half + HA + 1), cat(half + HB + 1), cat(4), flat(2)),
        in_specs=[smem] + [vmem] * (2 + 2 * n_par + 5),
        out_specs=(vmem,) * 6,
        scratch_shapes=[pltpu.VMEM((2,) + lat_tile.shape, F32), scratch(flat(4))],
        compiler_params=pltpu.CompilerParams(vmem_limit_bytes=24 * 2**20),
        cost_estimate=pl.CostEstimate(
            flops=2 * 10 * width * 1536 * 256, bytes_accessed=8 * 2**20, transcendentals=0
        ),
        name="inner",
    )(scene_shift, own, oth, *mine, *others, w_lat, b_lat[None], w_fpn, w_dec1, b_dec1[None])
    out, _, _ = pl.pallas_call(
        functools.partial(outer_body, n_par, n_rows, n_cols, tile_rows, tile_cols),
        out_shape=(jax.ShapeDtypeStruct((half, tile_cols), F32), row_a, flat(lines_b)),
        in_specs=[smem] + [vmem] * (n_par + 1 + 14) + [smem],
        out_specs=(vmem,) * 3,
        input_output_aliases={n_par + 2: 1, n_par + 3: 2},
        scratch_shapes=[
            scratch(flat(HA + HB)),
            scratch(cat(HA + 3)),
            scratch(cat(HB + 3)),
            scratch(flat(half)),
            scratch(cat(half + 2)),
            scratch(flat(half + 2)),
            scratch(cat(half + 2, tile_cols)),
        ],
        compiler_params=pltpu.CompilerParams(vmem_limit_bytes=24 * 2**20),
        name="outer",
    )(
        scene_shift, from_row, *corners, pyr_a, pyr_b, *kept,
        w_lat, b_lat[None], w_fpn, w_dec1, b_dec1[None], w_dec2, b_dec2[None], w_out[None], b_out,
    )
    return out


def staged(sizes, *args):
    return per_device(sizes, *args)


def solution(mesh):
    sizes = tuple(mesh.shape[axis] for axis in ("groups", "rows", "cols", "date"))
    return jax.shard_map(
        functools.partial(staged, sizes),
        mesh=mesh,
        in_specs=(P("date", ("groups", "rows"), "cols", None), P("groups", None, None)) + (P(),) * 9,
        out_specs=P(("groups", "rows", "date"), "cols"),
        check_vma=False,
    )
```

time: 22.8 us -> 20.7 us (0.908)
  the two profiles are of different devices: /device:TPU:0 before, /device:TPU:1 now
where the time goes in v2:
time: 20.7 us; the launch traced here: 20.6 us
  Pallas kernels  9.52 us (46%)
  starting transfers between devices  6.77 us (33%)
  waiting for transfers between devices  2.14 us (10%)
  local copies, waits for them, and re-layouts  1.19 us (6%)
  between operations  0.85 us (4%)
    ppermute x5, starting transfers between devices, send(): return lax.ppermute(value, ('groups', 'rows', 'cols', 'date'), pairs)  6.77 us
    pallas_call x1, Pallas kernels, per_device(): pl.pallas_call(functools.partial(outer_body, n_par, n_rows, n_cols, tile_...  5.81 us
    pallas_call x1, Pallas kernels, per_device(): pl.pallas_call(functools.partial(inner_body, n_par, n_rows, n_cols, tile_...  3.71 us
    ppermute x5, waiting for transfers between devices, send(): return lax.ppermute(value, ('groups', 'rows', 'cols', 'date'), pairs)  2.14 us
    dynamic_slice x1, local copies, waits for them, and re-layouts, per_device(): rows_own = lax.dynamic_slice_in_dim(own, (tile_rows - HB) * date, HB, 0)  1.05 us
  transfers between devices with their start and end apart: 5, of which 2 were waited for; matrix products, arithmetic and copies ran while one was open for 6% of the time, Pallas kernels for 18%

profile of v2, /device:TPU:1, one launch (start us, length us, event | category | flops | bytes accessed | tf_op | source)
XLA Modules:
  0.0 20.6 jit_solution(8007492388994144845)
XLA Ops:
  0.0 0.0 copy-start
  0.0 0.0 copy-start.4
  0.0 0.0 copy-start.6
  0.0 0.0 copy-start.5
  0.0 0.1 collective-permute-start
  0.1 1.0 %dynamic-slice_bitcast_fusion = bf16[7,128,128]{2,1,0:T(8,128)(2,1)S(1)} fusion(bf16[1,16,128,128]{3,2,1,0:T(8,128)(2,1)} %param.11, s32[]{:T(128)S(6)} %select_n.46), kind=kLoop, calls=%fused_computation.6 | loop fusion | bytes 458756 | tf_op jit(solution)/shard_map/dynamic_slice | solution.py:318
  1.2 1.0 %collective-permute-done.oth = bf16[16,128,128]{2,1,0:T(8,128)(2,1)S(1)} collective-permute-done((bf16[16,128,128]{2,1,0:T(8,128)(2,1)}, bf16[16,128,128]{2,1,0:T(8,128)(2,1)S(1)}, u32[]{:S(2)}, u32[]{:S(2)}) %collective-permute-start) | collective-permute-done | bytes 524320 | tf_op jit(solution)/shard_map/ppermute | solution.py:43
  2.3 2.7 %collective-permute-start.1 = (bf16[10,128,128]{2,1,0:T(8,128)(2,1)S(1)}, bf16[10,128,128]{2,1,0:T(8,128)(2,1)S(1)}, u32[]{:S(2)}, u32[]{:S(2)}) collective-permute-start(bf16[10,128,128]{2,1,0:T(8,128)(2,1)S(1)} %pad_maximum_fusion), channel_id=1, source_target_pairs={{0,16},{1,4},{2,18},{3,6},{4,1},{5,8},{6,3},{7,10},{8,5},{9,12},{1... | collective-permute-start | bytes 983048 | tf_op jit(solution)/shard_map/ppermute | solution.py:43
  5.1 0.0 copy-done.3
  5.1 1.3 %collective-permute-start.3 = (bf16[16,8,128]{2,1,0:T(8,128)(2,1)S(1)}, bf16[16,8,128]{2,1,0:T(8,128)(2,1)S(1)}, u32[]{:S(2)}, u32[]{:S(2)}) collective-permute-start(bf16[16,8,128]{2,1,0:T(8,128)(2,1)S(1)} %slice_select_fusion), channel_id=1, source_target_pairs={{0,2},{1,3},{2,0},{3,1},{4,6},{5,7},{6,4},{7,5},{8,10},{9,11},{10,... | collective-permute-start | bytes 98312 | tf_op jit(solution)/shard_map/ppermute | solution.py:43
  7.0 0.1 copy.15.shift
  7.1 1.1 %collective-permute-done.3.refs_0_ = bf16[16,8,128]{2,1,0:T(8,128)(2,1)S(1)} collective-permute-done((bf16[16,8,128]{2,1,0:T(8,128)(2,1)S(1)}, bf16[16,8,128]{2,1,0:T(8,128)(2,1)S(1)}, u32[]{:S(2)}, u32[]{:S(2)}) %collective-permute-start.3) | collective-permute-done | bytes 32800 | tf_op jit(solution)/shard_map/ppermute | solution.py:43
  8.2 1.2 %collective-permute-start.4 = (bf16[16,8,128]{2,1,0:T(8,128)(2,1)S(1)}, bf16[16,8,128]{2,1,0:T(8,128)(2,1)S(1)}, u32[]{:S(2)}, u32[]{:S(2)}) collective-permute-start(bf16[16,8,128]{2,1,0:T(8,128)(2,1)S(1)} %collective-permute-done.3.refs_0_), channel_id=1, source_target_pairs={{0,1},{1,0},{2,3},{3,2},{4,5},{5,4},{6,7},{7,6},{8,9},{9,8},{10,11... | collective-permute-start | bytes 98312 | tf_op jit(solution)/shard_map/ppermute | solution.py:43
  9.4 1.5 %collective-permute-start.2 = (bf16[10,8,128]{2,1,0:T(8,128)(2,1)S(1)}, bf16[10,8,128]{2,1,0:T(8,128)(2,1)S(1)}, u32[]{:S(2)}, u32[]{:S(2)}) collective-permute-start(bf16[10,8,128]{2,1,0:T(8,128)(2,1)S(1)} %fusion.2), channel_id=1, source_target_pairs={{0,16},{1,6},{2,18},{3,4},{4,3},{5,10},{6,1},{7,8},{8,7},{9,14},{1... | collective-permute-start | bytes 61448 | tf_op jit(solution)/shard_map/ppermute | solution.py:43
  10.9 0.0 collective-permute-done.4.refs_1_
  10.9 0.0 copy-done.4
  10.9 0.0 copy-done.6
  11.0 0.0 copy-start.2
  11.0 0.0 copy-start.7
  11.0 0.0 copy-start.8
  11.0 3.7 %inner.1 = (bf16[12,144,128]{2,1,0:T(8,128)(2,1)S(1)}, f32[2896,128]{1,0:T(8,128)S(1)}, bf16[12,144,384]{2,1,0:T(8,128)(2,1)S(1)}, bf16[16,144,384]{2,1,0:T(8,12...) custom-call(s32[4,2,2]{2,1,0:T(2,128)S(1)} %copy.15.shift, bf16[16,128,128]{2,1,0:T(8,128)(2,1)S(1)} %bitcast.9, ...), custom_call_target="tpu_custom_call" | custom-call | flops 1132462080 | bytes 8388608 | tf_op jit(solution)/shard_map/inner/pallas_call | solution.py:349
  14.7 0.0 collective-permute-done.2.refs_0_
  14.7 0.0 collective-permute-done.1.v_ref
  14.8 5.8 %outer.1 = (f32[8,128]{1,0:T(8,128)}, bf16[12,144,128]{2,1,0:T(8,128)(2,1)S(1)}, f32[2896,128]{1,0:T(8,128)S(1)}) custom-call(s32[4,2,2]{2,1,0:T(2,128)S(1)} %copy.15.shift, bf16[10,128,128]{2,1,0:T(8,128)(2,1)S(1)} %collective-permute-done.1.v_ref, ...), custom_call_target="tpu_custom_call", output_to_operand_aliasing={{1}: (3, {}), {2}: (4, {})} | custom-call | tf_op jit(solution)/shard_map/outer/pallas_call | solution.py:361
  (15 shorter events, 0.1 us)
Async XLA Ops:
  0.0 5.1 %copy-start.3 = (bf16[1,16,128,128]{3,2,1,0:T(8,128)(2,1)S(1)}, bf16[1,16,128,128]{3,2,1,0:T(8,128)(2,1)}, u32[]{:S(2)}) copy-start(bf16[1,16,128,128]{3,2,1,0:T(8,128)(2,1)} %param.11) | copy-start | bytes 1572868
  0.0 7.0 %copy-start.9 = (s32[4,2,2]{0,2,1:T(2,128)S(1)}, s32[4,2,2]{0,2,1:T(2,128)}, u32[]{:S(2)}) copy-start(s32[4,2,2]{0,2,1:T(2,128)} %param.12) | copy-start | bytes 196
  0.0 10.9 %copy-start.1 = (bf16[3,3,128,128]{3,2,1,0:T(8,128)(2,1)S(1)}, bf16[3,3,128,128]{3,2,1,0:T(8,128)(2,1)}, u32[]{:S(2)}) copy-start(bf16[3,3,128,128]{3,2,1,0:T(8,128)(2,1)} %refs_10_.1) | copy-start | bytes 884740
  0.0 10.9 %copy-start = (bf16[3,3,128,128]{3,2,1,0:T(8,128)(2,1)S(1)}, bf16[3,3,128,128]{3,2,1,0:T(8,128)(2,1)}, u32[]{:S(2)}) copy-start(bf16[3,3,128,128]{3,2,1,0:T(8,128)(2,1)} %refs_9_.1) | copy-start | bytes 884740
  0.0 10.9 %copy-start.4 = (bf16[128,128]{1,0:T(8,128)(2,1)S(1)}, bf16[128,128]{1,0:T(8,128)(2,1)}, u32[]{:S(2)}) copy-start(bf16[128,128]{1,0:T(8,128)(2,1)} %refs_7_.1) | copy-start | bytes 98308
  0.0 10.9 %copy-start.6 = (f32[128]{0:T(128)S(1)}, f32[128]{0:T(128)}, u32[]{:S(2)}) copy-start(f32[128]{0:T(128)} %param.17) | copy-start | bytes 1540
  0.0 10.9 %copy-start.5 = (f32[128]{0:T(128)S(1)}, f32[128]{0:T(128)}, u32[]{:S(2)}) copy-start(f32[128]{0:T(128)} %param.14) | copy-start | bytes 1540
  0.0 2.2 %collective-permute-start = (bf16[16,128,128]{2,1,0:T(8,128)(2,1)}, bf16[16,128,128]{2,1,0:T(8,128)(2,1)S(1)}, u32[]{:S(2)}, u32[]{:S(2)}) collective-permute-start(bf16[16,128,128]{2,1,0:T(8,128)(2,1)} %bitcast.7), channel_id=1, source_target_pairs={{0,1},{1,0},{2,3},{3,2},{4,5},{5,4},{6,7},{7,6},{8,9},{9,8},{10,11... | collective-permute-start | bytes 1572872 | tf_op jit(solution)/shard_map/ppermute | solution.py:43
  2.3 12.4 %collective-permute-start.1 = (bf16[10,128,128]{2,1,0:T(8,128)(2,1)S(1)}, bf16[10,128,128]{2,1,0:T(8,128)(2,1)S(1)}, u32[]{:S(2)}, u32[]{:S(2)}) collective-permute-start(bf16[10,128,128]{2,1,0:T(8,128)(2,1)S(1)} %pad_maximum_fusion), channel_id=1, source_target_pairs={{0,16},{1,4},{2,18},{3,6},{4,1},{5,8},{6,3},{7,10},{8,5},{9,12},{1... | collective-permute-start | bytes 983048 | tf_op jit(solution)/shard_map/ppermute | solution.py:43
  5.1 3.1 %collective-permute-start.3 = (bf16[16,8,128]{2,1,0:T(8,128)(2,1)S(1)}, bf16[16,8,128]{2,1,0:T(8,128)(2,1)S(1)}, u32[]{:S(2)}, u32[]{:S(2)}) collective-permute-start(bf16[16,8,128]{2,1,0:T(8,128)(2,1)S(1)} %slice_select_fusion), channel_id=1, source_target_pairs={{0,2},{1,3},{2,0},{3,1},{4,6},{5,7},{6,4},{7,5},{8,10},{9,11},{10,... | collective-permute-start | bytes 98312 | tf_op jit(solution)/shard_map/ppermute | solution.py:43
  8.2 2.7 %collective-permute-start.4 = (bf16[16,8,128]{2,1,0:T(8,128)(2,1)S(1)}, bf16[16,8,128]{2,1,0:T(8,128)(2,1)S(1)}, u32[]{:S(2)}, u32[]{:S(2)}) collective-permute-start(bf16[16,8,128]{2,1,0:T(8,128)(2,1)S(1)} %collective-permute-done.3.refs_0_), channel_id=1, source_target_pairs={{0,1},{1,0},{2,3},{3,2},{4,5},{5,4},{6,7},{7,6},{8,9},{9,8},{10,11... | collective-permute-start | bytes 98312 | tf_op jit(solution)/shard_map/ppermute | solution.py:43
  9.4 5.3 %collective-permute-start.2 = (bf16[10,8,128]{2,1,0:T(8,128)(2,1)S(1)}, bf16[10,8,128]{2,1,0:T(8,128)(2,1)S(1)}, u32[]{:S(2)}, u32[]{:S(2)}) collective-permute-start(bf16[10,8,128]{2,1,0:T(8,128)(2,1)S(1)} %fusion.2), channel_id=1, source_target_pairs={{0,16},{1,6},{2,18},{3,4},{4,3},{5,10},{6,1},{7,8},{8,7},{9,14},{1... | collective-permute-start | bytes 61448 | tf_op jit(solution)/shard_map/ppermute | solution.py:43
  11.0 3.8 %copy-start.2 = (bf16[3,3,128,128]{3,2,1,0:T(8,128)(2,1)S(1)}, bf16[3,3,128,128]{3,2,1,0:T(8,128)(2,1)}, u32[]{:S(2)}) copy-start(bf16[3,3,128,128]{3,2,1,0:T(8,128)(2,1)} %refs_12_.1) | copy-start | bytes 884740
  11.0 3.8 %copy-start.7 = (f32[128]{0:T(128)S(1)}, f32[128]{0:T(128)}, u32[]{:S(2)}) copy-start(f32[128]{0:T(128)} %param.19) | copy-start | bytes 1540
  11.0 3.8 %copy-start.8 = (bf16[128]{0:T(256)(128)(2,1)S(1)}, bf16[128]{0:T(256)(128)(2,1)}, u32[]{:S(2)}) copy-start(bf16[128]{0:T(256)(128)(2,1)} %param.20) | copy-start | bytes 772

commit v3 on v2

--- a/solution.py
+++ b/solution.py
@@ -43,15 +43,6 @@
     return lax.ppermute(value, ("groups", "rows", "cols", "date"), pairs)
 
 
-def conv_weights(w_ref):
-    chans = w_ref.shape[-1]
-    tall = w_ref[...].reshape(-1, chans)
-    none = jnp.zeros((3 * chans, chans), tall.dtype)
-    return jnp.concatenate(
-        [jnp.concatenate([tall, none], axis=0), jnp.concatenate([none, tall], axis=0)], axis=1
-    )
-
-
 def at(line, column, width):
     return CW + line * width + CW + column
 
@@ -68,22 +59,28 @@
 
 
 def gather(source, line, cat, index, count, column, width):
-    chans = source.shape[-1]
     start = at(line, column, width)
     for tap in range(3):
-        cat[index, :, tap * chans : (tap + 1) * chans] = source[
-            pl.ds(start + (tap - 1), count)
-        ].astype(BF16)
-
-
-def conv(parts, big):
-    lines = [
-        jnp.concatenate(
-            [cat[first + 2 * i + j] for cat, first, pairs in parts for i in range(pairs)], axis=0
-        )
-        for j in range(4)
-    ]
-    return jnp.dot(jnp.concatenate(lines, axis=1), big, preferred_element_type=F32)
+        cat[index, tap] = source[pl.ds(start + (tap - 1), count)].astype(BF16)
+
+
+def conv(parts, w_ref, ways=2):
+    taps = w_ref[...].reshape(-1, w_ref.shape[-1])
+    none = jnp.zeros((taps.shape[0] // 3, taps.shape[1]), taps.dtype)
+    tall = jnp.concatenate(
+        [jnp.concatenate([taps, none], axis=0), jnp.concatenate([none, taps], axis=0)], axis=1
+    )
+    tops = [(cat, first + 2 * i) for cat, first, pairs in parts for i in range(pairs)]
+    outs = []
+    for way in range(ways):
+        some = tops[way * len(tops) // ways : (way + 1) * len(tops) // ways]
+        lines = [
+            jnp.concatenate([cat[top + j, tap] for cat, top in some], axis=0)
+            for j in range(4)
+            for tap in range(3)
+        ]
+        outs.append(jnp.dot(jnp.concatenate(lines, axis=1), tall, preferred_element_type=F32))
+    return jnp.concatenate(outs, axis=0)
 
 
 def line_of(z, index, columns):
@@ -92,39 +89,76 @@
     return z[pair * columns : (pair + 1) * columns, k * chans : (k + 1) * chans]
 
 
-def tile_columns(row, col, there, shift, n_cols, tile_cols, width, chans):
-    cells = lax.broadcasted_iota(jnp.int32, (width, chans), 0) - CW
+def tile_columns(row, col, there, shift, n_cols, tile_cols, chans):
+    cells = lax.broadcasted_iota(jnp.int32, (STRIP, chans), 0)
     tiles = []
     for step in (0, -1, 1):
         c = jnp.clip(col + step, 0, n_cols - 1)
-        is_tile = there & (col + step >= 0) & (col + step < n_cols)
+        is_tile = (there & (col + step >= 0) & (col + step < n_cols)).astype(F32)
         sy, sx = shift[row, c, 0], shift[row, c, 1]
         low = sx + step * tile_cols
-        lo, n = {0: (0, width), -1: (0, STRIP), 1: (width - STRIP, STRIP)}[step]
-        x = cells[lo : lo + n]
-        mask = ((x >= low) & (x < low + tile_cols)).astype(F32) * is_tile.astype(F32)
-        tiles.append((sy, sx, lo, mask))
+        masks = []
+        for left in (True, False):
+            x = cells + (-CW if left else tile_cols + CW - STRIP)
+            masks.append(((x >= low) & (x < low + tile_cols)).astype(F32) * is_tile)
+        tiles.append((sy, sx, is_tile, masks[0], masks[1]))
     return tiles
 
 
-def spread(full, left, right):
+def difference(a_line, pyr_b, q_of, groups, inside, keep_line, width):
+    weight, level, count_l, count_r, level_l, level_r = 0.0, None, None, None, None, None
+    plus = lambda x, y: y if x is None else x + y
+    for tiles, hit_of in groups:
+        for k, (sy, sx, is_tile, left, right) in enumerate(tiles):
+            start = CW + (q_of(sy) + 2 + MO) * width - sx
+            hit = None if hit_of is None else hit_of(sy)
+            if k != 2:
+                mask = left if hit is None else left * hit
+                count_l = plus(count_l, mask)
+                level_l = plus(level_l, pyr_b[pl.ds(start, STRIP)] * mask)
+            if k != 1:
+                mask = right if hit is None else right * hit
+                count_r = plus(count_r, mask)
+                level_r = plus(level_r, pyr_b[pl.ds(start + width - STRIP, STRIP)] * mask)
+            if k == 0:
+                value = pyr_b[pl.ds(start + STRIP, width - 2 * STRIP)]
+                if hit is None:
+                    level = plus(level, value)
+                else:
+                    weight = weight + hit * is_tile
+                    level = plus(level, value * (hit * is_tile))
+    a = a_line.astype(F32)
+    outs = []
+    for part, count, total, edge in (
+        (a[:STRIP], count_l, level_l, inside[0]),
+        (a[width - STRIP :], count_r, level_r, inside[1]),
+    ):
+        value = jnp.abs(part - total / jnp.maximum(count, 1.0))
+        outs.append(value * (jnp.minimum(count, 1.0) * edge * keep_line))
+    if groups[0][1] is None:
+        middle = jnp.abs(a[STRIP : width - STRIP] - level) * keep_line
+    else:
+        share = jnp.where(weight > 1.5, 0.5, 1.0)
+        middle = jnp.abs(a[STRIP : width - STRIP] - level * share) * (jnp.minimum(weight, 1.0) * keep_line)
+    return jnp.concatenate([outs[0], middle, outs[1]], axis=0)
+
+
+def grid_columns(col, n_cols, tile_cols, chans):
+    x = lax.broadcasted_iota(jnp.int32, (STRIP, chans), 0) + col * tile_cols
+    return [
+        ((x + at >= 0) & (x + at < n_cols * tile_cols)).astype(F32) for at in (-CW, tile_cols + CW - STRIP)
+    ]
+
+
+def on_grid(line, inside, keep_line):
     return jnp.concatenate(
-        [full[:STRIP] + left, full[STRIP:-STRIP], full[-STRIP:] + right], axis=0
+        [
+            line[:STRIP] * (inside[0] * keep_line),
+            line[STRIP:-STRIP] * keep_line,
+            line[-STRIP:] * (inside[1] * keep_line),
+        ],
+        axis=0,
     )
-
-
-def placed(pyr_b, q_of, tiles, hits, width):
-    parts = []
-    for (sy, sx, lo, mask), hit in zip(tiles, hits, strict=True):
-        start = CW + (q_of(sy) + 2 + MO) * width + lo - sx
-        value = pyr_b[pl.ds(start, mask.shape[0])] * mask
-        parts.append(value if hit is None else value * hit)
-    return spread(*parts)
-
-
-def grid_columns(col, n_cols, tile_cols, width, chans):
-    x = lax.broadcasted_iota(jnp.int32, (width, chans), 0) - CW + col * tile_cols
-    return ((x >= 0) & (x < n_cols * tile_cols)).astype(F32)
 
 
 def in_grid(line, n_rows, tile_rows):
@@ -173,7 +207,7 @@
     for j in range(half + HB):
         gather(lat.at[1], j + (half - HB) * date, cat_b, j + date, width, -CW, width)
     pairs_a, pairs_b = half // 2, half // 2 + MO // 2
-    z = conv([(cat_a, 1, pairs_a), (cat_b, 1, pairs_b)], conv_weights(w_fpn)).astype(BF16)
+    z = conv([(cat_a, 1, pairs_a), (cat_b, 1, pairs_b)], w_fpn).astype(BF16)
     for i in range(2 * pairs_a):
         pyr_a[i + 4 * (1 - date)] = line_of(z, i, width)
     pyr_b[:CW] = jnp.zeros((CW, chans), F32)
@@ -181,24 +215,22 @@
     for i in range(2 * pairs_b):
         put(pyr_b, i + (4 + MO) * (1 - date), -CW, width, line_of(z, 2 * pairs_a + i, width).astype(F32))
 
-    tiles = tile_columns(row, col, row >= 0, shift, n_cols, tile_cols, width, chans)
-    count = spread(*[mask for *_, mask in tiles])
-    inside = grid_columns(col, n_cols, tile_cols, width, chans)
-    share = 1.0 / jnp.maximum(count, 1.0)
-    keep = jnp.minimum(count, 1.0) * inside
+    tiles = tile_columns(row, col, row >= 0, shift, n_cols, tile_cols, chans)
+    inside = grid_columns(col, n_cols, tile_cols, chans)
     for i in range(4):
         y = i + half * (1 - date)
-        level = placed(pyr_b, lambda sy, y=y: y - 2 - sy, tiles, [None] * 3, width) * share
-        value = jnp.abs(pyr_a[y].astype(F32) - level)
-        line = first_half * half + y - 2
-        put(dif, i, -CW, width, value * (keep * in_grid(line, n_rows, tile_rows)))
+        keep_line = in_grid(first_half * half + y - 2, n_rows, tile_rows)
+        value = difference(
+            pyr_a[y], pyr_b, lambda sy, y=y: y - 2 - sy, [(tiles, None)], inside, keep_line, width
+        )
+        put(dif, i, -CW, width, value)
     for i in range(4):
         gather(dif, i, cat_d, i, width, -CW, width)
-    z = conv([(cat_d, 0, 1)], conv_weights(w_dec1))
+    z = conv([(cat_d, 0, 1)], w_dec1, 1)
     z = jnp.maximum(z + jnp.concatenate([b_dec1[...]] * 2, 1), 0.0)
     for i in range(2):
-        line = first_half * half + i + half * (1 - date) - 1
-        put(hid, i, -CW, width, line_of(z, i, width) * (inside * in_grid(line, n_rows, tile_rows)))
+        keep_line = in_grid(first_half * half + i + half * (1 - date) - 1, n_rows, tile_rows)
+        put(hid, i, -CW, width, on_grid(line_of(z, i, width), inside, keep_line))
 
 
 def outer_body(n_par, n_rows, n_cols, tile_rows, tile_cols, shift, v_ref, *refs):
@@ -233,53 +265,67 @@
     for i in range(HB):
         gather(lat, i + HA, cat_b, i + 3 * date, width, -CW, width)
     pairs_b = 2 + MO // 2
-    z = conv([(cat_a, 0, 2), (cat_b, 0, pairs_b)], conv_weights(w_fpn)).astype(BF16)
+    z = conv([(cat_a, 0, 2), (cat_b, 0, pairs_b)], w_fpn).astype(BF16)
     for i in range(4):
         pyr_a[i + half * date] = line_of(z, i, width)
     for i in range(2 * pairs_b):
         put(pyr_b, i + (half + MO) * date, -CW, width, line_of(z, 4 + i, width).astype(F32))
 
     near_row = jnp.clip(row + jnp.where(date == 0, -1, 1), 0, n_rows - 1)
-    tiles = tile_columns(row, col, row >= 0, shift, n_cols, tile_cols, width, chans)
-    near = tile_columns(near_row, col, has_row, shift, n_cols, tile_cols, width, chans)
-    inside = grid_columns(col, n_cols, tile_cols, width, chans)
+    tiles = tile_columns(row, col, row >= 0, shift, n_cols, tile_cols, chans)
+    near = tile_columns(near_row, col, has_row, shift, n_cols, tile_cols, chans)
+    inside = grid_columns(col, n_cols, tile_cols, chans)
     for i in range(half):
-        y = i + 4 * date
+        y = jnp.where(date == 0, i, half + 3 - i)
         q_of = lambda sy, y=y: y - 2 - sy
 
-        def is_own(sy):
+        def is_own(sy, q_of=q_of):
             return jnp.where(date == 0, q_of(sy) >= 0, q_of(sy) < half).astype(F32)
 
-        own_hits = [is_own(sy) for sy, *_ in tiles]
-        near_hits = [1.0 - is_own(sy) for sy, *_ in near]
-        total = placed(pyr_b, q_of, tiles, own_hits, width) + placed(pyr_b, q_of, near, near_hits, width)
-        count = spread(*[t[-1] * h for t, h in zip(tiles, own_hits)]) + spread(*[t[-1] * h for t, h in zip(near, near_hits)])
-        value = jnp.abs(pyr_a[y].astype(F32) - total / jnp.maximum(count, 1.0))
-        line = first_half * half + y - 2
-        keep = jnp.minimum(count, 1.0) * inside * in_grid(line, n_rows, tile_rows)
-        put(dif, i, -CW, width, value * keep)
+        def is_near(sy, is_own=is_own):
+            return 1.0 - is_own(sy)
+
+        groups = [(tiles, is_own), (near, is_near)] if i < 2 + MO else [(tiles, None)]
+        keep_line = in_grid(first_half * half + y - 2, n_rows, tile_rows)
+        value = difference(pyr_a[y], pyr_b, q_of, groups, inside, keep_line, width)
+        put(dif, y - 4 * date, -CW, width, value)
 
     for i in range(2):
         cat_d[i + half * (1 - date)] = t_d[i + 2 * date]
         put(hid, i + half * (1 - date), -CW, width, t_h[pl.ds(CW + i * width, width)])
     for i in range(half):
         gather(dif, i, cat_d, i + 2 * date, width, -CW, width)
-    z = conv([(cat_d, 0, half // 2)], conv_weights(w_dec1))
+    z = conv([(cat_d, 0, half // 2)], w_dec1)
     z = jnp.maximum(z + jnp.concatenate([b_dec1[...]] * 2, 1), 0.0)
     for i in range(half):
         y = i + 2 * date
         line = first_half * half + y - 1
-        put(hid, y, -CW, width, line_of(z, i, width) * (inside * in_grid(line, n_rows, tile_rows)))
+        put(hid, y, -CW, width, on_grid(line_of(z, i, width), inside, in_grid(line, n_rows, tile_rows)))
     for i in range(half + 2):
         gather(hid, i, cat_h, i, tile_cols, 0, width)
-    z = conv([(cat_h, 0, half // 2)], conv_weights(w_dec2))
+    z = conv([(cat_h, 0, half // 2)], w_dec2)
     z = jnp.maximum(z + jnp.concatenate([b_dec2[...]] * 2, 1), 0.0).astype(BF16)
-    weight = jnp.broadcast_to(w_out[...], (16, chans))
-    for i in range(half):
-        logit = lax.dot_general(
-            weight, line_of(z, i, tile_cols), (((1,), (1,)), ((), ())), preferred_element_type=F32
-        )
-        out_ref[i : i + 1] = logit[:1] + b_out[0]
+    none = jnp.zeros((1, chans), BF16)
+    upper = jnp.concatenate([w_out[...], none], axis=1)
+    lower = jnp.concatenate([none, w_out[...]], axis=1)
+    weight = jnp.concatenate([upper, lower] * 8, axis=0)
+    logit = lax.dot_general(weight, z, (((1,), (1,)), ((), ())), preferred_element_type=F32)
+    for i in range(half // 2):
+        out_ref[2 * i : 2 * i + 2] = logit[:2, i * tile_cols : (i + 1) * tile_cols] + b_out[...]
+
+
+def fetch_body(n_par, tile_rows, tile_cols, x_hbm, rows, *refs):
+    edges, sems = refs[:n_par], refs[n_par]
+    _, col, date = position()
+    parts = [(x_hbm.at[pl.ds((tile_rows - HB) * date, HB)], rows)]
+    for p in range(n_par):
+        column = pl.multiple_of(jnp.where(col % 2 == p, tile_cols - CW, 0), 8)
+        parts.append((x_hbm.at[:, pl.ds(column, CW)], edges[p]))
+    copies = [pltpu.make_async_copy(a, b, sems.at[k]) for k, (a, b) in enumerate(parts)]
+    for copy in copies[::-1]:
+        copy.start()
+    for copy in copies:
+        copy.wait()
 
 
 def per_device(
@@ -291,6 +337,18 @@
     half, width = tile_rows // 2, tile_cols + 2 * CW
     n_par = 1 if n_cols == 2 else 2
     own = features[0]
+    tile = pltpu.with_memory_space_constraint(own, pltpu.HBM)
+    vmem = pl.BlockSpec(memory_space=pltpu.VMEM)
+    kind = lambda *shape: jax.ShapeDtypeStruct(shape + (chans,), BF16)
+    rows_own, *edges = pl.pallas_call(
+        functools.partial(fetch_body, n_par, tile_rows, tile_cols),
+        out_shape=(kind(HB, tile_cols),) + (kind(tile_rows, CW),) * n_par,
+        in_specs=[pl.BlockSpec(memory_space=pltpu.HBM)],
+        out_specs=(vmem,) * (1 + n_par),
+        scratch_shapes=[pltpu.SemaphoreType.DMA((1 + n_par,))],
+        compiler_params=pltpu.CompilerParams(vmem_limit_bytes=4 * 2**20),
+        name="fetch",
+    )(tile)
     first = date == 0
 
     def swap(value):
@@ -314,9 +372,7 @@
 
     mine, corners, others = [], [], []
     for p in range(n_par):
-        mine.append(send(edge(own, p), sizes, lambda r, c, d, p=p: (r, partner(c, p), d)))
-    rows_own = lax.dynamic_slice_in_dim(own, (tile_rows - HB) * date, HB, 0)
-    rows_own = lax.optimization_barrier(rows_own)
+        mine.append(send(edges[p], sizes, lambda r, c, d, p=p: (r, partner(c, p), d)))
     rows_oth = lax.dynamic_slice_in_dim(oth, (tile_rows - HB) * date, HB, 0)
     for_row = jnp.concatenate(
         [
@@ -327,11 +383,9 @@
     )
     from_row = send(for_row, sizes, shift_row)
     for p in range(n_par):
+        others.append(swap(mine[p]))
+    for p in range(n_par):
         corners.append(send(edge(for_row, p), sizes, functools.partial(corner, p)))
-    for p in range(n_par):
-        others.append(swap(mine[p]))
-
-    vmem = pl.BlockSpec(memory_space=pltpu.VMEM)
     smem = pl.BlockSpec(memory_space=pltpu.SMEM)
     lines_a, lines_b = half + 4, half + 4 + 2 * MO
 
@@ -339,7 +393,7 @@
         return jax.ShapeDtypeStruct((2 * CW + lines * width, chans), kind)
 
     def cat(lines, columns=width):
-        return jax.ShapeDtypeStruct((lines, columns, 3 * chans), BF16)
+        return jax.ShapeDtypeStruct((lines, 3, columns, chans), BF16)
 
     def scratch(shape):
         return pltpu.VMEM(shape.shape, shape.dtype)
@@ -361,7 +415,7 @@
     out, _, _ = pl.pallas_call(
         functools.partial(outer_body, n_par, n_rows, n_cols, tile_rows, tile_cols),
         out_shape=(jax.ShapeDtypeStruct((half, tile_cols), F32), row_a, flat(lines_b)),
-        in_specs=[smem] + [vmem] * (n_par + 1 + 14) + [smem],
+        in_specs=[smem] + [vmem] * (n_par + 1 + 15),
         out_specs=(vmem,) * 3,
         input_output_aliases={n_par + 2: 1, n_par + 3: 2},
         scratch_shapes=[
@@ -377,7 +431,7 @@
         name="outer",
     )(
         scene_shift, from_row, *corners, pyr_a, pyr_b, *kept,
-        w_lat, b_lat[None], w_fpn, w_dec1, b_dec1[None], w_dec2, b_dec2[None], w_out[None], b_out,
+        w_lat, b_lat[None], w_fpn, w_dec1, b_dec1[None], w_dec2, b_dec2[None], w_out[None], jnp.broadcast_to(b_out, (1, tile_cols)),
     )
     return out
 

time: 20.7 us -> 18.6 us (0.90)
  local copies, waits for them, and re-layouts: 1.19 us -> 0.15 us
  Pallas kernels: 9.52 us -> 8.58 us
    pallas_call x1, Pallas kernels: 5.81 us -> 4.27 us  [per_device(): pl.pallas_call(functools.partial(outer_body, n_par, n_rows, n_cols, tile_...]
    pallas_call x0 -> x1, Pallas kernels: none -> 1.08 us  [per_device(): pl.pallas_call(functools.partial(fetch_body, n_par, tile_rows, tile_cols)...]
    dynamic_slice x1 -> x0, local copies, waits for them, and re-layouts: 1.05 us -> none  [per_device(): rows_own = lax.dynamic_slice_in_dim(own, (tile_rows - HB) * date, HB, 0)]
    pallas_call x1, Pallas kernels: 3.71 us -> 3.24 us  [per_device(): pl.pallas_call(functools.partial(inner_body, n_par, n_rows, n_cols, tile_...]
  transfers between devices with their start and end apart: 5 -> 5, of which waited for: 2 -> 2; matrix products, arithmetic and copies ran while one was open for 6% -> 1% of each run, Pallas kernels for 18% -> 23%
where the time goes in v3:
time: 18.6 us; the launch traced here: 18.5 us
  Pallas kernels  8.58 us (46%)
  starting transfers between devices  6.7 us (36%)
  waiting for transfers between devices  2.11 us (11%)
  between operations  0.86 us (5%)
    ppermute x5, starting transfers between devices, send(): return lax.ppermute(value, ('groups', 'rows', 'cols', 'date'), pairs)  6.7 us
    pallas_call x1, Pallas kernels, per_device(): pl.pallas_call(functools.partial(outer_body, n_par, n_rows, n_cols, tile_...  4.27 us
    pallas_call x1, Pallas kernels, per_device(): pl.pallas_call(functools.partial(inner_body, n_par, n_rows, n_cols, tile_...  3.24 us
    ppermute x5, waiting for transfers between devices, send(): return lax.ppermute(value, ('groups', 'rows', 'cols', 'date'), pairs)  2.11 us
    pallas_call x1, Pallas kernels, per_device(): pl.pallas_call(functools.partial(fetch_body, n_par, tile_rows, tile_cols)...  1.08 us
  transfers between devices with their start and end apart: 5, of which 2 were waited for; matrix products, arithmetic and copies ran while one was open for 1% of the time, Pallas kernels for 23%

profile of v3, /device:TPU:1, one launch (start us, length us, event | category | flops | bytes accessed | tf_op | source)
XLA Modules:
  0.0 18.5 jit_solution(2502876947731098255)
XLA Ops:
  0.0 0.0 copy-start.1
  0.0 0.0 copy-start.4
  0.0 0.0 copy-start.6
  0.0 0.0 copy-start.5
  0.0 0.1 collective-permute-start
  0.1 1.1 %fetch.1 = (bf16[7,128,128]{2,1,0:T(8,128)(2,1)S(1)}, bf16[16,8,128]{2,1,0:T(8,128)(2,1)S(1)}) custom-call(bf16[16,128,128]{2,1,0:T(8,128)(2,1)} %bitcast.8), custom_call_target="tpu_custom_call" | custom-call | tf_op jit(solution)/shard_map/fetch/pallas_call | solution.py:343
  1.2 1.0 %collective-permute-done.oth = bf16[16,128,128]{2,1,0:T(8,128)(2,1)S(1)} collective-permute-done((bf16[16,128,128]{2,1,0:T(8,128)(2,1)}, bf16[16,128,128]{2,1,0:T(8,128)(2,1)S(1)}, u32[]{:S(2)}, u32[]{:S(2)}) %collective-permute-start) | collective-permute-done | bytes 524320 | tf_op jit(solution)/shard_map/ppermute | solution.py:43
  2.3 2.7 %collective-permute-start.1 = (bf16[10,128,128]{2,1,0:T(8,128)(2,1)S(1)}, bf16[10,128,128]{2,1,0:T(8,128)(2,1)S(1)}, u32[]{:S(2)}, u32[]{:S(2)}) collective-permute-start(bf16[10,128,128]{2,1,0:T(8,128)(2,1)S(1)} %pad_maximum_fusion), channel_id=1, source_target_pairs={{0,16},{1,4},{2,18},{3,6},{4,1},{5,8},{6,3},{7,10},{8,5},{9,12},{1... | collective-permute-start | bytes 983048 | tf_op jit(solution)/shard_map/ppermute | solution.py:43
  5.1 1.2 %collective-permute-start.3 = (bf16[16,8,128]{2,1,0:T(8,128)(2,1)S(1)}, bf16[16,8,128]{2,1,0:T(8,128)(2,1)S(1)}, u32[]{:S(2)}, u32[]{:S(2)}) collective-permute-start(bf16[16,8,128]{2,1,0:T(8,128)(2,1)S(1)} %get-tuple-element.15), channel_id=1, source_target_pairs={{0,2},{1,3},{2,0},{3,1},{4,6},{5,7},{6,4},{7,5},{8,10},{9,11},{10,... | collective-permute-start | bytes 98312 | tf_op jit(solution)/shard_map/ppermute | solution.py:43
  6.9 0.0 copy-done.9
  6.9 0.1 copy.15.shift
  7.0 1.1 %collective-permute-done.3.refs_0_ = bf16[16,8,128]{2,1,0:T(8,128)(2,1)S(1)} collective-permute-done((bf16[16,8,128]{2,1,0:T(8,128)(2,1)S(1)}, bf16[16,8,128]{2,1,0:T(8,128)(2,1)S(1)}, u32[]{:S(2)}, u32[]{:S(2)}) %collective-permute-start.3) | collective-permute-done | bytes 32800 | tf_op jit(solution)/shard_map/ppermute | solution.py:43
  8.1 1.2 %collective-permute-start.4 = (bf16[16,8,128]{2,1,0:T(8,128)(2,1)S(1)}, bf16[16,8,128]{2,1,0:T(8,128)(2,1)S(1)}, u32[]{:S(2)}, u32[]{:S(2)}) collective-permute-start(bf16[16,8,128]{2,1,0:T(8,128)(2,1)S(1)} %collective-permute-done.3.refs_0_), channel_id=1, source_target_pairs={{0,1},{1,0},{2,3},{3,2},{4,5},{5,4},{6,7},{7,6},{8,9},{9,8},{10,11... | collective-permute-start | bytes 98312 | tf_op jit(solution)/shard_map/ppermute | solution.py:43
  9.3 1.5 %collective-permute-start.2 = (bf16[10,8,128]{2,1,0:T(8,128)(2,1)S(1)}, bf16[10,8,128]{2,1,0:T(8,128)(2,1)S(1)}, u32[]{:S(2)}, u32[]{:S(2)}) collective-permute-start(bf16[10,8,128]{2,1,0:T(8,128)(2,1)S(1)} %fusion.2), channel_id=1, source_target_pairs={{0,16},{1,6},{2,18},{3,4},{4,3},{5,10},{6,1},{7,8},{8,7},{9,14},{1... | collective-permute-start | bytes 61448 | tf_op jit(solution)/shard_map/ppermute | solution.py:43
  10.8 0.0 collective-permute-done.4.refs_1_
  10.8 0.0 copy-done
  10.8 0.0 copy-done.2
  10.9 0.0 copy-start.3
  10.9 0.0 copy-start.7
  10.9 0.0 copy-start.8
  10.9 3.2 %inner.1 = (bf16[12,144,128]{2,1,0:T(8,128)(2,1)S(1)}, f32[2896,128]{1,0:T(8,128)S(1)}, bf16[12,3,144,128]{3,2,1,0:T(8,128)(2,1)S(1)}, bf16[16,3,144,128]{3,2,1,...) custom-call(s32[4,2,2]{2,1,0:T(2,128)S(1)} %copy.15.shift, ...), custom_call_target="tpu_custom_call" | custom-call | flops 1132462080 | bytes 8388608 | tf_op jit(solution)/shard_map/inner/pallas_call | solution.py:403
  14.2 0.0 collective-permute-done.2.refs_0_
  14.2 0.0 collective-permute-done.1.v_ref
  14.2 4.3 %outer.1 = (f32[8,128]{1,0:T(8,128)}, bf16[12,144,128]{2,1,0:T(8,128)(2,1)S(1)}, f32[2896,128]{1,0:T(8,128)S(1)}) custom-call(s32[4,2,2]{2,1,0:T(2,128)S(1)} %copy.15.shift, bf16[10,128,128]{2,1,0:T(8,128)(2,1)S(1)} %collective-permute-done.1.v_ref, ...), custom_call_target="tpu_custom_call", output_to_operand_aliasing={{1}: (3, {}), {2}: (4, {})} | custom-call | tf_op jit(solution)/shard_map/outer/pallas_call | solution.py:415
  (15 shorter events, 0.1 us)
Async XLA Ops:
  0.0 10.8 %copy-start = (bf16[1,16,128,128]{3,2,1,0:T(8,128)(2,1)S(1)}, bf16[1,16,128,128]{3,2,1,0:T(8,128)(2,1)}, u32[]{:S(2)}) copy-start(bf16[1,16,128,128]{3,2,1,0:T(8,128)(2,1)} %param.11) | copy-start | bytes 1572868
  0.0 6.9 %copy-start.9 = (s32[4,2,2]{0,2,1:T(2,128)S(1)}, s32[4,2,2]{0,2,1:T(2,128)}, u32[]{:S(2)}) copy-start(s32[4,2,2]{0,2,1:T(2,128)} %param.12) | copy-start | bytes 196
  0.0 10.8 %copy-start.2 = (bf16[3,3,128,128]{3,2,1,0:T(8,128)(2,1)S(1)}, bf16[3,3,128,128]{3,2,1,0:T(8,128)(2,1)}, u32[]{:S(2)}) copy-start(bf16[3,3,128,128]{3,2,1,0:T(8,128)(2,1)} %refs_10_.1) | copy-start | bytes 884740
  0.0 10.8 %copy-start.1 = (bf16[3,3,128,128]{3,2,1,0:T(8,128)(2,1)S(1)}, bf16[3,3,128,128]{3,2,1,0:T(8,128)(2,1)}, u32[]{:S(2)}) copy-start(bf16[3,3,128,128]{3,2,1,0:T(8,128)(2,1)} %refs_9_.1) | copy-start | bytes 884740
  0.0 10.8 %copy-start.4 = (bf16[128,128]{1,0:T(8,128)(2,1)S(1)}, bf16[128,128]{1,0:T(8,128)(2,1)}, u32[]{:S(2)}) copy-start(bf16[128,128]{1,0:T(8,128)(2,1)} %refs_7_.1) | copy-start | bytes 98308
  0.0 10.8 %copy-start.6 = (f32[128]{0:T(128)S(1)}, f32[128]{0:T(128)}, u32[]{:S(2)}) copy-start(f32[128]{0:T(128)} %param.17) | copy-start | bytes 1540
  0.0 10.8 %copy-start.5 = (f32[128]{0:T(128)S(1)}, f32[128]{0:T(128)}, u32[]{:S(2)}) copy-start(f32[128]{0:T(128)} %param.14) | copy-start | bytes 1540
  0.0 2.2 %collective-permute-start = (bf16[16,128,128]{2,1,0:T(8,128)(2,1)}, bf16[16,128,128]{2,1,0:T(8,128)(2,1)S(1)}, u32[]{:S(2)}, u32[]{:S(2)}) collective-permute-start(bf16[16,128,128]{2,1,0:T(8,128)(2,1)} %bitcast.7), channel_id=1, source_target_pairs={{0,1},{1,0},{2,3},{3,2},{4,5},{5,4},{6,7},{7,6},{8,9},{9,8},{10,11... | collective-permute-start | bytes 1572872 | tf_op jit(solution)/shard_map/ppermute | solution.py:43
  2.3 11.8 %collective-permute-start.1 = (bf16[10,128,128]{2,1,0:T(8,128)(2,1)S(1)}, bf16[10,128,128]{2,1,0:T(8,128)(2,1)S(1)}, u32[]{:S(2)}, u32[]{:S(2)}) collective-permute-start(bf16[10,128,128]{2,1,0:T(8,128)(2,1)S(1)} %pad_maximum_fusion), channel_id=1, source_target_pairs={{0,16},{1,4},{2,18},{3,6},{4,1},{5,8},{6,3},{7,10},{8,5},{9,12},{1... | collective-permute-start | bytes 983048 | tf_op jit(solution)/shard_map/ppermute | solution.py:43
  5.1 3.1 %collective-permute-start.3 = (bf16[16,8,128]{2,1,0:T(8,128)(2,1)S(1)}, bf16[16,8,128]{2,1,0:T(8,128)(2,1)S(1)}, u32[]{:S(2)}, u32[]{:S(2)}) collective-permute-start(bf16[16,8,128]{2,1,0:T(8,128)(2,1)S(1)} %get-tuple-element.15), channel_id=1, source_target_pairs={{0,2},{1,3},{2,0},{3,1},{4,6},{5,7},{6,4},{7,5},{8,10},{9,11},{10,... | collective-permute-start | bytes 98312 | tf_op jit(solution)/shard_map/ppermute | solution.py:43
  8.1 2.7 %collective-permute-start.4 = (bf16[16,8,128]{2,1,0:T(8,128)(2,1)S(1)}, bf16[16,8,128]{2,1,0:T(8,128)(2,1)S(1)}, u32[]{:S(2)}, u32[]{:S(2)}) collective-permute-start(bf16[16,8,128]{2,1,0:T(8,128)(2,1)S(1)} %collective-permute-done.3.refs_0_), channel_id=1, source_target_pairs={{0,1},{1,0},{2,3},{3,2},{4,5},{5,4},{6,7},{7,6},{8,9},{9,8},{10,11... | collective-permute-start | bytes 98312 | tf_op jit(solution)/shard_map/ppermute | solution.py:43
  9.3 4.8 %collective-permute-start.2 = (bf16[10,8,128]{2,1,0:T(8,128)(2,1)S(1)}, bf16[10,8,128]{2,1,0:T(8,128)(2,1)S(1)}, u32[]{:S(2)}, u32[]{:S(2)}) collective-permute-start(bf16[10,8,128]{2,1,0:T(8,128)(2,1)S(1)} %fusion.2), channel_id=1, source_target_pairs={{0,16},{1,6},{2,18},{3,4},{4,3},{5,10},{6,1},{7,8},{8,7},{9,14},{1... | collective-permute-start | bytes 61448 | tf_op jit(solution)/shard_map/ppermute | solution.py:43
  10.9 3.3 %copy-start.3 = (bf16[3,3,128,128]{3,2,1,0:T(8,128)(2,1)S(1)}, bf16[3,3,128,128]{3,2,1,0:T(8,128)(2,1)}, u32[]{:S(2)}) copy-start(bf16[3,3,128,128]{3,2,1,0:T(8,128)(2,1)} %refs_12_.1) | copy-start | bytes 884740
  10.9 3.3 %copy-start.7 = (f32[128]{0:T(128)S(1)}, f32[128]{0:T(128)}, u32[]{:S(2)}) copy-start(f32[128]{0:T(128)} %param.19) | copy-start | bytes 1540
  10.9 3.3 %copy-start.8 = (bf16[128]{0:T(256)(128)(2,1)S(1)}, bf16[128]{0:T(256)(128)(2,1)}, u32[]{:S(2)}) copy-start(bf16[128]{0:T(256)(128)(2,1)} %param.20) | copy-start | bytes 772

commit v4 on v3

v4 whole, which is shorter than its diff:
```python
import functools

import jax
import jax.numpy as jnp
from jax import lax
from jax.experimental import pallas as pl
from jax.experimental.pallas import tpu as pltpu
from jax.sharding import PartitionSpec as P


MO = 4
HA = 3
HB = HA + MO
CW = 8
STRIP = 16
F32 = jnp.float32
BF16 = jnp.bfloat16


def column_partner(col, parity, n_cols):
    right = col % 2 == parity
    return (col + 1) % n_cols if right else (col - 1) % n_cols


def send(value, sizes, target):
    n_groups, n_rows, n_cols, n_dates = sizes

    def place(group, row, col, date):
        return ((group * n_rows + row) * n_cols + col) * n_dates + date

    pairs = []
    for group in range(n_groups):
        for row in range(n_rows):
            for col in range(n_cols):
                for date in range(n_dates):
                    to = target(row, col, date)
                    end = (
                        place((group + 1) % n_groups, row, col, date)
                        if to is None
                        else place(group, *to)
                    )
                    pairs.append((place(group, row, col, date), end))
    return lax.ppermute(value, ("groups", "rows", "cols", "date"), pairs)


def at(line, column, width):
    return CW + line * width + CW + column


def position():
    return lax.axis_index("rows"), lax.axis_index("cols"), lax.axis_index("date")


def put(target, line, column, width, value):
    start = at(line, column, width)
    target[start : start + value.shape[0]] = value


def gather(source, line, cat, index, count, column, width):
    start = at(line, column, width)
    for tap in range(3):
        cat[index, tap] = source[start + tap - 1 : start + tap - 1 + count].astype(BF16)


def conv(parts, w_ref, date, ways=2):
    taps = [w_ref[a + (2 - 2 * a) * date].reshape(-1, w_ref.shape[-1]) for a in range(3)]
    none = jnp.zeros_like(taps[0])
    tall = jnp.concatenate(
        [jnp.concatenate(taps + [none], axis=0), jnp.concatenate([none] + taps, axis=0)], axis=1
    )
    tops = [(cat, first + 2 * i) for cat, first, pairs in parts for i in range(pairs)]
    outs = []
    for way in range(ways):
        some = tops[way * len(tops) // ways : (way + 1) * len(tops) // ways]
        lines = [
            jnp.concatenate([cat[top + j, tap] for cat, top in some], axis=0)
            for j in range(4)
            for tap in range(3)
        ]
        outs.append(jnp.dot(jnp.concatenate(lines, axis=1), tall, preferred_element_type=F32))
    return jnp.concatenate(outs, axis=0)


def line_of(z, index, columns):
    chans = z.shape[1] // 2
    pair, k = divmod(index, 2)
    return z[pair * columns : (pair + 1) * columns, k * chans : (k + 1) * chans]


def put_sides(lat, line, col, n_cols, tile_cols, width, halves):
    even = col % 2 == 0
    right = halves[0] * (even & (col < n_cols - 1)).astype(F32)
    left = halves[0] * (~even).astype(F32)
    if len(halves) == 2:
        right = right + halves[1] * (~even & (col < n_cols - 1)).astype(F32)
        left = left + halves[1] * (even & (col > 0)).astype(F32)
    put(lat, line, -CW, width, left)
    put(lat, line, tile_cols, width, right)


def tile_columns(row, col, there, shift, date, n_cols, tile_cols, chans):
    cells = lax.broadcasted_iota(jnp.int32, (STRIP, chans), 0)
    tiles = []
    for step in (0, -1, 1):
        c = jnp.clip(col + step, 0, n_cols - 1)
        is_tile = (there & (col + step >= 0) & (col + step < n_cols)).astype(F32)
        sy, sx = shift[row, c, 0] * (1 - 2 * date), shift[row, c, 1]
        low = sx + step * tile_cols
        masks = []
        for left in (True, False):
            x = cells + (-CW if left else tile_cols + CW - STRIP)
            masks.append(((x >= low) & (x < low + tile_cols)).astype(F32) * is_tile)
        tiles.append((sy, sx, is_tile, masks[0], masks[1]))
    return tiles


def shares(count):
    share = jnp.where(count > 1.5, 0.5, 1.0)
    share = jnp.where(count > 2.5, 1.0 / 3.0, share)
    return jnp.where(count > 3.5, 0.25, share)


def difference(a_line, pyr_b, u, groups, inside, keep_line, width):
    plus = lambda x, y: y if x is None else x + y
    count = [None, None]
    level = [None, None]
    mids = []
    for tiles, hit_of in groups:
        for k, (sy, sx, is_tile, *masks) in enumerate(tiles):
            start = CW + (u - sy + 2 + MO) * width - sx
            hit = None if hit_of is None else hit_of(sy)
            for side in range(2):
                if k != 2 - side:
                    mask = masks[side] if hit is None else masks[side] * hit
                    count[side] = plus(count[side], mask)
                    strip = pyr_b[pl.ds(start + side * (width - STRIP), STRIP)] * mask
                    level[side] = plus(level[side], strip)
            if k == 0:
                value = pyr_b[pl.ds(start + STRIP, width - 2 * STRIP)]
                mids.append((value, None if hit is None else hit * is_tile))
    a = a_line.astype(F32)
    outs = []
    for side in range(2):
        part = a[:STRIP] if side == 0 else a[width - STRIP :]
        value = jnp.abs(part - level[side] * shares(count[side]))
        keep = jnp.minimum(count[side], 1.0) * inside[side]
        outs.append(value * (keep if keep_line is None else keep * keep_line))
    middle = a[STRIP : width - STRIP]
    if len(mids) == 1:
        middle = jnp.abs(middle - mids[0][0])
    else:
        weight = mids[0][1] + mids[1][1]
        share = jnp.where(weight > 1.5, 0.5, 1.0)
        keep = jnp.minimum(weight, 1.0)
        keep = keep if keep_line is None else keep * keep_line
        total = mids[0][0] * (mids[0][1] * share) + mids[1][0] * (mids[1][1] * share)
        middle = jnp.abs(middle - total) * keep
    return jnp.concatenate([outs[0], middle, outs[1]], axis=0)


def grid_columns(col, n_cols, tile_cols, chans):
    x = lax.broadcasted_iota(jnp.int32, (STRIP, chans), 0) + col * tile_cols
    return [
        ((x + at >= 0) & (x + at < n_cols * tile_cols)).astype(F32)
        for at in (-CW, tile_cols + CW - STRIP)
    ]


def on_grid(line, inside, keep_line):
    parts = [line[:STRIP] * inside[0], line[STRIP:-STRIP], line[-STRIP:] * inside[1]]
    if keep_line is not None:
        parts = [part * keep_line for part in parts]
    return jnp.concatenate(parts, axis=0)


def inner_body(n_par, n_cols, tile_rows, tile_cols, shift, own, oth, *refs):
    mine, others = refs[:n_par], refs[n_par : 2 * n_par]
    (w_lat, b_lat, w_fpn, w_dec1, b_dec1,
     pyr_a, pyr_b, t_a, t_b, t_d, hid, lat_a, lat_b, cat_a, cat_b, cat_d, dif) = refs[2 * n_par :]
    row, col, date = position()
    half, width, chans = tile_rows // 2, tile_cols + 2 * CW, own.shape[-1]
    weight, bias = w_lat[...], b_lat[...]

    def lateral(x):
        return jnp.dot(x, weight, preferred_element_type=F32) + bias

    for lat, cat, lines, is_own in (
        (lat_a, cat_a, half + HA, date == 0),
        (lat_b, cat_b, half + HB, date == 1),
    ):
        rows = [u + (tile_rows - 1 - 2 * u) * date for u in range(lines)]

        def pick(x, y, is_own=is_own):
            return jnp.where(is_own, x, y)

        z = lateral(jnp.concatenate([pick(own[t], oth[t]) for t in rows], axis=0))
        for u in range(lines):
            put(lat, u, 0, width, z[u * tile_cols : (u + 1) * tile_cols])
        z = [
            lateral(jnp.concatenate([pick(mine[p][t], others[p][t]) for t in rows], axis=0))
            for p in range(n_par)
        ]
        for u in range(lines):
            put_sides(lat, u, col, n_cols, tile_cols, width, [x[u * CW : (u + 1) * CW] for x in z])
        for u in range(lines):
            gather(lat, u, cat, u, width, -CW, width)
    for u in range(3):
        t_a[u] = cat_a[u]
        t_b[u] = cat_b[u]
    pairs_a, pairs_b = half // 2, half // 2 + MO // 2
    z = conv([(cat_a, 1, pairs_a), (cat_b, 1, pairs_b)], w_fpn, date).astype(BF16)
    for i in range(2 * pairs_a):
        pyr_a[i] = line_of(z, i, width)
    pyr_b[:CW] = jnp.zeros((CW, chans), F32)
    pyr_b[pyr_b.shape[0] - CW :] = jnp.zeros((CW, chans), F32)
    for i in range(2 * pairs_b):
        put(pyr_b, i + 4 + MO, -CW, width, line_of(z, 2 * pairs_a + i, width).astype(F32))

    tiles = tile_columns(row, col, row >= 0, shift, date, n_cols, tile_cols, chans)
    inside = grid_columns(col, n_cols, tile_cols, chans)
    for i in range(4):
        u = i + half - 2
        value = difference(pyr_a[u - 2], pyr_b, u, [(tiles, None)], inside, None, width)
        put(dif, i, -CW, width, value)
    for i in range(4):
        gather(dif, i, cat_d, i, width, -CW, width)
    for i in range(2):
        t_d[i] = cat_d[i]
    z = conv([(cat_d, 0, 1)], w_dec1, date, 1)
    z = jnp.maximum(z + jnp.concatenate([b_dec1[...]] * 2, 1), 0.0)
    for i in range(2):
        put(hid, i, -CW, width, on_grid(line_of(z, i, width), inside, None))


def outer_body(n_par, n_rows, n_cols, tile_rows, tile_cols, shift, v_ref, *refs):
    corners = refs[:n_par]
    (in_a, _, t_a, t_b, t_d, t_h, w_lat, b_lat, w_fpn, w_dec1, b_dec1, w_dec2, b_dec2, w_out, b_out,
     out_ref, pyr_b, pyr_a, lat, cat_a, cat_b, dif, cat_d, hid, cat_h) = refs[n_par:]
    row, col, date = position()
    half, width, chans = tile_rows // 2, tile_cols + 2 * CW, w_lat.shape[-1]
    has_row = jnp.where(date == 0, row > 0, row < n_rows - 1)
    row_keep = has_row.astype(F32)
    weight, bias = w_lat[...], b_lat[...]

    def lateral(x):
        return (jnp.dot(x, weight, preferred_element_type=F32) + bias) * row_keep

    lines = [i + (HA - 1 - 2 * i) * date for i in range(HA)]
    lines += [HA + i + (HB - 1 - 2 * i) * date for i in range(HB)]
    z = lateral(jnp.concatenate([v_ref[i] for i in lines], axis=0))
    for i in range(HA + HB):
        put(lat, i, 0, width, z[i * tile_cols : (i + 1) * tile_cols])
    z = [lateral(jnp.concatenate([corners[p][i] for i in lines], axis=0)) for p in range(n_par)]
    for i in range(HA + HB):
        put_sides(lat, i, col, n_cols, tile_cols, width, [x[i * CW : (i + 1) * CW] for x in z])
    for i in range(HA):
        gather(lat, i, cat_a, i, width, -CW, width)
    for i in range(HB):
        gather(lat, i + HA, cat_b, i, width, -CW, width)
    for i in range(3):
        cat_a[i + HA] = t_a[i]
        cat_b[i + HB] = t_b[i]
    pairs_b = 2 + MO // 2
    z = conv([(cat_a, 0, 2), (cat_b, 0, pairs_b)], w_fpn, date).astype(BF16)
    for i in range(4):
        pyr_a[i] = line_of(z, i, width)
    for i in range(2 * pairs_b):
        put(pyr_b, i, -CW, width, line_of(z, 4 + i, width).astype(F32))

    near_row = jnp.clip(row + jnp.where(date == 0, -1, 1), 0, n_rows - 1)
    tiles = tile_columns(row, col, row >= 0, shift, date, n_cols, tile_cols, chans)
    near = tile_columns(near_row, col, has_row, shift, date, n_cols, tile_cols, chans)
    inside = grid_columns(col, n_cols, tile_cols, chans)
    for i in range(half):
        u = i - 2
        groups = [(tiles, None)]
        if u < MO:
            groups = [
                (tiles, lambda sy, u=u: (u - sy >= 0).astype(F32)),
                (near, lambda sy, u=u: (u - sy < 0).astype(F32)),
            ]
        a_line = pyr_a[u + 2] if u < 2 else in_a[u - 2]
        value = difference(a_line, pyr_b, u, groups, inside, row_keep if u < 0 else None, width)
        put(dif, i, -CW, width, value)
    for i in range(half):
        gather(dif, i, cat_d, i, width, -CW, width)
    for i in range(2):
        cat_d[i + half] = t_d[i]
        put(hid, i + half, -CW, width, t_h[CW + i * width : CW + (i + 1) * width])
    z = conv([(cat_d, 0, half // 2)], w_dec1, date)
    z = jnp.maximum(z + jnp.concatenate([b_dec1[...]] * 2, 1), 0.0)
    for i in range(half):
        put(hid, i, -CW, width, on_grid(line_of(z, i, width), inside, None if i else row_keep))
    for i in range(half + 2):
        gather(hid, i, cat_h, i, tile_cols, 0, width)
    z = conv([(cat_h, 0, half // 2)], w_dec2, date)
    z = jnp.maximum(z + jnp.concatenate([b_dec2[...]] * 2, 1), 0.0).astype(BF16)
    none = jnp.zeros((1, chans), BF16)
    upper = jnp.concatenate([w_out[...], none], axis=1)
    lower = jnp.concatenate([none, w_out[...]], axis=1)
    weight = jnp.concatenate([upper, lower] * 8, axis=0)
    logit = lax.dot_general(weight, z, (((1,), (1,)), ((), ())), preferred_element_type=F32)
    for i in range(half):
        pair, k = divmod(i, 2)
        line = logit[k : k + 1, pair * tile_cols : (pair + 1) * tile_cols] + b_out[...]
        out_ref[pl.ds(i + (half - 1 - 2 * i) * date, 1)] = line


def fetch_body(n_par, tile_rows, tile_cols, x_hbm, rows, *refs):
    edges, sems = refs[:n_par], refs[n_par]
    _, col, date = position()
    parts = [(x_hbm.at[pl.ds((tile_rows - HB) * date, HB)], rows)]
    for p in range(n_par):
        column = pl.multiple_of(jnp.where(col % 2 == p, tile_cols - CW, 0), 8)
        parts.append((x_hbm.at[:, pl.ds(column, CW)], edges[p]))
    copies = [pltpu.make_async_copy(a, b, sems.at[k]) for k, (a, b) in enumerate(parts)]
    for copy in copies[::-1]:
        copy.start()
    for copy in copies:
        copy.wait()


def per_device(
    sizes, features, scene_shift, w_lat, b_lat, w_fpn, w_dec1, b_dec1, w_dec2, b_dec2, w_out, b_out
):
    _, n_rows, n_cols, _ = sizes
    tile_rows, tile_cols, chans = features.shape[1:]
    col, date = lax.axis_index("cols"), lax.axis_index("date")
    half, width = tile_rows // 2, tile_cols + 2 * CW
    n_par = 1 if n_cols == 2 else 2
    own = features[0]
    tile = pltpu.with_memory_space_constraint(own, pltpu.HBM)
    vmem = pl.BlockSpec(memory_space=pltpu.VMEM)
    kind = lambda *shape: jax.ShapeDtypeStruct(shape + (chans,), BF16)
    rows_own, *edges = pl.pallas_call(
        functools.partial(fetch_body, n_par, tile_rows, tile_cols),
        out_shape=(kind(HB, tile_cols),) + (kind(tile_rows, CW),) * n_par,
        in_specs=[pl.BlockSpec(memory_space=pltpu.HBM)],
        out_specs=(vmem,) * (1 + n_par),
        scratch_shapes=[pltpu.SemaphoreType.DMA((1 + n_par,))],
        compiler_params=pltpu.CompilerParams(vmem_limit_bytes=4 * 2**20),
        name="fetch",
    )(tile)
    first = date == 0

    def swap(value):
        return send(value, sizes, lambda r, c, d: (r, c, 1 - d))

    def edge(x, parity):
        return jnp.where(col % 2 == parity, x[:, tile_cols - CW :], x[:, :CW])

    def partner(c, parity):
        return column_partner(c, parity, n_cols)

    oth = swap(own)

    def shift_row(r, c, d):
        near = r - 1 + 2 * d
        return (near, c, 1 - d) if 0 <= near < n_rows else None

    def corner(p, r, c, d):
        near = shift_row(r, c, d)
        return None if near is None else (near[0], partner(c, p), near[2])

    mine, corners, others = [], [], []
    for p in range(n_par):
        mine.append(send(edges[p], sizes, lambda r, c, d, p=p: (r, partner(c, p), d)))
    rows_oth = lax.dynamic_slice_in_dim(oth, (tile_rows - HB) * date, HB, 0)
    for_row = jnp.concatenate(
        [
            jnp.where(first, rows_own[:HA], rows_oth[HB - HA :]),
            jnp.where(first, rows_oth, rows_own),
        ],
        axis=0,
    )
    from_row = send(for_row, sizes, shift_row)
    for p in range(n_par):
        others.append(swap(mine[p]))
    for p in range(n_par):
        corners.append(send(edge(for_row, p), sizes, functools.partial(corner, p)))
    smem = pl.BlockSpec(memory_space=pltpu.SMEM)
    lines_b = half + 4 + 2 * MO

    def flat(lines, kind=F32):
        return jax.ShapeDtypeStruct((2 * CW + lines * width, chans), kind)

    def cat(lines, columns=width):
        return jax.ShapeDtypeStruct((lines, 3, columns, chans), BF16)

    def scratch(shape):
        return pltpu.VMEM(shape.shape, shape.dtype)

    def lines_of(lines):
        return jax.ShapeDtypeStruct((lines, width, chans), BF16)

    pyr_a, pyr_b, *kept = pl.pallas_call(
        functools.partial(inner_body, n_par, n_cols, tile_rows, tile_cols),
        out_shape=(lines_of(half), flat(lines_b), cat(3), cat(3), cat(2), flat(2)),
        in_specs=[smem] + [vmem] * (2 + 2 * n_par + 5),
        out_specs=(vmem,) * 6,
        scratch_shapes=[
            scratch(flat(half + HA)),
            scratch(flat(half + HB)),
            scratch(cat(half + HA)),
            scratch(cat(half + HB)),
            scratch(cat(4)),
            scratch(flat(4)),
        ],
        compiler_params=pltpu.CompilerParams(vmem_limit_bytes=28 * 2**20),
        cost_estimate=pl.CostEstimate(
            flops=2 * 10 * width * 1536 * 256, bytes_accessed=8 * 2**20, transcendentals=0
        ),
        name="inner",
    )(scene_shift, own, oth, *mine, *others, w_lat, b_lat[None], w_fpn, w_dec1, b_dec1[None])
    out, _ = pl.pallas_call(
        functools.partial(outer_body, n_par, n_rows, n_cols, tile_rows, tile_cols),
        out_shape=(jax.ShapeDtypeStruct((half, tile_cols), F32), flat(lines_b)),
        in_specs=[smem] + [vmem] * (n_par + 1 + 15),
        out_specs=(vmem,) * 2,
        input_output_aliases={n_par + 3: 1},
        scratch_shapes=[
            scratch(lines_of(4)),
            scratch(flat(HA + HB)),
            scratch(cat(HA + 3)),
            scratch(cat(HB + 3)),
            scratch(flat(half)),
            scratch(cat(half + 2)),
            scratch(flat(half + 2)),
            scratch(cat(half + 2, tile_cols)),
        ],
        compiler_params=pltpu.CompilerParams(vmem_limit_bytes=24 * 2**20),
        name="outer",
    )(
        scene_shift, from_row, *corners, pyr_a, pyr_b, *kept,
        w_lat, b_lat[None], w_fpn, w_dec1, b_dec1[None], w_dec2, b_dec2[None], w_out[None],
        jnp.broadcast_to(b_out, (1, tile_cols)),
    )
    return out


def staged(sizes, *args):
    return per_device(sizes, *args)


def solution(mesh):
    sizes = tuple(mesh.shape[axis] for axis in ("groups", "rows", "cols", "date"))
    return jax.shard_map(
        functools.partial(staged, sizes),
        mesh=mesh,
        in_specs=(P("date", ("groups", "rows"), "cols", None), P("groups", None, None)) + (P(),) * 9,
        out_specs=P(("groups", "rows", "date"), "cols"),
        check_vma=False,
    )
```

time: 18.6 us -> 17.9 us (0.962)
  Pallas kernels: 8.58 us -> 7.85 us
    pallas_call x1, Pallas kernels: 4.27 us -> 3.87 us  [per_device(): pl.pallas_call(functools.partial(outer_body, n_par, n_rows, n_cols, tile_...]
    pallas_call x1, Pallas kernels: 3.24 us -> 2.9 us  [per_device(): pl.pallas_call(functools.partial(inner_body, n_par, n_cols, tile_rows, ti...]
  transfers between devices with their start and end apart: 5 -> 5, of which waited for: 2 -> 2; matrix products, arithmetic and copies ran while one was open for 1% -> 1% of each run, Pallas kernels for 23% -> 22%
where the time goes in v4:
time: 17.9 us; the launch traced here: 17.8 us
  Pallas kernels  7.85 us (44%)
  starting transfers between devices  6.7 us (37%)
  waiting for transfers between devices  2.11 us (12%)
  between operations  0.86 us (5%)
    ppermute x5, starting transfers between devices, send(): return lax.ppermute(value, ('groups', 'rows', 'cols', 'date'), pairs)  6.7 us
    pallas_call x1, Pallas kernels, per_device(): pl.pallas_call(functools.partial(outer_body, n_par, n_rows, n_cols, tile_...  3.87 us
    pallas_call x1, Pallas kernels, per_device(): pl.pallas_call(functools.partial(inner_body, n_par, n_cols, tile_rows, ti...  2.9 us
    ppermute x5, waiting for transfers between devices, send(): return lax.ppermute(value, ('groups', 'rows', 'cols', 'date'), pairs)  2.11 us
    pallas_call x1, Pallas kernels, per_device(): pl.pallas_call(functools.partial(fetch_body, n_par, tile_rows, tile_cols)...  1.08 us
  transfers between devices with their start and end apart: 5, of which 2 were waited for; matrix products, arithmetic and copies ran while one was open for 1% of the time, Pallas kernels for 22%

profile of v4, /device:TPU:1, one launch (start us, length us, event | category | flops | bytes accessed | tf_op | source)
XLA Modules:
  0.0 17.8 jit_solution(10522142779487520205)
XLA Ops:
  0.0 0.0 copy-start.1
  0.0 0.0 copy-start.4
  0.0 0.0 copy-start.6
  0.0 0.0 copy-start.5
  0.0 0.1 collective-permute-start
  0.1 1.1 %fetch.1 = (bf16[7,128,128]{2,1,0:T(8,128)(2,1)S(1)}, bf16[16,8,128]{2,1,0:T(8,128)(2,1)S(1)}) custom-call(bf16[16,128,128]{2,1,0:T(8,128)(2,1)} %bitcast.8), custom_call_target="tpu_custom_call" | custom-call | tf_op jit(solution)/shard_map/fetch/pallas_call | solution.py:335
  1.2 1.0 %collective-permute-done.oth = bf16[16,128,128]{2,1,0:T(8,128)(2,1)S(1)} collective-permute-done((bf16[16,128,128]{2,1,0:T(8,128)(2,1)}, bf16[16,128,128]{2,1,0:T(8,128)(2,1)S(1)}, u32[]{:S(2)}, u32[]{:S(2)}) %collective-permute-start) | collective-permute-done | bytes 524320 | tf_op jit(solution)/shard_map/ppermute | solution.py:43
  2.3 2.7 %collective-permute-start.1 = (bf16[10,128,128]{2,1,0:T(8,128)(2,1)S(1)}, bf16[10,128,128]{2,1,0:T(8,128)(2,1)S(1)}, u32[]{:S(2)}, u32[]{:S(2)}) collective-permute-start(bf16[10,128,128]{2,1,0:T(8,128)(2,1)S(1)} %pad_maximum_fusion), channel_id=1, source_target_pairs={{0,16},{1,4},{2,18},{3,6},{4,1},{5,8},{6,3},{7,10},{8,5},{9,12},{1... | collective-permute-start | bytes 983048 | tf_op jit(solution)/shard_map/ppermute | solution.py:43
  5.1 1.2 %collective-permute-start.3 = (bf16[16,8,128]{2,1,0:T(8,128)(2,1)S(1)}, bf16[16,8,128]{2,1,0:T(8,128)(2,1)S(1)}, u32[]{:S(2)}, u32[]{:S(2)}) collective-permute-start(bf16[16,8,128]{2,1,0:T(8,128)(2,1)S(1)} %get-tuple-element.15), channel_id=1, source_target_pairs={{0,2},{1,3},{2,0},{3,1},{4,6},{5,7},{6,4},{7,5},{8,10},{9,11},{10,... | collective-permute-start | bytes 98312 | tf_op jit(solution)/shard_map/ppermute | solution.py:43
  6.9 0.1 copy.14.shift
  7.0 1.1 %collective-permute-done.3.refs_0_ = bf16[16,8,128]{2,1,0:T(8,128)(2,1)S(1)} collective-permute-done((bf16[16,8,128]{2,1,0:T(8,128)(2,1)S(1)}, bf16[16,8,128]{2,1,0:T(8,128)(2,1)S(1)}, u32[]{:S(2)}, u32[]{:S(2)}) %collective-permute-start.3) | collective-permute-done | bytes 32800 | tf_op jit(solution)/shard_map/ppermute | solution.py:43
  8.1 1.2 %collective-permute-start.4 = (bf16[16,8,128]{2,1,0:T(8,128)(2,1)S(1)}, bf16[16,8,128]{2,1,0:T(8,128)(2,1)S(1)}, u32[]{:S(2)}, u32[]{:S(2)}) collective-permute-start(bf16[16,8,128]{2,1,0:T(8,128)(2,1)S(1)} %collective-permute-done.3.refs_0_), channel_id=1, source_target_pairs={{0,1},{1,0},{2,3},{3,2},{4,5},{5,4},{6,7},{7,6},{8,9},{9,8},{10,11... | collective-permute-start | bytes 98312 | tf_op jit(solution)/shard_map/ppermute | solution.py:43
  9.3 1.5 %collective-permute-start.2 = (bf16[10,8,128]{2,1,0:T(8,128)(2,1)S(1)}, bf16[10,8,128]{2,1,0:T(8,128)(2,1)S(1)}, u32[]{:S(2)}, u32[]{:S(2)}) collective-permute-start(bf16[10,8,128]{2,1,0:T(8,128)(2,1)S(1)} %fusion.2), channel_id=1, source_target_pairs={{0,16},{1,6},{2,18},{3,4},{4,3},{5,10},{6,1},{7,8},{8,7},{9,14},{1... | collective-permute-start | bytes 61448 | tf_op jit(solution)/shard_map/ppermute | solution.py:43
  10.8 0.0 collective-permute-done.4.refs_1_
  10.8 0.0 copy-done.2
  10.9 0.0 copy-start.3
  10.9 0.0 copy-start.7
  10.9 0.0 copy-start.8
  10.9 2.9 %inner.1 = (bf16[8,144,128]{2,1,0:T(8,128)(2,1)S(1)}, f32[2896,128]{1,0:T(8,128)S(1)}, bf16[3,3,144,128]{3,2,1,0:T(8,128)(2,1)S(1)}, bf16[3,3,144,128]{3,2,1,0:T...) custom-call(s32[4,2,2]{2,1,0:T(2,128)S(1)} %copy.14.shift, ...), custom_call_target="tpu_custom_call" | custom-call | flops 1132462080 | bytes 8388608 | tf_op jit(solution)/shard_map/inner/pallas_call | solution.py:396
  13.8 0.0 collective-permute-done.2.refs_0_
  13.8 0.0 collective-permute-done.1.v_ref
  13.9 0.0 copy-done.3
  13.9 0.0 copy-done.7
  13.9 3.9 %outer.1 = (f32[8,128]{1,0:T(8,128)}, f32[2896,128]{1,0:T(8,128)S(1)}) custom-call(s32[4,2,2]{2,1,0:T(2,128)S(1)} %copy.14.shift, bf16[10,128,128]{2,1,0:T(8,128)(2,1)S(1)} %collective-permute-done.1.v_ref, bf16[10,8,128]{2,1,0:T(8,128)(2,1)S(1)} %collective-permute-done.2.refs_0_, ...), custom_call_target="tpu_custom_call", output_to_operand_aliasing={{1}: (4, {})} | custom-call | tf_op jit(solution)/shard_map/outer/pallas_call | solution.py:415
  (15 shorter events, 0.1 us)
Async XLA Ops:
  0.0 10.8 %copy-start = (bf16[1,16,128,128]{3,2,1,0:T(8,128)(2,1)S(1)}, bf16[1,16,128,128]{3,2,1,0:T(8,128)(2,1)}, u32[]{:S(2)}) copy-start(bf16[1,16,128,128]{3,2,1,0:T(8,128)(2,1)} %param.11) | copy-start | bytes 1572868
  0.0 6.9 %copy-start.9 = (s32[4,2,2]{0,2,1:T(2,128)S(1)}, s32[4,2,2]{0,2,1:T(2,128)}, u32[]{:S(2)}) copy-start(s32[4,2,2]{0,2,1:T(2,128)} %param.12) | copy-start | bytes 196
  0.0 10.8 %copy-start.2 = (bf16[3,3,128,128]{3,2,1,0:T(8,128)(2,1)S(1)}, bf16[3,3,128,128]{3,2,1,0:T(8,128)(2,1)}, u32[]{:S(2)}) copy-start(bf16[3,3,128,128]{3,2,1,0:T(8,128)(2,1)} %refs_10_.1) | copy-start | bytes 884740
  0.0 10.8 %copy-start.1 = (bf16[3,3,128,128]{3,2,1,0:T(8,128)(2,1)S(1)}, bf16[3,3,128,128]{3,2,1,0:T(8,128)(2,1)}, u32[]{:S(2)}) copy-start(bf16[3,3,128,128]{3,2,1,0:T(8,128)(2,1)} %refs_9_.1) | copy-start | bytes 884740
  0.0 10.8 %copy-start.4 = (bf16[128,128]{1,0:T(8,128)(2,1)S(1)}, bf16[128,128]{1,0:T(8,128)(2,1)}, u32[]{:S(2)}) copy-start(bf16[128,128]{1,0:T(8,128)(2,1)} %refs_7_.1) | copy-start | bytes 98308
  0.0 10.8 %copy-start.6 = (f32[128]{0:T(128)S(1)}, f32[128]{0:T(128)}, u32[]{:S(2)}) copy-start(f32[128]{0:T(128)} %param.17) | copy-start | bytes 1540
  0.0 10.8 %copy-start.5 = (f32[128]{0:T(128)S(1)}, f32[128]{0:T(128)}, u32[]{:S(2)}) copy-start(f32[128]{0:T(128)} %param.14) | copy-start | bytes 1540
  0.0 2.2 %collective-permute-start = (bf16[16,128,128]{2,1,0:T(8,128)(2,1)}, bf16[16,128,128]{2,1,0:T(8,128)(2,1)S(1)}, u32[]{:S(2)}, u32[]{:S(2)}) collective-permute-start(bf16[16,128,128]{2,1,0:T(8,128)(2,1)} %bitcast.7), channel_id=1, source_target_pairs={{0,1},{1,0},{2,3},{3,2},{4,5},{5,4},{6,7},{7,6},{8,9},{9,8},{10,11... | collective-permute-start | bytes 1572872 | tf_op jit(solution)/shard_map/ppermute | solution.py:43
  2.3 11.5 %collective-permute-start.1 = (bf16[10,128,128]{2,1,0:T(8,128)(2,1)S(1)}, bf16[10,128,128]{2,1,0:T(8,128)(2,1)S(1)}, u32[]{:S(2)}, u32[]{:S(2)}) collective-permute-start(bf16[10,128,128]{2,1,0:T(8,128)(2,1)S(1)} %pad_maximum_fusion), channel_id=1, source_target_pairs={{0,16},{1,4},{2,18},{3,6},{4,1},{5,8},{6,3},{7,10},{8,5},{9,12},{1... | collective-permute-start | bytes 983048 | tf_op jit(solution)/shard_map/ppermute | solution.py:43
  5.1 3.1 %collective-permute-start.3 = (bf16[16,8,128]{2,1,0:T(8,128)(2,1)S(1)}, bf16[16,8,128]{2,1,0:T(8,128)(2,1)S(1)}, u32[]{:S(2)}, u32[]{:S(2)}) collective-permute-start(bf16[16,8,128]{2,1,0:T(8,128)(2,1)S(1)} %get-tuple-element.15), channel_id=1, source_target_pairs={{0,2},{1,3},{2,0},{3,1},{4,6},{5,7},{6,4},{7,5},{8,10},{9,11},{10,... | collective-permute-start | bytes 98312 | tf_op jit(solution)/shard_map/ppermute | solution.py:43
  8.1 2.7 %collective-permute-start.4 = (bf16[16,8,128]{2,1,0:T(8,128)(2,1)S(1)}, bf16[16,8,128]{2,1,0:T(8,128)(2,1)S(1)}, u32[]{:S(2)}, u32[]{:S(2)}) collective-permute-start(bf16[16,8,128]{2,1,0:T(8,128)(2,1)S(1)} %collective-permute-done.3.refs_0_), channel_id=1, source_target_pairs={{0,1},{1,0},{2,3},{3,2},{4,5},{5,4},{6,7},{7,6},{8,9},{9,8},{10,11... | collective-permute-start | bytes 98312 | tf_op jit(solution)/shard_map/ppermute | solution.py:43
  9.3 4.5 %collective-permute-start.2 = (bf16[10,8,128]{2,1,0:T(8,128)(2,1)S(1)}, bf16[10,8,128]{2,1,0:T(8,128)(2,1)S(1)}, u32[]{:S(2)}, u32[]{:S(2)}) collective-permute-start(bf16[10,8,128]{2,1,0:T(8,128)(2,1)S(1)} %fusion.2), channel_id=1, source_target_pairs={{0,16},{1,6},{2,18},{3,4},{4,3},{5,10},{6,1},{7,8},{8,7},{9,14},{1... | collective-permute-start | bytes 61448 | tf_op jit(solution)/shard_map/ppermute | solution.py:43
  10.9 3.0 %copy-start.3 = (bf16[3,3,128,128]{3,2,1,0:T(8,128)(2,1)S(1)}, bf16[3,3,128,128]{3,2,1,0:T(8,128)(2,1)}, u32[]{:S(2)}) copy-start(bf16[3,3,128,128]{3,2,1,0:T(8,128)(2,1)} %refs_12_.1) | copy-start | bytes 884740
  10.9 3.0 %copy-start.7 = (f32[128]{0:T(128)S(1)}, f32[128]{0:T(128)}, u32[]{:S(2)}) copy-start(f32[128]{0:T(128)} %param.19) | copy-start | bytes 1540
  10.9 3.0 %copy-start.8 = (bf16[128]{0:T(256)(128)(2,1)S(1)}, bf16[128]{0:T(256)(128)(2,1)}, u32[]{:S(2)}) copy-start(bf16[128]{0:T(256)(128)(2,1)} %param.20) | copy-start | bytes 772

commit v5 on v4

--- a/solution.py
+++ b/solution.py
@@ -62,23 +62,27 @@
         cat[index, tap] = source[start + tap - 1 : start + tap - 1 + count].astype(BF16)
 
 
-def conv(parts, w_ref, date, ways=2):
+def conv(groups, w_ref, date, ways=2):
     taps = [w_ref[a + (2 - 2 * a) * date].reshape(-1, w_ref.shape[-1]) for a in range(3)]
     none = jnp.zeros_like(taps[0])
     tall = jnp.concatenate(
         [jnp.concatenate(taps + [none], axis=0), jnp.concatenate([none] + taps, axis=0)], axis=1
     )
-    tops = [(cat, first + 2 * i) for cat, first, pairs in parts for i in range(pairs)]
+    pairs = [lines[top : top + 4] for lines in groups for top in range(0, len(lines) - 2, 2)]
     outs = []
     for way in range(ways):
-        some = tops[way * len(tops) // ways : (way + 1) * len(tops) // ways]
+        some = pairs[way * len(pairs) // ways : (way + 1) * len(pairs) // ways]
         lines = [
-            jnp.concatenate([cat[top + j, tap] for cat, top in some], axis=0)
+            jnp.concatenate([pair[j][0][pair[j][1], tap] for pair in some], axis=0)
             for j in range(4)
             for tap in range(3)
         ]
         outs.append(jnp.dot(jnp.concatenate(lines, axis=1), tall, preferred_element_type=F32))
     return jnp.concatenate(outs, axis=0)
+
+
+def run(cat, first, count):
+    return [(cat, first + i) for i in range(count)]
 
 
 def line_of(z, index, columns):
@@ -122,39 +126,41 @@
 
 def difference(a_line, pyr_b, u, groups, inside, keep_line, width):
     plus = lambda x, y: y if x is None else x + y
+    blank = pyr_b.shape[0] - CW - width
     count = [None, None]
     level = [None, None]
-    mids = []
+    middle, weight = None, 0.0
     for tiles, hit_of in groups:
         for k, (sy, sx, is_tile, *masks) in enumerate(tiles):
             start = CW + (u - sy + 2 + MO) * width - sx
-            hit = None if hit_of is None else hit_of(sy)
+            hit = None
+            if hit_of is not None:
+                hit = hit_of(sy).astype(F32)
+                start = jnp.where(hit_of(sy), start, blank)
             for side in range(2):
                 if k != 2 - side:
                     mask = masks[side] if hit is None else masks[side] * hit
                     count[side] = plus(count[side], mask)
-                    strip = pyr_b[pl.ds(start + side * (width - STRIP), STRIP)] * mask
+                    strip = pyr_b[pl.ds(start + side * (width - STRIP), STRIP)] * masks[side]
                     level[side] = plus(level[side], strip)
             if k == 0:
-                value = pyr_b[pl.ds(start + STRIP, width - 2 * STRIP)]
-                mids.append((value, None if hit is None else hit * is_tile))
-    a = a_line.astype(F32)
+                if hit is not None:
+                    weight = weight + hit * is_tile
+                    start = jnp.where(is_tile > 0, start, blank)
+                middle = plus(middle, pyr_b[pl.ds(start + STRIP, width - 2 * STRIP)])
     outs = []
     for side in range(2):
-        part = a[:STRIP] if side == 0 else a[width - STRIP :]
+        part = a_line[:STRIP] if side == 0 else a_line[width - STRIP :]
         value = jnp.abs(part - level[side] * shares(count[side]))
         keep = jnp.minimum(count[side], 1.0) * inside[side]
         outs.append(value * (keep if keep_line is None else keep * keep_line))
-    middle = a[STRIP : width - STRIP]
-    if len(mids) == 1:
-        middle = jnp.abs(middle - mids[0][0])
+    part = a_line[STRIP : width - STRIP]
+    if len(groups) == 1:
+        middle = jnp.abs(part - middle)
     else:
-        weight = mids[0][1] + mids[1][1]
-        share = jnp.where(weight > 1.5, 0.5, 1.0)
         keep = jnp.minimum(weight, 1.0)
         keep = keep if keep_line is None else keep * keep_line
-        total = mids[0][0] * (mids[0][1] * share) + mids[1][0] * (mids[1][1] * share)
-        middle = jnp.abs(middle - total) * keep
+        middle = jnp.abs(part - middle * jnp.where(weight > 1.5, 0.5, 1.0)) * keep
     return jnp.concatenate([outs[0], middle, outs[1]], axis=0)
 
 
@@ -173,10 +179,12 @@
     return jnp.concatenate(parts, axis=0)
 
 
-def inner_body(n_par, n_cols, tile_rows, tile_cols, shift, own, oth, *refs):
+def inner_body(n_par, n_cols, tile_rows, tile_cols, shift_in, own, oth, *refs):
     mine, others = refs[:n_par], refs[n_par : 2 * n_par]
     (w_lat, b_lat, w_fpn, w_dec1, b_dec1,
-     pyr_a, pyr_b, t_a, t_b, t_d, hid, lat_a, lat_b, cat_a, cat_b, cat_d, dif) = refs[2 * n_par :]
+     pyr_a, pyr_b, t_a, t_b, t_d, hid, lat_a, lat_b, cat_a, cat_b, cat_d, dif, shift, sem) = refs[2 * n_par :]
+    shift_copy = pltpu.make_async_copy(shift_in, shift, sem)
+    shift_copy.start()
     row, col, date = position()
     half, width, chans = tile_rows // 2, tile_cols + 2 * CW, own.shape[-1]
     weight, bias = w_lat[...], b_lat[...]
@@ -208,14 +216,16 @@
         t_a[u] = cat_a[u]
         t_b[u] = cat_b[u]
     pairs_a, pairs_b = half // 2, half // 2 + MO // 2
-    z = conv([(cat_a, 1, pairs_a), (cat_b, 1, pairs_b)], w_fpn, date).astype(BF16)
+    z = conv([run(cat_a, 1, 2 * pairs_a + 2), run(cat_b, 1, 2 * pairs_b + 2)], w_fpn, date)
     for i in range(2 * pairs_a):
         pyr_a[i] = line_of(z, i, width)
     pyr_b[:CW] = jnp.zeros((CW, chans), F32)
-    pyr_b[pyr_b.shape[0] - CW :] = jnp.zeros((CW, chans), F32)
+    blank = pyr_b.shape[0] - CW - width
+    pyr_b[blank:] = jnp.zeros((width + CW, chans), F32)
     for i in range(2 * pairs_b):
-        put(pyr_b, i + 4 + MO, -CW, width, line_of(z, 2 * pairs_a + i, width).astype(F32))
-
+        put(pyr_b, i + 4 + MO, -CW, width, line_of(z, 2 * pairs_a + i, width))
+
+    shift_copy.wait()
     tiles = tile_columns(row, col, row >= 0, shift, date, n_cols, tile_cols, chans)
     inside = grid_columns(col, n_cols, tile_cols, chans)
     for i in range(4):
@@ -226,24 +236,26 @@
         gather(dif, i, cat_d, i, width, -CW, width)
     for i in range(2):
         t_d[i] = cat_d[i]
-    z = conv([(cat_d, 0, 1)], w_dec1, date, 1)
+    z = conv([run(cat_d, 0, 4)], w_dec1, date, 1)
     z = jnp.maximum(z + jnp.concatenate([b_dec1[...]] * 2, 1), 0.0)
     for i in range(2):
         put(hid, i, -CW, width, on_grid(line_of(z, i, width), inside, None))
 
 
-def outer_body(n_par, n_rows, n_cols, tile_rows, tile_cols, shift, v_ref, *refs):
+def outer_body(n_par, n_rows, n_cols, tile_rows, tile_cols, shift_in, v_ref, *refs):
     corners = refs[:n_par]
     (in_a, _, t_a, t_b, t_d, t_h, w_lat, b_lat, w_fpn, w_dec1, b_dec1, w_dec2, b_dec2, w_out, b_out,
-     out_ref, pyr_b, pyr_a, lat, cat_a, cat_b, dif, cat_d, hid, cat_h) = refs[n_par:]
+     out_ref, pyr_b, pyr_a, lat, cat_a, cat_b, dif, cat_d, hid, cat_h, shift, sem) = refs[n_par:]
+    shift_copy = pltpu.make_async_copy(shift_in, shift, sem)
+    shift_copy.start()
     row, col, date = position()
     half, width, chans = tile_rows // 2, tile_cols + 2 * CW, w_lat.shape[-1]
     has_row = jnp.where(date == 0, row > 0, row < n_rows - 1)
     row_keep = has_row.astype(F32)
-    weight, bias = w_lat[...], b_lat[...]
+    weight, bias = jnp.where(has_row, w_lat[...], 0), b_lat[...] * row_keep
 
     def lateral(x):
-        return (jnp.dot(x, weight, preferred_element_type=F32) + bias) * row_keep
+        return jnp.dot(x, weight, preferred_element_type=F32) + bias
 
     lines = [i + (HA - 1 - 2 * i) * date for i in range(HA)]
     lines += [HA + i + (HB - 1 - 2 * i) * date for i in range(HB)]
@@ -257,17 +269,15 @@
         gather(lat, i, cat_a, i, width, -CW, width)
     for i in range(HB):
         gather(lat, i + HA, cat_b, i, width, -CW, width)
-    for i in range(3):
-        cat_a[i + HA] = t_a[i]
-        cat_b[i + HB] = t_b[i]
     pairs_b = 2 + MO // 2
-    z = conv([(cat_a, 0, 2), (cat_b, 0, pairs_b)], w_fpn, date).astype(BF16)
+    z = conv([run(cat_a, 0, HA) + run(t_a, 0, 3), run(cat_b, 0, HB) + run(t_b, 0, 3)], w_fpn, date)
     for i in range(4):
         pyr_a[i] = line_of(z, i, width)
     for i in range(2 * pairs_b):
-        put(pyr_b, i, -CW, width, line_of(z, 4 + i, width).astype(F32))
+        put(pyr_b, i, -CW, width, line_of(z, 4 + i, width))
 
     near_row = jnp.clip(row + jnp.where(date == 0, -1, 1), 0, n_rows - 1)
+    shift_copy.wait()
     tiles = tile_columns(row, col, row >= 0, shift, date, n_cols, tile_cols, chans)
     near = tile_columns(near_row, col, has_row, shift, date, n_cols, tile_cols, chans)
     inside = grid_columns(col, n_cols, tile_cols, chans)
@@ -276,24 +286,23 @@
         groups = [(tiles, None)]
         if u < MO:
             groups = [
-                (tiles, lambda sy, u=u: (u - sy >= 0).astype(F32)),
-                (near, lambda sy, u=u: (u - sy < 0).astype(F32)),
+                (tiles, lambda sy, u=u: u - sy >= 0),
+                (near, lambda sy, u=u: u - sy < 0),
             ]
         a_line = pyr_a[u + 2] if u < 2 else in_a[u - 2]
         value = difference(a_line, pyr_b, u, groups, inside, row_keep if u < 0 else None, width)
         put(dif, i, -CW, width, value)
     for i in range(half):
         gather(dif, i, cat_d, i, width, -CW, width)
-    for i in range(2):
-        cat_d[i + half] = t_d[i]
-        put(hid, i + half, -CW, width, t_h[CW + i * width : CW + (i + 1) * width])
-    z = conv([(cat_d, 0, half // 2)], w_dec1, date)
+    z = conv([run(cat_d, 0, half) + run(t_d, 0, 2)], w_dec1, date)
     z = jnp.maximum(z + jnp.concatenate([b_dec1[...]] * 2, 1), 0.0)
     for i in range(half):
         put(hid, i, -CW, width, on_grid(line_of(z, i, width), inside, None if i else row_keep))
-    for i in range(half + 2):
+    for i in range(half):
         gather(hid, i, cat_h, i, tile_cols, 0, width)
-    z = conv([(cat_h, 0, half // 2)], w_dec2, date)
+    for i in range(2):
+        gather(t_h, i, cat_h, i + half, tile_cols, 0, width)
+    z = conv([run(cat_h, 0, half + 2)], w_dec2, date)
     z = jnp.maximum(z + jnp.concatenate([b_dec2[...]] * 2, 1), 0.0).astype(BF16)
     none = jnp.zeros((1, chans), BF16)
     upper = jnp.concatenate([w_out[...], none], axis=1)
@@ -378,8 +387,8 @@
         others.append(swap(mine[p]))
     for p in range(n_par):
         corners.append(send(edge(for_row, p), sizes, functools.partial(corner, p)))
-    smem = pl.BlockSpec(memory_space=pltpu.SMEM)
-    lines_b = half + 4 + 2 * MO
+    shifts = [pltpu.SMEM(scene_shift.shape, jnp.int32), pltpu.SemaphoreType.DMA]
+    lines_b = half + 4 + 2 * MO + 1
 
     def flat(lines, kind=F32):
         return jax.ShapeDtypeStruct((2 * CW + lines * width, chans), kind)
@@ -391,12 +400,12 @@
         return pltpu.VMEM(shape.shape, shape.dtype)
 
     def lines_of(lines):
-        return jax.ShapeDtypeStruct((lines, width, chans), BF16)
+        return jax.ShapeDtypeStruct((lines, width, chans), F32)
 
     pyr_a, pyr_b, *kept = pl.pallas_call(
         functools.partial(inner_body, n_par, n_cols, tile_rows, tile_cols),
         out_shape=(lines_of(half), flat(lines_b), cat(3), cat(3), cat(2), flat(2)),
-        in_specs=[smem] + [vmem] * (2 + 2 * n_par + 5),
+        in_specs=[pl.BlockSpec(memory_space=pl.ANY)] + [vmem] * (2 + 2 * n_par + 5),
         out_specs=(vmem,) * 6,
         scratch_shapes=[
             scratch(flat(half + HA)),
@@ -405,6 +414,7 @@
             scratch(cat(half + HB)),
             scratch(cat(4)),
             scratch(flat(4)),
+            *shifts,
         ],
         compiler_params=pltpu.CompilerParams(vmem_limit_bytes=28 * 2**20),
         cost_estimate=pl.CostEstimate(
@@ -415,18 +425,19 @@
     out, _ = pl.pallas_call(
         functools.partial(outer_body, n_par, n_rows, n_cols, tile_rows, tile_cols),
         out_shape=(jax.ShapeDtypeStruct((half, tile_cols), F32), flat(lines_b)),
-        in_specs=[smem] + [vmem] * (n_par + 1 + 15),
+        in_specs=[pl.BlockSpec(memory_space=pl.ANY)] + [vmem] * (n_par + 1 + 15),
         out_specs=(vmem,) * 2,
         input_output_aliases={n_par + 3: 1},
         scratch_shapes=[
             scratch(lines_of(4)),
             scratch(flat(HA + HB)),
-            scratch(cat(HA + 3)),
-            scratch(cat(HB + 3)),
+            scratch(cat(HA)),
+            scratch(cat(HB)),
             scratch(flat(half)),
-            scratch(cat(half + 2)),
-            scratch(flat(half + 2)),
+            scratch(cat(half)),
+            scratch(flat(half)),
             scratch(cat(half + 2, tile_cols)),
+            *shifts,
         ],
         compiler_params=pltpu.CompilerParams(vmem_limit_bytes=24 * 2**20),
         name="outer",

time: 17.9 us -> 17 us (0.950)
  Pallas kernels: 7.85 us -> 6.72 us
  waiting for transfers between devices: 2.11 us -> 2.36 us
    pallas_call x1, Pallas kernels: 2.9 us -> 2.33 us  [per_device(): pl.pallas_call(functools.partial(inner_body, n_par, n_cols, tile_rows, ti...]
    pallas_call x1, Pallas kernels: 3.87 us -> 3.32 us  [per_device(): pl.pallas_call(functools.partial(outer_body, n_par, n_rows, n_cols, tile_...]
    ppermute x5, waiting for transfers between devices: 2.11 us -> 2.36 us  [send(): return lax.ppermute(value, ('groups', 'rows', 'cols', 'date'), pairs)]
  transfers between devices with their start and end apart: 5 -> 5, of which waited for: 2 -> 3; matrix products, arithmetic and copies ran while one was open for 1% -> 1% of each run, Pallas kernels for 22% -> 20%
where the time goes in v5:
time: 17 us; the launch traced here: 16.9 us
  Pallas kernels  6.72 us (40%)
  starting transfers between devices  6.7 us (39%)
  waiting for transfers between devices  2.36 us (14%)
  between operations  0.84 us (5%)
    ppermute x5, starting transfers between devices, send(): return lax.ppermute(value, ('groups', 'rows', 'cols', 'date'), pairs)  6.7 us
    pallas_call x1, Pallas kernels, per_device(): pl.pallas_call(functools.partial(outer_body, n_par, n_rows, n_cols, tile_...  3.32 us
    ppermute x5, waiting for transfers between devices, send(): return lax.ppermute(value, ('groups', 'rows', 'cols', 'date'), pairs)  2.36 us
    pallas_call x1, Pallas kernels, per_device(): pl.pallas_call(functools.partial(inner_body, n_par, n_cols, tile_rows, ti...  2.33 us
    pallas_call x1, Pallas kernels, per_device(): pl.pallas_call(functools.partial(fetch_body, n_par, tile_rows, tile_cols)...  1.08 us
  transfers between devices with their start and end apart: 5, of which 3 were waited for; matrix products, arithmetic and copies ran while one was open for 1% of the time, Pallas kernels for 20%

profile of v5, /device:TPU:1, one launch (start us, length us, event | category | flops | bytes accessed | tf_op | source)
XLA Modules:
  0.0 16.9 jit_solution(14094752607015478170)
XLA Ops:
  0.0 0.0 copy-start.1
  0.0 0.0 copy-start.4
  0.0 0.0 copy-start.6
  0.0 0.0 copy-start.5
  0.0 0.1 collective-permute-start
  0.1 1.1 %fetch.1 = (bf16[7,128,128]{2,1,0:T(8,128)(2,1)S(1)}, bf16[16,8,128]{2,1,0:T(8,128)(2,1)S(1)}) custom-call(bf16[16,128,128]{2,1,0:T(8,128)(2,1)} %bitcast.8), custom_call_target="tpu_custom_call" | custom-call | tf_op jit(solution)/shard_map/fetch/pallas_call | solution.py:344
  1.2 1.0 %collective-permute-done.oth = bf16[16,128,128]{2,1,0:T(8,128)(2,1)S(1)} collective-permute-done((bf16[16,128,128]{2,1,0:T(8,128)(2,1)}, bf16[16,128,128]{2,1,0:T(8,128)(2,1)S(1)}, u32[]{:S(2)}, u32[]{:S(2)}) %collective-permute-start) | collective-permute-done | bytes 524320 | tf_op jit(solution)/shard_map/ppermute | solution.py:43
  2.3 2.7 %collective-permute-start.1 = (bf16[10,128,128]{2,1,0:T(8,128)(2,1)S(1)}, bf16[10,128,128]{2,1,0:T(8,128)(2,1)S(1)}, u32[]{:S(2)}, u32[]{:S(2)}) collective-permute-start(bf16[10,128,128]{2,1,0:T(8,128)(2,1)S(1)} %pad_maximum_fusion), channel_id=1, source_target_pairs={{0,16},{1,4},{2,18},{3,6},{4,1},{5,8},{6,3},{7,10},{8,5},{9,12},{1... | collective-permute-start | bytes 983048 | tf_op jit(solution)/shard_map/ppermute | solution.py:43
  5.1 1.2 %collective-permute-start.3 = (bf16[16,8,128]{2,1,0:T(8,128)(2,1)S(1)}, bf16[16,8,128]{2,1,0:T(8,128)(2,1)S(1)}, u32[]{:S(2)}, u32[]{:S(2)}) collective-permute-start(bf16[16,8,128]{2,1,0:T(8,128)(2,1)S(1)} %get-tuple-element.15), channel_id=1, source_target_pairs={{0,2},{1,3},{2,0},{3,1},{4,6},{5,7},{6,4},{7,5},{8,10},{9,11},{10,... | collective-permute-start | bytes 98312 | tf_op jit(solution)/shard_map/ppermute | solution.py:43
  6.9 0.0 copy-done.9
  6.9 0.1 copy.14.shift_in
  7.0 1.1 %collective-permute-done.3.refs_0_ = bf16[16,8,128]{2,1,0:T(8,128)(2,1)S(1)} collective-permute-done((bf16[16,8,128]{2,1,0:T(8,128)(2,1)S(1)}, bf16[16,8,128]{2,1,0:T(8,128)(2,1)S(1)}, u32[]{:S(2)}, u32[]{:S(2)}) %collective-permute-start.3) | collective-permute-done | bytes 32800 | tf_op jit(solution)/shard_map/ppermute | solution.py:43
  8.1 1.2 %collective-permute-start.4 = (bf16[16,8,128]{2,1,0:T(8,128)(2,1)S(1)}, bf16[16,8,128]{2,1,0:T(8,128)(2,1)S(1)}, u32[]{:S(2)}, u32[]{:S(2)}) collective-permute-start(bf16[16,8,128]{2,1,0:T(8,128)(2,1)S(1)} %collective-permute-done.3.refs_0_), channel_id=1, source_target_pairs={{0,1},{1,0},{2,3},{3,2},{4,5},{5,4},{6,7},{7,6},{8,9},{9,8},{10,11... | collective-permute-start | bytes 98312 | tf_op jit(solution)/shard_map/ppermute | solution.py:43
  9.3 1.5 %collective-permute-start.2 = (bf16[10,8,128]{2,1,0:T(8,128)(2,1)S(1)}, bf16[10,8,128]{2,1,0:T(8,128)(2,1)S(1)}, u32[]{:S(2)}, u32[]{:S(2)}) collective-permute-start(bf16[10,8,128]{2,1,0:T(8,128)(2,1)S(1)} %fusion.2), channel_id=1, source_target_pairs={{0,16},{1,6},{2,18},{3,4},{4,3},{5,10},{6,1},{7,8},{8,7},{9,14},{1... | collective-permute-start | bytes 61448 | tf_op jit(solution)/shard_map/ppermute | solution.py:43
  10.8 0.0 collective-permute-done.4.refs_1_
  10.8 0.0 copy-done.2
  10.9 0.0 copy-start.3
  10.9 0.0 copy-start.7
  10.9 0.0 copy-start.8
  10.9 2.3 %inner.1 = (f32[8,144,128]{2,1,0:T(8,128)S(1)}, f32[3040,128]{1,0:T(8,128)S(1)}, bf16[3,3,144,128]{3,2,1,0:T(8,128)(2,1)S(1)}, bf16[3,3,144,128]{3,2,1,0:T(8,128...) custom-call(s32[4,2,2]{2,1,0:T(2,128)S(1)} %copy.14.shift_in, ...), custom_call_target="tpu_custom_call" | custom-call | flops 1132462080 | bytes 8388608 | tf_op jit(solution)/shard_map/inner/pallas_call | solution.py:405
  13.3 0.3 %collective-permute-done.2.refs_0_ = bf16[10,8,128]{2,1,0:T(8,128)(2,1)S(1)} collective-permute-done((bf16[10,8,128]{2,1,0:T(8,128)(2,1)S(1)}, bf16[10,8,128]{2,1,0:T(8,128)(2,1)S(1)}, u32[]{:S(2)}, u32[]{:S(2)}) %collective-permute-start.2) | collective-permute-done | bytes 20512 | tf_op jit(solution)/shard_map/ppermute | solution.py:43
  13.5 0.0 collective-permute-done.1.v_ref
  13.5 0.0 copy-done.3
  13.5 3.3 %outer.1 = (f32[8,128]{1,0:T(8,128)}, f32[3040,128]{1,0:T(8,128)S(1)}) custom-call(s32[4,2,2]{2,1,0:T(2,128)S(1)} %copy.14.shift_in, bf16[10,128,128]{2,1,0:T(8,128)(2,1)S(1)} %collective-permute-done.1.v_ref, bf16[10,8,128]{2,1,0:T(8,128)(2,1)S(1)} %collective-permute-done.2.refs_0_, ...), custom_call_target="tpu_custom_call", output_to_operand_aliasing={{1}: (4, {})} | custom-call | tf_op jit(solution)/shard_map/outer/pallas_call | solution.py:425
  (15 shorter events, 0.1 us)
Async XLA Ops:
  0.0 10.8 %copy-start = (bf16[1,16,128,128]{3,2,1,0:T(8,128)(2,1)S(1)}, bf16[1,16,128,128]{3,2,1,0:T(8,128)(2,1)}, u32[]{:S(2)}) copy-start(bf16[1,16,128,128]{3,2,1,0:T(8,128)(2,1)} %param.11) | copy-start | bytes 1572868
  0.0 6.9 %copy-start.9 = (s32[4,2,2]{0,2,1:T(2,128)S(1)}, s32[4,2,2]{0,2,1:T(2,128)}, u32[]{:S(2)}) copy-start(s32[4,2,2]{0,2,1:T(2,128)} %param.12) | copy-start | bytes 196
  0.0 10.8 %copy-start.2 = (bf16[3,3,128,128]{3,2,1,0:T(8,128)(2,1)S(1)}, bf16[3,3,128,128]{3,2,1,0:T(8,128)(2,1)}, u32[]{:S(2)}) copy-start(bf16[3,3,128,128]{3,2,1,0:T(8,128)(2,1)} %refs_10_.1) | copy-start | bytes 884740
  0.0 10.8 %copy-start.1 = (bf16[3,3,128,128]{3,2,1,0:T(8,128)(2,1)S(1)}, bf16[3,3,128,128]{3,2,1,0:T(8,128)(2,1)}, u32[]{:S(2)}) copy-start(bf16[3,3,128,128]{3,2,1,0:T(8,128)(2,1)} %refs_9_.1) | copy-start | bytes 884740
  0.0 10.8 %copy-start.4 = (bf16[128,128]{1,0:T(8,128)(2,1)S(1)}, bf16[128,128]{1,0:T(8,128)(2,1)}, u32[]{:S(2)}) copy-start(bf16[128,128]{1,0:T(8,128)(2,1)} %refs_7_.1) | copy-start | bytes 98308
  0.0 10.8 %copy-start.6 = (f32[128]{0:T(128)S(1)}, f32[128]{0:T(128)}, u32[]{:S(2)}) copy-start(f32[128]{0:T(128)} %param.17) | copy-start | bytes 1540
  0.0 10.8 %copy-start.5 = (f32[128]{0:T(128)S(1)}, f32[128]{0:T(128)}, u32[]{:S(2)}) copy-start(f32[128]{0:T(128)} %param.14) | copy-start | bytes 1540
  0.0 2.2 %collective-permute-start = (bf16[16,128,128]{2,1,0:T(8,128)(2,1)}, bf16[16,128,128]{2,1,0:T(8,128)(2,1)S(1)}, u32[]{:S(2)}, u32[]{:S(2)}) collective-permute-start(bf16[16,128,128]{2,1,0:T(8,128)(2,1)} %bitcast.7), channel_id=1, source_target_pairs={{0,1},{1,0},{2,3},{3,2},{4,5},{5,4},{6,7},{7,6},{8,9},{9,8},{10,11... | collective-permute-start | bytes 1572872 | tf_op jit(solution)/shard_map/ppermute | solution.py:43
  2.3 11.2 %collective-permute-start.1 = (bf16[10,128,128]{2,1,0:T(8,128)(2,1)S(1)}, bf16[10,128,128]{2,1,0:T(8,128)(2,1)S(1)}, u32[]{:S(2)}, u32[]{:S(2)}) collective-permute-start(bf16[10,128,128]{2,1,0:T(8,128)(2,1)S(1)} %pad_maximum_fusion), channel_id=1, source_target_pairs={{0,16},{1,4},{2,18},{3,6},{4,1},{5,8},{6,3},{7,10},{8,5},{9,12},{1... | collective-permute-start | bytes 983048 | tf_op jit(solution)/shard_map/ppermute | solution.py:43
  5.1 3.1 %collective-permute-start.3 = (bf16[16,8,128]{2,1,0:T(8,128)(2,1)S(1)}, bf16[16,8,128]{2,1,0:T(8,128)(2,1)S(1)}, u32[]{:S(2)}, u32[]{:S(2)}) collective-permute-start(bf16[16,8,128]{2,1,0:T(8,128)(2,1)S(1)} %get-tuple-element.15), channel_id=1, source_target_pairs={{0,2},{1,3},{2,0},{3,1},{4,6},{5,7},{6,4},{7,5},{8,10},{9,11},{10,... | collective-permute-start | bytes 98312 | tf_op jit(solution)/shard_map/ppermute | solution.py:43
  8.1 2.7 %collective-permute-start.4 = (bf16[16,8,128]{2,1,0:T(8,128)(2,1)S(1)}, bf16[16,8,128]{2,1,0:T(8,128)(2,1)S(1)}, u32[]{:S(2)}, u32[]{:S(2)}) collective-permute-start(bf16[16,8,128]{2,1,0:T(8,128)(2,1)S(1)} %collective-permute-done.3.refs_0_), channel_id=1, source_target_pairs={{0,1},{1,0},{2,3},{3,2},{4,5},{5,4},{6,7},{7,6},{8,9},{9,8},{10,11... | collective-permute-start | bytes 98312 | tf_op jit(solution)/shard_map/ppermute | solution.py:43
  9.3 4.2 %collective-permute-start.2 = (bf16[10,8,128]{2,1,0:T(8,128)(2,1)S(1)}, bf16[10,8,128]{2,1,0:T(8,128)(2,1)S(1)}, u32[]{:S(2)}, u32[]{:S(2)}) collective-permute-start(bf16[10,8,128]{2,1,0:T(8,128)(2,1)S(1)} %fusion.2), channel_id=1, source_target_pairs={{0,16},{1,6},{2,18},{3,4},{4,3},{5,10},{6,1},{7,8},{8,7},{9,14},{1... | collective-permute-start | bytes 61448 | tf_op jit(solution)/shard_map/ppermute | solution.py:43
  10.9 2.6 %copy-start.3 = (bf16[3,3,128,128]{3,2,1,0:T(8,128)(2,1)S(1)}, bf16[3,3,128,128]{3,2,1,0:T(8,128)(2,1)}, u32[]{:S(2)}) copy-start(bf16[3,3,128,128]{3,2,1,0:T(8,128)(2,1)} %refs_12_.1) | copy-start | bytes 884740
  10.9 2.6 %copy-start.7 = (f32[128]{0:T(128)S(1)}, f32[128]{0:T(128)}, u32[]{:S(2)}) copy-start(f32[128]{0:T(128)} %param.19) | copy-start | bytes 1540
  10.9 2.6 %copy-start.8 = (bf16[128]{0:T(256)(128)(2,1)S(1)}, bf16[128]{0:T(256)(128)(2,1)}, u32[]{:S(2)}) copy-start(bf16[128]{0:T(256)(128)(2,1)} %param.20) | copy-start | bytes 772

commit v6 on v5

--- a/solution.py
+++ b/solution.py
@@ -218,12 +218,13 @@
     pairs_a, pairs_b = half // 2, half // 2 + MO // 2
     z = conv([run(cat_a, 1, 2 * pairs_a + 2), run(cat_b, 1, 2 * pairs_b + 2)], w_fpn, date)
     for i in range(2 * pairs_a):
-        pyr_a[i] = line_of(z, i, width)
+        pyr_a[i] = line_of(z, i, width).astype(BF16).astype(F32)
     pyr_b[:CW] = jnp.zeros((CW, chans), F32)
     blank = pyr_b.shape[0] - CW - width
     pyr_b[blank:] = jnp.zeros((width + CW, chans), F32)
     for i in range(2 * pairs_b):
-        put(pyr_b, i + 4 + MO, -CW, width, line_of(z, 2 * pairs_a + i, width))
+        line = line_of(z, 2 * pairs_a + i, width).astype(BF16).astype(F32)
+        put(pyr_b, i + 4 + MO, -CW, width, line)
 
     shift_copy.wait()
     tiles = tile_columns(row, col, row >= 0, shift, date, n_cols, tile_cols, chans)

time: 17 us -> 17 us (level)
  no operation moved by 1% of the time
where the time goes in v6:
time: 17 us; the launch traced here: 16.9 us
  Pallas kernels  6.73 us (40%)
  starting transfers between devices  6.7 us (39%)
  waiting for transfers between devices  2.36 us (14%)
  between operations  0.84 us (5%)
    ppermute x5, starting transfers between devices, send(): return lax.ppermute(value, ('groups', 'rows', 'cols', 'date'), pairs)  6.7 us
    pallas_call x1, Pallas kernels, per_device(): pl.pallas_call(functools.partial(outer_body, n_par, n_rows, n_cols, tile_...  3.32 us
    ppermute x5, waiting for transfers between devices, send(): return lax.ppermute(value, ('groups', 'rows', 'cols', 'date'), pairs)  2.36 us
    pallas_call x1, Pallas kernels, per_device(): pl.pallas_call(functools.partial(inner_body, n_par, n_cols, tile_rows, ti...  2.33 us
    pallas_call x1, Pallas kernels, per_device(): pl.pallas_call(functools.partial(fetch_body, n_par, tile_rows, tile_cols)...  1.08 us
  transfers between devices with their start and end apart: 5, of which 3 were waited for; matrix products, arithmetic and copies ran while one was open for 1% of the time, Pallas kernels for 20%

profile of v6, /device:TPU:1, one launch (start us, length us, event | category | flops | bytes accessed | tf_op | source)
XLA Modules:
  0.0 16.9 jit_solution(4698117740587657885)
XLA Ops:
  0.0 0.0 copy-start.1
  0.0 0.0 copy-start.4
  0.0 0.0 copy-start.6
  0.0 0.0 copy-start.5
  0.0 0.1 collective-permute-start
  0.1 1.1 %fetch.1 = (bf16[7,128,128]{2,1,0:T(8,128)(2,1)S(1)}, bf16[16,8,128]{2,1,0:T(8,128)(2,1)S(1)}) custom-call(bf16[16,128,128]{2,1,0:T(8,128)(2,1)} %bitcast.8), custom_call_target="tpu_custom_call" | custom-call | tf_op jit(solution)/shard_map/fetch/pallas_call | solution.py:345
  1.2 1.0 %collective-permute-done.oth = bf16[16,128,128]{2,1,0:T(8,128)(2,1)S(1)} collective-permute-done((bf16[16,128,128]{2,1,0:T(8,128)(2,1)}, bf16[16,128,128]{2,1,0:T(8,128)(2,1)S(1)}, u32[]{:S(2)}, u32[]{:S(2)}) %collective-permute-start) | collective-permute-done | bytes 524320 | tf_op jit(solution)/shard_map/ppermute | solution.py:43
  2.3 2.7 %collective-permute-start.1 = (bf16[10,128,128]{2,1,0:T(8,128)(2,1)S(1)}, bf16[10,128,128]{2,1,0:T(8,128)(2,1)S(1)}, u32[]{:S(2)}, u32[]{:S(2)}) collective-permute-start(bf16[10,128,128]{2,1,0:T(8,128)(2,1)S(1)} %pad_maximum_fusion), channel_id=1, source_target_pairs={{0,16},{1,4},{2,18},{3,6},{4,1},{5,8},{6,3},{7,10},{8,5},{9,12},{1... | collective-permute-start | bytes 983048 | tf_op jit(solution)/shard_map/ppermute | solution.py:43
  5.1 1.2 %collective-permute-start.3 = (bf16[16,8,128]{2,1,0:T(8,128)(2,1)S(1)}, bf16[16,8,128]{2,1,0:T(8,128)(2,1)S(1)}, u32[]{:S(2)}, u32[]{:S(2)}) collective-permute-start(bf16[16,8,128]{2,1,0:T(8,128)(2,1)S(1)} %get-tuple-element.15), channel_id=1, source_target_pairs={{0,2},{1,3},{2,0},{3,1},{4,6},{5,7},{6,4},{7,5},{8,10},{9,11},{10,... | collective-permute-start | bytes 98312 | tf_op jit(solution)/shard_map/ppermute | solution.py:43
  6.9 0.0 copy-done.9
  6.9 0.1 copy.14.shift_in
  7.0 1.1 %collective-permute-done.3.refs_0_ = bf16[16,8,128]{2,1,0:T(8,128)(2,1)S(1)} collective-permute-done((bf16[16,8,128]{2,1,0:T(8,128)(2,1)S(1)}, bf16[16,8,128]{2,1,0:T(8,128)(2,1)S(1)}, u32[]{:S(2)}, u32[]{:S(2)}) %collective-permute-start.3) | collective-permute-done | bytes 32800 | tf_op jit(solution)/shard_map/ppermute | solution.py:43
  8.1 1.2 %collective-permute-start.4 = (bf16[16,8,128]{2,1,0:T(8,128)(2,1)S(1)}, bf16[16,8,128]{2,1,0:T(8,128)(2,1)S(1)}, u32[]{:S(2)}, u32[]{:S(2)}) collective-permute-start(bf16[16,8,128]{2,1,0:T(8,128)(2,1)S(1)} %collective-permute-done.3.refs_0_), channel_id=1, source_target_pairs={{0,1},{1,0},{2,3},{3,2},{4,5},{5,4},{6,7},{7,6},{8,9},{9,8},{10,11... | collective-permute-start | bytes 98312 | tf_op jit(solution)/shard_map/ppermute | solution.py:43
  9.3 1.5 %collective-permute-start.2 = (bf16[10,8,128]{2,1,0:T(8,128)(2,1)S(1)}, bf16[10,8,128]{2,1,0:T(8,128)(2,1)S(1)}, u32[]{:S(2)}, u32[]{:S(2)}) collective-permute-start(bf16[10,8,128]{2,1,0:T(8,128)(2,1)S(1)} %fusion.2), channel_id=1, source_target_pairs={{0,16},{1,6},{2,18},{3,4},{4,3},{5,10},{6,1},{7,8},{8,7},{9,14},{1... | collective-permute-start | bytes 61448 | tf_op jit(solution)/shard_map/ppermute | solution.py:43
  10.8 0.0 collective-permute-done.4.refs_1_
  10.8 0.0 copy-done.2
  10.9 0.0 copy-start.3
  10.9 0.0 copy-start.7
  10.9 0.0 copy-start.8
  10.9 2.3 %inner.1 = (f32[8,144,128]{2,1,0:T(8,128)S(1)}, f32[3040,128]{1,0:T(8,128)S(1)}, bf16[3,3,144,128]{3,2,1,0:T(8,128)(2,1)S(1)}, bf16[3,3,144,128]{3,2,1,0:T(8,128...) custom-call(s32[4,2,2]{2,1,0:T(2,128)S(1)} %copy.14.shift_in, ...), custom_call_target="tpu_custom_call" | custom-call | flops 1132462080 | bytes 8388608 | tf_op jit(solution)/shard_map/inner/pallas_call | solution.py:406
  13.3 0.3 %collective-permute-done.2.refs_0_ = bf16[10,8,128]{2,1,0:T(8,128)(2,1)S(1)} collective-permute-done((bf16[10,8,128]{2,1,0:T(8,128)(2,1)S(1)}, bf16[10,8,128]{2,1,0:T(8,128)(2,1)S(1)}, u32[]{:S(2)}, u32[]{:S(2)}) %collective-permute-start.2) | collective-permute-done | bytes 20512 | tf_op jit(solution)/shard_map/ppermute | solution.py:43
  13.5 0.0 collective-permute-done.1.v_ref
  13.5 0.0 copy-done.3
  13.5 3.3 %outer.1 = (f32[8,128]{1,0:T(8,128)}, f32[3040,128]{1,0:T(8,128)S(1)}) custom-call(s32[4,2,2]{2,1,0:T(2,128)S(1)} %copy.14.shift_in, bf16[10,128,128]{2,1,0:T(8,128)(2,1)S(1)} %collective-permute-done.1.v_ref, bf16[10,8,128]{2,1,0:T(8,128)(2,1)S(1)} %collective-permute-done.2.refs_0_, ...), custom_call_target="tpu_custom_call", output_to_operand_aliasing={{1}: (4, {})} | custom-call | tf_op jit(solution)/shard_map/outer/pallas_call | solution.py:426
  (15 shorter events, 0.1 us)
Async XLA Ops:
  0.0 10.8 %copy-start = (bf16[1,16,128,128]{3,2,1,0:T(8,128)(2,1)S(1)}, bf16[1,16,128,128]{3,2,1,0:T(8,128)(2,1)}, u32[]{:S(2)}) copy-start(bf16[1,16,128,128]{3,2,1,0:T(8,128)(2,1)} %param.11) | copy-start | bytes 1572868
  0.0 6.9 %copy-start.9 = (s32[4,2,2]{0,2,1:T(2,128)S(1)}, s32[4,2,2]{0,2,1:T(2,128)}, u32[]{:S(2)}) copy-start(s32[4,2,2]{0,2,1:T(2,128)} %param.12) | copy-start | bytes 196
  0.0 10.8 %copy-start.2 = (bf16[3,3,128,128]{3,2,1,0:T(8,128)(2,1)S(1)}, bf16[3,3,128,128]{3,2,1,0:T(8,128)(2,1)}, u32[]{:S(2)}) copy-start(bf16[3,3,128,128]{3,2,1,0:T(8,128)(2,1)} %refs_10_.1) | copy-start | bytes 884740
  0.0 10.8 %copy-start.1 = (bf16[3,3,128,128]{3,2,1,0:T(8,128)(2,1)S(1)}, bf16[3,3,128,128]{3,2,1,0:T(8,128)(2,1)}, u32[]{:S(2)}) copy-start(bf16[3,3,128,128]{3,2,1,0:T(8,128)(2,1)} %refs_9_.1) | copy-start | bytes 884740
  0.0 10.8 %copy-start.4 = (bf16[128,128]{1,0:T(8,128)(2,1)S(1)}, bf16[128,128]{1,0:T(8,128)(2,1)}, u32[]{:S(2)}) copy-start(bf16[128,128]{1,0:T(8,128)(2,1)} %refs_7_.1) | copy-start | bytes 98308
  0.0 10.8 %copy-start.6 = (f32[128]{0:T(128)S(1)}, f32[128]{0:T(128)}, u32[]{:S(2)}) copy-start(f32[128]{0:T(128)} %param.17) | copy-start | bytes 1540
  0.0 10.8 %copy-start.5 = (f32[128]{0:T(128)S(1)}, f32[128]{0:T(128)}, u32[]{:S(2)}) copy-start(f32[128]{0:T(128)} %param.14) | copy-start | bytes 1540
  0.0 2.2 %collective-permute-start = (bf16[16,128,128]{2,1,0:T(8,128)(2,1)}, bf16[16,128,128]{2,1,0:T(8,128)(2,1)S(1)}, u32[]{:S(2)}, u32[]{:S(2)}) collective-permute-start(bf16[16,128,128]{2,1,0:T(8,128)(2,1)} %bitcast.7), channel_id=1, source_target_pairs={{0,1},{1,0},{2,3},{3,2},{4,5},{5,4},{6,7},{7,6},{8,9},{9,8},{10,11... | collective-permute-start | bytes 1572872 | tf_op jit(solution)/shard_map/ppermute | solution.py:43
  2.3 11.2 %collective-permute-start.1 = (bf16[10,128,128]{2,1,0:T(8,128)(2,1)S(1)}, bf16[10,128,128]{2,1,0:T(8,128)(2,1)S(1)}, u32[]{:S(2)}, u32[]{:S(2)}) collective-permute-start(bf16[10,128,128]{2,1,0:T(8,128)(2,1)S(1)} %pad_maximum_fusion), channel_id=1, source_target_pairs={{0,16},{1,4},{2,18},{3,6},{4,1},{5,8},{6,3},{7,10},{8,5},{9,12},{1... | collective-permute-start | bytes 983048 | tf_op jit(solution)/shard_map/ppermute | solution.py:43
  5.1 3.1 %collective-permute-start.3 = (bf16[16,8,128]{2,1,0:T(8,128)(2,1)S(1)}, bf16[16,8,128]{2,1,0:T(8,128)(2,1)S(1)}, u32[]{:S(2)}, u32[]{:S(2)}) collective-permute-start(bf16[16,8,128]{2,1,0:T(8,128)(2,1)S(1)} %get-tuple-element.15), channel_id=1, source_target_pairs={{0,2},{1,3},{2,0},{3,1},{4,6},{5,7},{6,4},{7,5},{8,10},{9,11},{10,... | collective-permute-start | bytes 98312 | tf_op jit(solution)/shard_map/ppermute | solution.py:43
  8.1 2.7 %collective-permute-start.4 = (bf16[16,8,128]{2,1,0:T(8,128)(2,1)S(1)}, bf16[16,8,128]{2,1,0:T(8,128)(2,1)S(1)}, u32[]{:S(2)}, u32[]{:S(2)}) collective-permute-start(bf16[16,8,128]{2,1,0:T(8,128)(2,1)S(1)} %collective-permute-done.3.refs_0_), channel_id=1, source_target_pairs={{0,1},{1,0},{2,3},{3,2},{4,5},{5,4},{6,7},{7,6},{8,9},{9,8},{10,11... | collective-permute-start | bytes 98312 | tf_op jit(solution)/shard_map/ppermute | solution.py:43
  9.3 4.2 %collective-permute-start.2 = (bf16[10,8,128]{2,1,0:T(8,128)(2,1)S(1)}, bf16[10,8,128]{2,1,0:T(8,128)(2,1)S(1)}, u32[]{:S(2)}, u32[]{:S(2)}) collective-permute-start(bf16[10,8,128]{2,1,0:T(8,128)(2,1)S(1)} %fusion.2), channel_id=1, source_target_pairs={{0,16},{1,6},{2,18},{3,4},{4,3},{5,10},{6,1},{7,8},{8,7},{9,14},{1... | collective-permute-start | bytes 61448 | tf_op jit(solution)/shard_map/ppermute | solution.py:43
  10.9 2.6 %copy-start.3 = (bf16[3,3,128,128]{3,2,1,0:T(8,128)(2,1)S(1)}, bf16[3,3,128,128]{3,2,1,0:T(8,128)(2,1)}, u32[]{:S(2)}) copy-start(bf16[3,3,128,128]{3,2,1,0:T(8,128)(2,1)} %refs_12_.1) | copy-start | bytes 884740
  10.9 2.6 %copy-start.7 = (f32[128]{0:T(128)S(1)}, f32[128]{0:T(128)}, u32[]{:S(2)}) copy-start(f32[128]{0:T(128)} %param.19) | copy-start | bytes 1540
  10.9 2.6 %copy-start.8 = (bf16[128]{0:T(256)(128)(2,1)S(1)}, bf16[128]{0:T(256)(128)(2,1)}, u32[]{:S(2)}) copy-start(bf16[128]{0:T(256)(128)(2,1)} %param.20) | copy-start | bytes 772
